TPU v7x, 32 devices: a whole 2x2x4 slice. The times are simulated.
32 devices in a mesh: fsdp: 4 (over y, x), ctx: 4 (over z), tp: 2 (over core).
Axes of the slice: x: 2, y: 2, z: 4, core: 2. Of those that a mesh axis runs over, the one named last changes fastest.
Arguments:
- tokens: bfloat16 [8, 256, 768], P('fsdp', 'ctx'), may hold values from -6 to 6
- group_order: int32 [8], replicated, may hold values from 0 to 7, each once
- attn_gain: float32 [768], replicated, may hold values from 0.1 to 1.9
- attn_shift: float32 [768], replicated, may hold values from -3 to 3
- qkv_weight: bfloat16 [768, 2304], P(('fsdp', 'ctx'), 'tp'), as said below
- qkv_bias: float32 [2304], P('tp'), may hold values from -3 to 3
- dense_weight: bfloat16 [768, 768], P('tp', ('fsdp', 'ctx')), may hold values from -3 to 3
- dense_bias: float32 [768], replicated, may hold values from -3 to 3
- mlp_gain: float32 [768], replicated, may hold values from 0.1 to 1.9
- mlp_shift: float32 [768], replicated, may hold values from -3 to 3
- up_weight: bfloat16 [768, 3072], P(('fsdp', 'ctx'), 'tp'), may hold values from -0.21875 to 0.21875
- up_bias: float32 [3072], P('tp'), may hold values from -3 to 3
- down_weight: bfloat16 [3072, 768], P('tp', ('fsdp', 'ctx')), may hold values from -0.109375 to 0.109375
- down_bias: float32 [768], replicated, may hold values from -3 to 3
- out_grad: float32 [8, 256, 768], P('fsdp', 'ctx'), may hold values from -6 to 6
Outputs:
- block_out: bfloat16 [8, 256, 768], P('fsdp', 'ctx')
- tokens_grad: float32 [8, 256, 768], P('fsdp', 'ctx')
- attn_gain_grad: float32 [768], replicated
- attn_shift_grad: float32 [768], replicated
- qkv_weight_grad: float32 [768, 2304], P(('fsdp', 'ctx'), 'tp')
- qkv_bias_grad: float32 [2304], P('tp')
- dense_weight_grad: float32 [768, 768], P('tp', ('fsdp', 'ctx'))
- dense_bias_grad: float32 [768], replicated
- mlp_gain_grad: float32 [768], replicated
- mlp_shift_grad: float32 [768], replicated
- up_weight_grad: float32 [768, 3072], P(('fsdp', 'ctx'), 'tp')
- up_bias_grad: float32 [3072], P('tp')
- down_weight_grad: float32 [3072, 768], P('tp', ('fsdp', 'ctx'))
- down_bias_grad: float32 [768], replicated
Inputs may be any that keep to these rules, and one draw needn't show every extreme that they name: Each block number appears once; slot s of every sequence holds positions group_order[s] * 32 to group_order[s] * 32 + 31. `qkv_weight`: columns ordered by head, then query, key and value, then the 64 dimensions of a head.
All inputs are finite; a program needn't handle non-finite values.
Results may differ from a plain program's by a relative error of at most 0.0099.
Values may be sent and summed in bfloat16 or wider, within the bound.
No kernel may reach another device: no remote copies, remote signals or barrier semaphores. Data moves between devices by JAX's collectives and lax.ppermute only.
A program may use at most 128 MiB of HBM per device.

v0:
```python
import functools
import math

import jax
import jax.numpy as jnp
from jax import lax
from jax.experimental import pallas as pl
from jax.experimental.pallas import tpu as pltpu
from jax.sharding import PartitionSpec as P


HD = 64
ROT = 16
BLK = 32


EPSILON = 1e-05
NEGATIVE = -1e30
ROOT_HALF = 0.7071067811865476
INV_ROOT_TWO_PI = 0.3989422804014327
CONTRACT_LAST = (((1,), (1,)), ((), ()))
CONTRACT_FIRST = (((0,), (0,)), ((), ()))


def angle_tables(position):
    half = ROT // 2
    frequency = 1.0 / 10000.0 ** (jnp.arange(half, dtype=jnp.float32) * (2.0 / ROT))
    phase = position.astype(jnp.float32)[:, None] * frequency[None, :]
    return (jnp.cos(phase), jnp.sin(phase))


def positions(order, start, count):
    index = start + jnp.arange(count, dtype=jnp.int32)
    slot = index // BLK
    table = jnp.arange(order.shape[0], dtype=jnp.int32)
    first = jnp.sum(jnp.where(slot[:, None] == table[None, :], order[None, :], 0), axis=1)
    return first * BLK + index % BLK


def swapped(parts, index):
    bit = 1
    while bit < len(parts):
        is_set = (index & bit) != 0
        parts = [jnp.where(is_set, parts[j ^ bit], parts[j]) for j in range(len(parts))]
        bit *= 2
    return parts


def swap(value, axis, bit):
    return lax.ppermute(value, axis, [(i, i ^ bit) for i in range(lax.axis_size(axis))])


def exchange(parts, axis):
    return [parts[0]] + [swap(parts[k], axis, k) for k in range(1, len(parts))]


def spread(value, axis):
    return exchange([value] * lax.axis_size(axis), axis)


def gather_order(count):
    order, bit = [0], count // 2
    while bit:
        order = order + [k ^ bit for k in order]
        bit //= 2
    return order


def gather_chunks(value, axis, dim):
    bit = lax.axis_size(axis) // 2
    while bit:
        other = swap(value, axis, bit)
        value = jnp.concatenate([value, other], axis=dim)
        bit //= 2
    return value


def scatter_chunks(value, axis, dim):
    count = lax.axis_size(axis)
    bit = 1
    while bit < count:
        kept, sent = jnp.split(value, 2, axis=dim)
        other = swap(sent.astype(jnp.bfloat16), axis, bit)
        value = kept + other.astype(jnp.float32)
        bit *= 2
    return value


def butterfly(value, axis):
    bit = 1
    while bit < lax.axis_size(axis):
        other = swap(value, axis, bit)
        value = value + other
        bit *= 2
    return value


def one_hot_slots(value, index, count):
    slots = jnp.arange(count, dtype=jnp.int32)[:, None] == index
    return jnp.where(slots, value[None, :], 0.0).reshape(-1)


def dot(left, right):
    return jnp.dot(left, right, preferred_element_type=jnp.float32)


def dot_last(left, right):
    return lax.dot_general(left, right, CONTRACT_LAST, preferred_element_type=jnp.float32)


def dot_first(left, right):
    return lax.dot_general(left, right, CONTRACT_FIRST, preferred_element_type=jnp.float32)


def normed_rows(rows):
    middle = jnp.mean(rows, axis=-1, keepdims=True)
    centred = rows - middle
    inverse = lax.rsqrt(jnp.mean(centred * centred, axis=-1, keepdims=True) + EPSILON)
    return centred * inverse, inverse


VMEM_LIMIT = 60 * 1024 * 1024
LANES = 128


def local_kernel(body, out_shapes, scratch=(), flops=0, moved=0):
    in_vmem = pl.BlockSpec(memory_space=pltpu.VMEM)
    return pl.pallas_call(
        body,
        out_shape=out_shapes,
        out_specs=jax.tree.map(lambda _: in_vmem, out_shapes),
        scratch_shapes=list(scratch),
        compiler_params=pltpu.CompilerParams(vmem_limit_bytes=VMEM_LIMIT),
        cost_estimate=pl.CostEstimate(flops=flops, bytes_accessed=moved, transcendentals=0),
    )


def shaped(shape, kind):
    return jax.ShapeDtypeStruct(tuple(shape), kind)


def rotary_tables(position):
    cosine, sine = angle_tables(position)
    rest = jnp.ones((position.shape[0], HD - ROT), jnp.float32)
    none = jnp.zeros((position.shape[0], HD - ROT), jnp.float32)
    cos_head = jnp.concatenate([cosine, cosine, rest], axis=1)
    sin_head = jnp.concatenate([-sine, sine, none], axis=1)
    return jnp.concatenate([cos_head] * 2, axis=1), jnp.concatenate([sin_head] * 2, axis=1)


def early_message_kernel(groups, qkv_cols, features, qkv_ref, dense_ref, *outs):
    at = lax.rem(lax.axis_index("ctx"), groups)
    dense_t = dense_ref[...]
    parts = [
        jnp.concatenate(
            [
                qkv_ref[:, g * qkv_cols : (g + 1) * qkv_cols],
                dense_t[:, g * features : (g + 1) * features],
            ],
            axis=1,
        )
        for g in range(groups)
    ]
    for out, part in zip(outs, swapped(parts, at)):
        out[...] = part


def late_message_kernel(count, ff, padded, up_ref, down_ref, *outs):
    at = lax.axis_index("ctx")
    down_t = down_ref[...]
    rows = up_ref.shape[0]
    gap = [jnp.zeros((rows, padded - ff), jnp.bfloat16)] if padded > ff else []
    parts = [
        jnp.concatenate(
            [up_ref[:, r * ff : (r + 1) * ff]] + gap + [down_t[:, r * ff : (r + 1) * ff]] + gap,
            axis=1,
        )
        for r in range(count)
    ]
    for out, part in zip(outs, swapped(parts, at)):
        out[...] = part


def ordered_kernel(*refs):
    parts, out = refs[:-1], refs[-1]
    for r, part in enumerate(swapped([part[...] for part in parts], lax.axis_index("ctx"))):
        out[r] = part


def place_weight(parts, weight):
    at = lax.axis_index("fsdp")
    block = parts[0].shape[0]
    for k, part in enumerate(parts):
        start = pl.multiple_of((at ^ k) * block, 16)
        weight[pl.ds(start, block), :] = part[...]


def send_blocks(total, outs):
    at = lax.axis_index("fsdp")
    block = outs[0].shape[0]
    for k, out in enumerate(outs):
        start = pl.multiple_of((at ^ k) * block, 16)
        out[...] = total[pl.ds(start, block), :].astype(out.dtype)


def attention_kernel(
    fsdp_count,
    core_count,
    near,
    head_groups,
    own_heads,
    copies,
    seqs,
    *refs,
):
    row_refs = refs[:core_count]
    parts = refs[core_count : core_count + fsdp_count]
    (norms, bias, cos_ref, sin_ref, pos_col, pos_row) = refs[
        core_count + fsdp_count : core_count + fsdp_count + 6
    ]
    gain, shift = norms[0:1, :], norms[1:2, :]
    outs = refs[core_count + fsdp_count + 6 :]
    branch, norm_out, sums = outs[:3]
    grad_outs = outs[3 : 3 + fsdp_count]
    weight, grads, mixed, total = outs[3 + fsdp_count :]
    cols = weight.shape[1]
    features = own_heads * HD
    qkv_cols = 3 * features
    scale = 1.0 / math.sqrt(HD)
    ctx_at = lax.axis_index("ctx")
    seq_at = lax.rem(lax.div(ctx_at, head_groups), seqs)
    core = lax.div(seq_at, near) ^ lax.axis_index("tp")
    inner = lax.rem(seq_at, near)
    place_weight(parts, weight)
    seq_tokens, seq_grads = row_refs[0][0, inner], row_refs[0][1, inner]
    for j in range(1, core_count):
        seq_tokens = jnp.where(core == j, row_refs[j][0, inner], seq_tokens)
        seq_grads = jnp.where(core == j, row_refs[j][1, inner], seq_grads)
    centred, _ = normed_rows(seq_tokens.astype(jnp.float32))
    attn_in = (centred * gain + shift).astype(jnp.bfloat16)
    lane = lax.broadcasted_iota(jnp.int32, (1, cols), 1)
    rotated = (lane < qkv_cols) & (lane % (3 * HD) < 2 * HD)
    first = lane % HD < ROT // 2
    repeat = cols // LANES
    cos_all = jnp.where(rotated, jnp.concatenate([cos_ref[...]] * repeat, axis=1), 1.0)
    sin_all = jnp.where(rotated, jnp.concatenate([sin_ref[...]] * repeat, axis=1), 0.0)

    def turn(values, sine):
        ahead = pltpu.roll(values, cols - ROT // 2, 1)
        behind = pltpu.roll(values, ROT // 2, 1)
        return values * cos_all + jnp.where(first, ahead, behind) * sine

    projected = dot(attn_in, weight[...]) + bias[...]
    turned = turn(projected, sin_all).astype(jnp.bfloat16)
    ctx_low = dot(seq_grads, weight[:, qkv_cols:]).astype(jnp.bfloat16)
    allowed = pos_row[...] <= pos_col[...]
    keep = None
    if copies > 1:
        keep = lax.div(ctx_at, head_groups * seqs) == 0
    grads[...] = jnp.zeros(grads.shape, jnp.float32)
    mixed[...] = jnp.zeros(mixed.shape, jnp.bfloat16)
    for head in range(own_heads):
        at = head * 3 * HD
        query = turned[:, at : at + HD]
        key = turned[:, at + HD : at + 2 * HD]
        value = turned[:, at + 2 * HD : at + 3 * HD]
        low = ctx_low[:, head * HD : (head + 1) * HD]
        scores = jnp.where(allowed, dot_last(query, key) * scale, NEGATIVE)
        peak = jnp.max(scores, axis=-1, keepdims=True)
        weights = jnp.where(allowed, jnp.exp(scores - peak), 0.0)
        probs = weights / jnp.sum(weights, axis=-1, keepdims=True)
        probs_low = probs.astype(jnp.bfloat16)
        attended = dot(probs_low, value)
        delta = jnp.sum(low.astype(jnp.float32) * attended, axis=-1, keepdims=True)
        score_grad = probs * (dot_last(low, value) - delta)
        if copies > 1:
            score_grad = jnp.where(keep, score_grad, 0.0)
            probs_low = jnp.where(keep, probs_low, jnp.zeros_like(probs_low))
            attended = jnp.where(keep, attended, 0.0)
        score_low = score_grad.astype(jnp.bfloat16)
        grads[:, at : at + HD] = dot(score_low, key) * scale
        grads[:, at + HD : at + 2 * HD] = dot_first(score_low, query) * scale
        grads[:, at + 2 * HD : at + 3 * HD] = dot_first(probs_low, low)
        mixed[:, qkv_cols + head * HD : qkv_cols + (head + 1) * HD] = attended.astype(jnp.bfloat16)
    proj_grad = turn(grads[...], -sin_all)
    proj_low = proj_grad.astype(jnp.bfloat16)
    total[...] = dot_first(attn_in, proj_low) + dot_first(seq_grads, mixed[...])
    send_blocks(total, grad_outs)
    branch[...] = dot_last(mixed[...], weight[...])
    norm_grad = dot_last(proj_low, weight[...])
    norm_out[...] = norm_grad * gain
    sums[...] = jnp.concatenate(
        [
            jnp.sum(norm_grad * centred, axis=0, keepdims=True),
            jnp.sum(norm_grad, axis=0, keepdims=True),
            jnp.sum(proj_grad, axis=0, keepdims=True),
        ],
        axis=0,
    )


def mlp_kernel(fsdp_count, core_count, near, head_groups, seqs, padded, *refs):
    row_refs = refs[:core_count]
    parts = refs[core_count : core_count + fsdp_count]
    norm_ref, bias, attn_branch, attn_norm = refs[
        core_count + fsdp_count : core_count + fsdp_count + 4
    ]
    gain, shift = norm_ref[2:3, :], norm_ref[3:4, :]
    outs = refs[core_count + fsdp_count + 4 :]
    branches = outs[:core_count]
    norms = outs[core_count : 2 * core_count]
    sums, bias_out = outs[2 * core_count : 2 * core_count + 2]
    grad_outs = outs[2 * core_count + 2 : 2 * core_count + 2 + fsdp_count]
    weight, total = outs[2 * core_count + 2 + fsdp_count :]
    size = attn_branch.shape[0]
    seq_at = lax.rem(lax.div(lax.axis_index("ctx"), head_groups), seqs)
    core = lax.div(seq_at, near) ^ lax.axis_index("tp")
    inner = lax.rem(seq_at, near)
    place_weight(parts, weight)
    up, down = weight[:, :padded], weight[:, padded:]
    gain_sum = shift_sum = bias_sum = 0.0
    for j in range(core_count):
        width = weight.shape[0]
        rows = row_refs[j][0].reshape(near * size, width)
        grad_rows = row_refs[j][1].reshape(near * size, width)
        centred, _ = normed_rows(rows.astype(jnp.float32))
        mlp_in = (centred * gain + shift).astype(jnp.bfloat16)
        pre_act = dot(mlp_in, up) + bias[...]
        normal = 0.5 * (1.0 + lax.erf(pre_act * ROOT_HALF))
        hidden = (pre_act * normal).astype(jnp.bfloat16)
        slope = normal + pre_act * jnp.exp(-0.5 * pre_act * pre_act) * INV_ROOT_TWO_PI
        pre_grad = dot(grad_rows, down) * slope
        pre_low = pre_grad.astype(jnp.bfloat16)
        up_part, down_part = dot_first(mlp_in, pre_low), dot_first(grad_rows, hidden)
        if j:
            total[:, :padded] += up_part
            total[:, padded:] += down_part
        else:
            total[:, :padded] = up_part
            total[:, padded:] = down_part
        norm_grad = dot_last(pre_low, up)
        gain_sum = gain_sum + jnp.sum(norm_grad * centred, axis=0, keepdims=True)
        shift_sum = shift_sum + jnp.sum(norm_grad, axis=0, keepdims=True)
        bias_sum = bias_sum + jnp.sum(pre_grad, axis=0, keepdims=True)
        norm_grad = norm_grad * gain
        branch = dot_last(hidden, down)
        for i in range(near):
            here = (core == j) & (inner == i)
            span = slice(i * size, (i + 1) * size)
            branches[j][span, :] = branch[span] + jnp.where(here, attn_branch[...], 0.0)
            norms[j][span, :] = norm_grad[span] + jnp.where(here, attn_norm[...], 0.0)
    send_blocks(total, grad_outs)
    sums[...] = jnp.concatenate([gain_sum, shift_sum], axis=0)
    bias_out[...] = bias_sum


def sum_blocks_kernel(fsdp_count, *refs):
    parts, outs = refs[:fsdp_count], refs[fsdp_count:]
    at = lax.axis_index("ctx")
    for k, out in enumerate(outs):
        rank = at ^ k
        block = parts[0][rank]
        for part in parts[1:]:
            block = block + part[rank].astype(jnp.float32)
        out[...] = block.astype(out.dtype)


def early_end_kernel(count, groups, qkv_cols, features, *refs):
    parts, (qkv_out, dense_out) = refs[:count], refs[count:]
    at = lax.rem(lax.axis_index("ctx"), groups)
    sums = []
    for g in range(groups):
        block = parts[g][...].astype(jnp.float32)
        for part in parts[g + groups :: groups]:
            block = block + part[...].astype(jnp.float32)
        sums.append(block)
    for g, block in enumerate(swapped(sums, at)):
        qkv_out[:, g * qkv_cols : (g + 1) * qkv_cols] = block[:, :qkv_cols]
        dense_out[:, g * features : (g + 1) * features] = block[:, qkv_cols:]


def late_end_kernel(count, ff, padded, *refs):
    parts, (up_out, down_out) = refs[:count], refs[count:]
    blocks = [part[...].astype(jnp.float32) for part in parts]
    for r, block in enumerate(swapped(blocks, lax.axis_index("ctx"))):
        up_out[:, r * ff : (r + 1) * ff] = block[:, :ff]
        down_out[:, r * ff : (r + 1) * ff] = block[:, padded : padded + ff]


def on_device(
    tokens,
    group_order,
    attn_gain,
    attn_shift,
    qkv_weight,
    qkv_bias,
    dense_weight,
    dense_bias,
    mlp_gain,
    mlp_shift,
    up_weight,
    up_bias,
    down_weight,
    down_bias,
    out_grad,
):
    bf16, f32 = jnp.bfloat16, jnp.float32
    seqs, length, width = tokens.shape
    fsdp_count, ctx_count, tp_count = (lax.axis_size(a) for a in ("fsdp", "ctx", "tp"))
    ctx_at, tp_at = lax.axis_index("ctx"), lax.axis_index("tp")
    rows_here = qkv_weight.shape[0]
    block_rows = ctx_count * rows_here
    heads = qkv_bias.shape[0] // (3 * HD)
    hidden_all = up_bias.shape[0]
    head_groups = math.gcd(heads, ctx_count)
    own_heads = heads // head_groups
    copies = ctx_count // head_groups // seqs
    features = own_heads * HD
    qkv_cols = 3 * features
    cols = qkv_cols + features
    ff = hidden_all // ctx_count
    padded = -(-ff // LANES) * LANES
    head_at = ctx_at % head_groups
    near = seqs // tp_count
    size = ctx_count * length
    near_rows = near * size

    early = local_kernel(
        functools.partial(early_message_kernel, head_groups, qkv_cols, features),
        [shaped((rows_here, cols), bf16)] * head_groups,
    )(qkv_weight, dense_weight.T)
    late = local_kernel(
        functools.partial(late_message_kernel, ctx_count, ff, padded),
        [shaped((rows_here, 2 * padded), bf16)] * ctx_count,
    )(up_weight, down_weight.T)
    early_rows = exchange([early[k % head_groups] for k in range(ctx_count)], "ctx")

    def near_part(array):
        parts = [array[j * near : (j + 1) * near] for j in range(tp_count)]
        return swapped(parts, tp_at)[0]

    own_tokens = near_part(tokens)
    own_grads = near_part(out_grad)
    message = jnp.stack([own_tokens, own_grads.astype(bf16)])
    late_rows = exchange(late, "ctx")
    chunks = gather_chunks(message[:, :, None], "ctx", 2)
    chunks = chunks.reshape(2, near, size, width)

    def own_rows(parts):
        shape = (ctx_count, rows_here, parts[0].shape[1])
        return local_kernel(ordered_kernel, shaped(shape, bf16))(*parts).reshape(block_rows, -1)

    early_parts = spread(own_rows(early_rows), "fsdp")
    late_parts = spread(own_rows(late_rows), "fsdp")
    by_core = spread(chunks, "tp")

    position = jnp.concatenate(
        [
            positions(group_order, (ctx_at ^ k) * length, length)
            for k in gather_order(ctx_count)
        ]
    )
    cos_table, sin_table = rotary_tables(position)
    place = position.astype(f32)
    norms = jnp.stack([attn_gain, attn_shift, mlp_gain, mlp_shift])

    def row(vector):
        return vector.reshape(1, -1)

    qkv_parts = [qkv_bias[g * qkv_cols : (g + 1) * qkv_cols] for g in range(head_groups)]
    qkv_own = jnp.pad(swapped(qkv_parts, head_at)[0], (0, features))
    up_parts = [up_bias[r * ff : (r + 1) * ff] for r in range(ctx_count)]
    up_own = jnp.pad(swapped(up_parts, ctx_at)[0], (0, padded - ff))

    def grad_blocks(columns):
        return [
            shaped((block_rows, columns), bf16 if k else f32) for k in range(fsdp_count)
        ]

    attn_branch, attn_norm, attn_sums, *early_grads = local_kernel(
        functools.partial(
            attention_kernel, fsdp_count, tp_count, near, head_groups, own_heads, copies, seqs
        ),
        [shaped((size, width), f32), shaped((size, width), f32), shaped((3, cols), f32)]
        + grad_blocks(cols),
        [
            pltpu.VMEM((width, cols), bf16),
            pltpu.VMEM((size, cols), f32),
            pltpu.VMEM((size, cols), bf16),
            pltpu.VMEM((width, cols), f32),
        ],
        flops=16 * size * width * cols,
        moved=16 * size * width,
    )(
        *by_core,
        *early_parts,
        norms,
        row(qkv_own),
        cos_table,
        sin_table,
        place.reshape(-1, 1),
        row(place),
    )
    outs = local_kernel(
        functools.partial(mlp_kernel, fsdp_count, tp_count, near, head_groups, seqs, padded),
        [shaped((near_rows, width), f32)] * (2 * tp_count)
        + [shaped((2, width), f32), shaped((1, padded), f32)]
        + grad_blocks(2 * padded),
        [pltpu.VMEM((width, 2 * padded), bf16), pltpu.VMEM((width, 2 * padded), f32)],
        flops=12 * seqs * size * width * padded,
        moved=32 * size * width,
    )(
        *by_core,
        *late_parts,
        norms,
        row(up_own),
        attn_branch,
        attn_norm,
    )
    branch_parts, norm_parts = outs[:tp_count], outs[tp_count : 2 * tp_count]
    mlp_sums, up_bias_part = outs[2 * tp_count : 2 * tp_count + 2]
    late_grads = outs[2 * tp_count + 2 :]

    def scatter_rows(parts):
        half = sum(exchange(parts, "tp")).reshape(near, ctx_count, length, width)
        return scatter_chunks(half, "ctx", 1).reshape(near, length, width)

    def both_cores(half):
        return jnp.concatenate(swapped(spread(half, "tp"), tp_at), axis=0)

    def scatter_weights(parts):
        columns = parts[0].shape[1]
        received = [part.reshape(ctx_count, rows_here, columns) for part in exchange(parts, "fsdp")]
        pieces = local_kernel(
            functools.partial(sum_blocks_kernel, fsdp_count),
            [shaped((rows_here, columns), bf16 if k else f32) for k in range(ctx_count)],
        )(*received)
        return exchange(pieces, "ctx")

    early_pieces = scatter_weights(early_grads)
    late_pieces = scatter_weights(late_grads)
    branches = scatter_rows(branch_parts)
    inner = scatter_rows(norm_parts)
    block_half = own_tokens.astype(f32) + branches + (dense_bias + down_bias)
    block_out = both_cores(block_half.astype(bf16))
    own_centred, own_inverse = normed_rows(own_tokens.astype(f32))
    inner = (
        inner
        - jnp.mean(inner, axis=-1, keepdims=True)
        - own_centred * jnp.mean(inner * own_centred, axis=-1, keepdims=True)
    )
    tokens_grad = both_cores(own_grads + own_inverse * inner)
    qkv_weight_grad, dense_weight_grad = local_kernel(
        functools.partial(early_end_kernel, ctx_count, head_groups, qkv_cols, features),
        [shaped(qkv_weight.shape, f32), shaped(dense_weight.shape[::-1], f32)],
    )(*early_pieces)
    up_weight_grad, down_weight_grad = local_kernel(
        functools.partial(late_end_kernel, ctx_count, ff, padded),
        [shaped(up_weight.shape, f32), shaped(down_weight.shape[::-1], f32)],
    )(*late_pieces)

    gain_parts = jnp.concatenate([attn_sums[:2].reshape(-1), mlp_sums.reshape(-1)])
    bias_parts = jnp.concatenate(
        [
            jnp.sum(out_grad, axis=(0, 1)),
            one_hot_slots(attn_sums[2, :qkv_cols], head_at, head_groups),
            one_hot_slots(up_bias_part[0, :ff], ctx_at, ctx_count),
        ]
    )
    small = jnp.concatenate([butterfly(gain_parts, "tp"), bias_parts])
    small = butterfly(butterfly(small, "fsdp"), "ctx")
    cuts = []
    start = 0
    for extent in [width] * 5 + [3 * HD * heads, hidden_all]:
        cuts.append(small[start : start + extent])
        start += extent
    return (
        block_out,
        tokens_grad,
        cuts[0],
        cuts[1],
        qkv_weight_grad,
        cuts[5],
        dense_weight_grad.T,
        cuts[4],
        cuts[2],
        cuts[3],
        up_weight_grad,
        cuts[6],
        down_weight_grad.T,
        cuts[4],
    )


def solution(mesh):
    in_specs = (
        P("fsdp", "ctx", None),
        P(),
        P(),
        P(),
        P(("fsdp", "ctx"), "tp"),
        P("tp"),
        P("tp", ("fsdp", "ctx")),
        P(),
        P(),
        P(),
        P(("fsdp", "ctx"), "tp"),
        P("tp"),
        P("tp", ("fsdp", "ctx")),
        P(),
        P("fsdp", "ctx", None),
    )
    out_specs = (
        P("fsdp", "ctx", None),
        P("fsdp", "ctx", None),
        P(),
        P(),
        P(("fsdp", "ctx"), "tp"),
        P("tp"),
        P("tp", ("fsdp", "ctx")),
        P(),
        P(),
        P(),
        P(("fsdp", "ctx"), "tp"),
        P("tp"),
        P("tp", ("fsdp", "ctx")),
        P(),
    )

    return jax.shard_map(
        on_device, mesh=mesh, in_specs=in_specs, out_specs=out_specs, check_vma=False
    )
```

profile of v0, /device:TPU:0, one launch (start us, length us, event | category | flops | bytes accessed | tf_op | source)
XLA Modules:
  0.0 156.1 jit_solution(16022846897195994290)
XLA Ops:
  0.7 1.7 %shard_map.256 = (bf16[48,768]{1,0:T(8,128)(2,1)}, bf16[48,768]{1,0:T(8,128)(2,1)}) custom-call(bf16[48,1152]{1,0:T(8,128)(2,1)} %qkv_ref.1, bf16[48,384]{1,0:T(8,128)(2,1)} %bitcast.61), custom_call_target="tpu_custom_call" | custom-call | tf_op jit(solution)/shard_map/pallas_call | solution.py:428
  2.4 5.1 %collective-permute-start.11 = (bf16[48,768]{1,0:T(8,128)(2,1)}, bf16[48,768]{1,0:T(8,128)(2,1)S(1)}, u32[]{:S(2)}, u32[]{:S(2)}) collective-permute-start(bf16[48,768]{1,0:T(8,128)(2,1)} %get-tuple-element.54), channel_id=1, source_target_pairs={{0,6},{2,4},{4,2},{6,0},{1,7},{3,5},{5,3},{7,1},{8,14},{10,12},{12... | collective-permute-start | bytes 221192 | tf_op jit(solution)/shard_map/ppermute | solution.py:50
  7.4 1.1 convert_reduce_fusion
  9.4 2.1 %collective-permute-start.10 = (bf16[48,768]{1,0:T(8,128)(2,1)S(1)}, bf16[48,768]{1,0:T(8,128)(2,1)S(1)}, u32[]{:S(2)}, u32[]{:S(2)}) collective-permute-start(bf16[48,768]{1,0:T(8,128)(2,1)S(1)} %copy-done.7), channel_id=1, source_target_pairs={{0,4},{2,6},{4,0},{6,2},{1,5},{3,7},{5,1},{7,3},{8,12},{10,14},{12... | collective-permute-start | bytes 221192 | tf_op jit(solution)/shard_map/ppermute | solution.py:50
  11.6 1.7 %shard_map.254 = (bf16[48,768]{1,0:T(8,128)(2,1)}, bf16[48,768]{1,0:T(8,128)(2,1)}, bf16[48,768]{1,0:T(8,128)(2,1)}, bf16[48,768]{1,0:T(8,128)(2,1)}) custom-call(bf16[48,1536]{1,0:T(8,128)(2,1)} %up_ref.1, bf16[48,1536]{1,0:T(8,128)(2,1)} %bitcast.60), custom_call_target="tpu_custom_call" | custom-call | tf_op jit(solution)/shard_map/pallas_call | solution.py:432
  13.3 2.0 %collective-permute-start.3 = (bf16[48,768]{1,0:T(8,128)(2,1)}, bf16[48,768]{1,0:T(8,128)(2,1)S(1)}, u32[]{:S(2)}, u32[]{:S(2)}) collective-permute-start(bf16[48,768]{1,0:T(8,128)(2,1)} %get-tuple-element.50), channel_id=1, source_target_pairs={{0,2},{2,0},{4,6},{6,4},{1,3},{3,1},{5,7},{7,5},{8,10},{10,8},{12,... | collective-permute-start | bytes 221192 | tf_op jit(solution)/shard_map/ppermute | solution.py:50
  16.2 6.3 %collective-permute-done = bf16[2,1,1,64,768]{4,3,0,2,1:T(8,128)(2,1)S(1)} collective-permute-done((bf16[2,1,1,64,768]{4,3,0,2,1:T(8,128)(2,1)S(1)}, bf16[2,1,1,64,768]{4,3,0,2,1:T(8,128)(2,1)S(1)}, u32[]{:S(2)}, u32[]{:S(2)}) %collective-permute-start) | collective-permute-done | bytes 196640 | tf_op jit(solution)/shard_map/ppermute | solution.py:50
  22.7 0.8 copy.40.refs_10_
  27.0 4.8 %collective-permute-done.1 = bf16[2,1,2,64,768]{4,3,0,2,1:T(8,128)(2,1)S(1)} collective-permute-done((bf16[2,1,2,64,768]{4,3,0,2,1:T(8,128)(2,1)S(1)}, bf16[2,1,2,64,768]{4,3,0,2,1:T(8,128)(2,1)S(1)}, u32[]{:S(2)}, u32[]{:S(2)}) %collective-permute-start.1) | collective-permute-done | bytes 393248 | tf_op jit(solution)/shard_map/ppermute | solution.py:50
  32.6 0.9 concatenate.70.refs_8_
  33.5 0.9 concatenate.71.refs_9_
  36.3 1.7 %shard_map.257 = bf16[4,48,768]{2,1,0:T(8,128)(2,1)} custom-call(bf16[48,768]{1,0:T(8,128)(2,1)} %get-tuple-element.53.refs_0_, bf16[48,768]{1,0:T(8,128)(2,1)} %copy-done.9, bf16[48,768]{1,0:T(8,128)(2,1)} %copy-done.10, bf16[48,768]{1,0:T(8,128)(2,1)} %copy-done.8), custom_call_target="tpu_custom_call" | custom-call | tf_op jit(solution)/shard_map/pallas_call | solution.py:451
  38.0 1.5 collective-permute-start.12
  39.5 1.5 collective-permute-start.13
  42.2 1.9 %collective-permute-start.4 = (bf16[48,768]{1,0:T(8,128)(2,1)S(1)}, bf16[48,768]{1,0:T(8,128)(2,1)S(1)}, u32[]{:S(2)}, u32[]{:S(2)}) collective-permute-start(bf16[48,768]{1,0:T(8,128)(2,1)S(1)} %copy-done.37), channel_id=1, source_target_pairs={{0,4},{2,6},{4,0},{6,2},{1,5},{3,7},{5,1},{7,3},{8,12},{10,14},{12... | collective-permute-start | bytes 221192 | tf_op jit(solution)/shard_map/ppermute | solution.py:50
  44.1 4.5 %collective-permute-done.4.refs_2_ = bf16[48,768]{1,0:T(8,128)(2,1)S(1)} collective-permute-done((bf16[48,768]{1,0:T(8,128)(2,1)S(1)}, bf16[48,768]{1,0:T(8,128)(2,1)S(1)}, u32[]{:S(2)}, u32[]{:S(2)}) %collective-permute-start.4) | collective-permute-done | bytes 73760 | tf_op jit(solution)/shard_map/ppermute | solution.py:50
  48.6 2.7 %collective-permute-start.5 = (bf16[48,768]{1,0:T(8,128)(2,1)S(1)}, bf16[48,768]{1,0:T(8,128)(2,1)S(1)}, u32[]{:S(2)}, u32[]{:S(2)}) collective-permute-start(bf16[48,768]{1,0:T(8,128)(2,1)S(1)} %copy-done.36), channel_id=1, source_target_pairs={{0,6},{2,4},{4,2},{6,0},{1,7},{3,5},{5,3},{7,1},{8,14},{10,12},{12... | collective-permute-start | bytes 221192 | tf_op jit(solution)/shard_map/ppermute | solution.py:50
  51.3 3.4 %collective-permute-done.5.refs_3_ = bf16[48,768]{1,0:T(8,128)(2,1)S(1)} collective-permute-done((bf16[48,768]{1,0:T(8,128)(2,1)S(1)}, bf16[48,768]{1,0:T(8,128)(2,1)S(1)}, u32[]{:S(2)}, u32[]{:S(2)}) %collective-permute-start.5) | collective-permute-done | bytes 73760 | tf_op jit(solution)/shard_map/ppermute | solution.py:50
  55.3 1.7 %shard_map.255 = bf16[4,48,768]{2,1,0:T(8,128)(2,1)} custom-call(bf16[48,768]{1,0:T(8,128)(2,1)} %get-tuple-element.49.refs_0_, bf16[48,768]{1,0:T(8,128)(2,1)} %copy-done.6, bf16[48,768]{1,0:T(8,128)(2,1)} %copy-done.11, bf16[48,768]{1,0:T(8,128)(2,1)} %copy-done.12), custom_call_target="tpu_custom_call" | custom-call | tf_op jit(solution)/shard_map/pallas_call | solution.py:451
  57.1 1.5 collective-permute-start.6
  58.6 1.5 collective-permute-start.7
  61.4 8.9 %shard_map.258 = (f32[256,768]{1,0:T(8,128)}, f32[256,768]{1,0:T(8,128)}, f32[3,768]{1,0:T(4,128)}, f32[192,768]{1,0:T(8,128)}, bf16[192,768]{1,0:T(8,128)(2,1)}...) custom-call(bf16[2,1,256,768]{3,2,1,0:T(8,128)(2,1)} %bitcast.45, ...), custom_call_target="tpu_custom_call" | custom-call | flops 2415919104 | bytes 3145728 | tf_op jit(solution)/shard_map/pallas_call | solution.py:480
  73.0 7.3 %shard_map.259 = (f32[256,768]{1,0:T(8,128)}, f32[256,768]{1,0:T(8,128)}, f32[256,768]{1,0:T(8,128)}, f32[256,768]{1,0:T(8,128)}, f32[2,768]{1,0:T(2,128)}, /*in...) custom-call(bf16[2,1,256,768]{3,2,1,0:T(8,128)(2,1)} %bitcast.46, ...), custom_call_target="tpu_custom_call" | custom-call | flops 1811939328 | bytes 6291456 | tf_op jit(solution)/shard_map/pallas_call | solution.py:504
  82.3 1.2 collective-permute-start.24
  83.5 2.7 %collective-permute-done.24 = f32[6528]{0:T(1024)S(1)} collective-permute-done((f32[6528]{0:T(1024)S(1)}, f32[6528]{0:T(1024)S(1)}, u32[]{:S(2)}, u32[]{:S(2)}) %collective-permute-start.24) | collective-permute-done | bytes 26144 | tf_op jit(solution)/shard_map/ppermute | solution.py:50
  86.3 1.6 %collective-permute-start.25 = (f32[6528]{0:T(1024)S(1)}, f32[6528]{0:T(1024)S(1)}, u32[]{:S(2)}, u32[]{:S(2)}) collective-permute-start(f32[6528]{0:T(1024)S(1)} %fusion.19), channel_id=1, source_target_pairs={{0,16},{8,24},{16,0},{24,8},{1,17},{9,25},{17,1},{25,9},{2,18},{10... | collective-permute-start | bytes 78344 | tf_op jit(solution)/shard_map/ppermute | solution.py:50
  87.9 1.1 collective-permute-start.34
  90.3 3.9 %collective-permute-done.26 = f32[6528]{0:T(1024)S(1)} collective-permute-done((f32[6528]{0:T(1024)S(1)}, f32[6528]{0:T(1024)S(1)}, u32[]{:S(2)}, u32[]{:S(2)}) %collective-permute-start.26) | collective-permute-done | bytes 26144 | tf_op jit(solution)/shard_map/ppermute | solution.py:50
  94.2 1.4 collective-permute-start.27
  95.6 3.3 %collective-permute-done.27 = f32[6528]{0:T(1024)S(1)} collective-permute-done((f32[6528]{0:T(1024)S(1)}, f32[6528]{0:T(1024)S(1)}, u32[]{:S(2)}, u32[]{:S(2)}) %collective-permute-start.27) | collective-permute-done | bytes 26144 | tf_op jit(solution)/shard_map/ppermute | solution.py:50
  99.0 2.5 %collective-permute-start.36 = (bf16[192,768]{1,0:T(8,128)(2,1)}, bf16[192,768]{1,0:T(8,128)(2,1)}, u32[]{:S(2)}, u32[]{:S(2)}) collective-permute-start(bf16[192,768]{1,0:T(8,128)(2,1)} %get-tuple-element.77), channel_id=1, source_target_pairs={{0,24},{8,16},{16,8},{24,0},{1,25},{9,17},{17,9},{25,1},{2,26},{10... | collective-permute-start | bytes 884744 | tf_op jit(solution)/shard_map/ppermute | solution.py:50
  101.4 0.9 collective-permute-start.28
  102.5 2.5 %collective-permute-start.30 = (bf16[192,768]{1,0:T(8,128)(2,1)}, bf16[192,768]{1,0:T(8,128)(2,1)}, u32[]{:S(2)}, u32[]{:S(2)}) collective-permute-start(bf16[192,768]{1,0:T(8,128)(2,1)} %get-tuple-element.67), channel_id=1, source_target_pairs={{0,24},{8,16},{16,8},{24,0},{1,25},{9,17},{17,9},{25,1},{2,26},{10... | collective-permute-start | bytes 884744 | tf_op jit(solution)/shard_map/ppermute | solution.py:50
  105.2 1.2 add.327
  106.5 3.7 %collective-permute-done.36 = bf16[192,768]{1,0:T(8,128)(2,1)} collective-permute-done((bf16[192,768]{1,0:T(8,128)(2,1)}, bf16[192,768]{1,0:T(8,128)(2,1)}, u32[]{:S(2)}, u32[]{:S(2)}) %collective-permute-start.36) | collective-permute-done | bytes 294944 | tf_op jit(solution)/shard_map/ppermute | solution.py:50
  110.4 2.1 %shard_map.262 = (f32[48,768]{1,0:T(8,128)}, bf16[48,768]{1,0:T(8,128)(2,1)}, bf16[48,768]{1,0:T(8,128)(2,1)}, bf16[48,768]{1,0:T(8,128)(2,1)}) custom-call(f32[4,48,768]{2,1,0:T(8,128)} %bitcast.48, bf16[4,48,768]{2,1,0:T(8,128)(2,1)} %bitcast.57, bf16[4,48,768]{2,1,0:T(8,128)(2,1)} %bitcast.58, bf16[4,48,768]{2,1,0:T(8,128)(2,1)} %bitcast.28.refs_3_), custom_call_target="tpu_custom_call" | custom-call | tf_op jit(solution)/shard_map/pallas_call | solution.py:534
  112.5 2.2 %collective-permute-done.28 = bf16[192,768]{1,0:T(8,128)(2,1)S(1)} collective-permute-done((bf16[192,768]{1,0:T(8,128)(2,1)}, bf16[192,768]{1,0:T(8,128)(2,1)S(1)}, u32[]{:S(2)}, u32[]{:S(2)}) %collective-permute-start.28) | collective-permute-done | bytes 294944 | tf_op jit(solution)/shard_map/ppermute | solution.py:50
  115.2 2.5 %collective-permute-start.38 = (bf16[48,768]{1,0:T(8,128)(2,1)}, bf16[48,768]{1,0:T(8,128)(2,1)S(1)}, u32[]{:S(2)}, u32[]{:S(2)}) collective-permute-start(bf16[48,768]{1,0:T(8,128)(2,1)} %get-tuple-element.80), channel_id=1, source_target_pairs={{0,4},{2,6},{4,0},{6,2},{1,5},{3,7},{5,1},{7,3},{8,12},{10,14},{12... | collective-permute-start | bytes 221192 | tf_op jit(solution)/shard_map/ppermute | solution.py:50
  117.7 2.6 %collective-permute-start.39 = (bf16[48,768]{1,0:T(8,128)(2,1)}, bf16[48,768]{1,0:T(8,128)(2,1)S(1)}, u32[]{:S(2)}, u32[]{:S(2)}) collective-permute-start(bf16[48,768]{1,0:T(8,128)(2,1)} %get-tuple-element.81), channel_id=1, source_target_pairs={{0,6},{2,4},{4,2},{6,0},{1,7},{3,5},{5,3},{7,1},{8,14},{10,12},{12... | collective-permute-start | bytes 221192 | tf_op jit(solution)/shard_map/ppermute | solution.py:50
  120.3 2.1 %shard_map.260 = (f32[48,768]{1,0:T(8,128)}, bf16[48,768]{1,0:T(8,128)(2,1)}, bf16[48,768]{1,0:T(8,128)(2,1)}, bf16[48,768]{1,0:T(8,128)(2,1)}) custom-call(f32[4,48,768]{2,1,0:T(8,128)} %bitcast.47, bf16[4,48,768]{2,1,0:T(8,128)(2,1)} %bitcast.59, bf16[4,48,768]{2,1,0:T(8,128)(2,1)} %bitcast.22.refs_2_, bf16[4,48,768]{2,1,0:T(8,128)(2,1)} %bitcast.23.refs_3_), custom_call_target="tpu_custom_call" | custom-call | tf_op jit(solution)/shard_map/pallas_call | solution.py:534
  122.6 2.1 %collective-permute-start.16 = (bf16[1,2,64,768]{3,2,1,0:T(8,128)(2,1)S(1)}, bf16[1,2,64,768]{3,2,1,0:T(8,128)(2,1)S(1)}, u32[]{:S(2)}, u32[]{:S(2)}) collective-permute-start(bf16[1,2,64,768]{3,2,1,0:T(8,128)(2,1)S(1)} %split.63), channel_id=1, source_target_pairs={{0,2},{2,0},{4,6},{6,4},{1,3},{3,1},{5,7},{7,5},{8,10},{10,8},{12,... | collective-permute-start | bytes 589832 | tf_op jit(solution)/shard_map/ppermute | solution.py:50
  124.7 5.4 %collective-permute-done.16 = bf16[1,2,64,768]{3,2,1,0:T(8,128)(2,1)S(1)} collective-permute-done((bf16[1,2,64,768]{3,2,1,0:T(8,128)(2,1)S(1)}, bf16[1,2,64,768]{3,2,1,0:T(8,128)(2,1)S(1)}, u32[]{:S(2)}, u32[]{:S(2)}) %collective-permute-start.16) | collective-permute-done | bytes 196640 | tf_op jit(solution)/shard_map/ppermute | solution.py:50
  130.1 0.9 collective-permute-start.21
  131.1 5.5 %collective-permute-done.21 = bf16[1,1,64,768]{3,2,1,0:T(8,128)(2,1)S(1)} collective-permute-done((bf16[1,1,64,768]{3,2,1,0:T(8,128)(2,1)S(1)}, bf16[1,1,64,768]{3,2,1,0:T(8,128)(2,1)S(1)}, u32[]{:S(2)}, u32[]{:S(2)}) %collective-permute-start.21) | collective-permute-done | bytes 98336 | tf_op jit(solution)/shard_map/ppermute | solution.py:50
  137.0 6.7 %collective-permute-done.17 = bf16[1,1,64,768]{3,2,1,0:T(8,128)(2,1)S(1)} collective-permute-done((bf16[1,1,64,768]{3,2,1,0:T(8,128)(2,1)S(1)}, bf16[1,1,64,768]{3,2,1,0:T(8,128)(2,1)S(1)}, u32[]{:S(2)}, u32[]{:S(2)}) %collective-permute-start.17) | collective-permute-done | bytes 98336 | tf_op jit(solution)/shard_map/ppermute | solution.py:50
  144.6 1.3 collective-permute-start.33
  148.3 1.9 %shard_map.263 = (f32[48,1536]{1,0:T(8,128)}, f32[48,1536]{1,0:T(8,128)}) custom-call(f32[48,768]{1,0:T(8,128)} %get-tuple-element.78.refs_0_, bf16[48,768]{1,0:T(8,128)(2,1)} %copy-done.13, bf16[48,768]{1,0:T(8,128)(2,1)} %copy-done.14, bf16[48,768]{1,0:T(8,128)(2,1)} %copy-done.15), custom_call_target="tpu_custom_call" | custom-call | tf_op jit(solution)/shard_map/pallas_call | solution.py:557
  151.4 1.8 %shard_map.261 = (f32[48,1152]{1,0:T(8,128)}, f32[48,384]{1,0:T(8,128)}) custom-call(f32[48,768]{1,0:T(8,128)} %get-tuple-element.68.refs_0_, bf16[48,768]{1,0:T(8,128)(2,1)} %copy-done.16, bf16[48,768]{1,0:T(8,128)(2,1)} %copy-done.17, bf16[48,768]{1,0:T(8,128)(2,1)} %copy-done.18), custom_call_target="tpu_custom_call" | custom-call | tf_op jit(solution)/shard_map/pallas_call | solution.py:553
  (201 shorter events, 26.1 us)
Async XLA Ops:
  0.6 7.9 %copy-start = (f32[2,64,768]{2,1,0:T(8,128)S(1)}, f32[2,64,768]{2,1,0:T(8,128)}, u32[]{:S(2)}) copy-start(f32[2,64,768]{2,1,0:T(8,128)} %param.29) | copy-start | bytes 1179652
  2.4 32.7 %collective-permute-start.11 = (bf16[48,768]{1,0:T(8,128)(2,1)}, bf16[48,768]{1,0:T(8,128)(2,1)S(1)}, u32[]{:S(2)}, u32[]{:S(2)}) collective-permute-start(bf16[48,768]{1,0:T(8,128)(2,1)} %get-tuple-element.54), channel_id=1, source_target_pairs={{0,6},{2,4},{4,2},{6,0},{1,7},{3,5},{5,3},{7,1},{8,14},{10,12},{12... | collective-permute-start | bytes 221192 | tf_op jit(solution)/shard_map/ppermute | solution.py:50
  7.4 27.6 %collective-permute-start.9 = (bf16[48,768]{1,0:T(8,128)(2,1)}, bf16[48,768]{1,0:T(8,128)(2,1)S(1)}, u32[]{:S(2)}, u32[]{:S(2)}) collective-permute-start(bf16[48,768]{1,0:T(8,128)(2,1)} %get-tuple-element.54), channel_id=1, source_target_pairs={{0,2},{2,0},{4,6},{6,4},{1,3},{3,1},{5,7},{7,5},{8,10},{10,8},{12,... | collective-permute-start | bytes 221192 | tf_op jit(solution)/shard_map/ppermute | solution.py:50
  8.6 14.0 %collective-permute-start = (bf16[2,1,1,64,768]{4,3,0,2,1:T(8,128)(2,1)S(1)}, bf16[2,1,1,64,768]{4,3,0,2,1:T(8,128)(2,1)S(1)}, u32[]{:S(2)}, u32[]{:S(2)}) collective-permute-start(bf16[2,1,1,64,768]{4,3,0,2,1:T(8,128)(2,1)S(1)} %maximum_bitcast_fusion), channel_id=1, source_target_pairs={{0,4},{2,6},{4,0},{6,2},{1,5},{3,7},{5,1},{7,3},{8,12},{10,14},{12... | collective-permute-start | bytes 589832 | tf_op jit(solution)/shard_map/ppermute | solution.py:50
  9.4 25.6 %collective-permute-start.10 = (bf16[48,768]{1,0:T(8,128)(2,1)S(1)}, bf16[48,768]{1,0:T(8,128)(2,1)S(1)}, u32[]{:S(2)}, u32[]{:S(2)}) collective-permute-start(bf16[48,768]{1,0:T(8,128)(2,1)S(1)} %copy-done.7), channel_id=1, source_target_pairs={{0,4},{2,6},{4,0},{6,2},{1,5},{3,7},{5,1},{7,3},{8,12},{10,14},{12... | collective-permute-start | bytes 221192 | tf_op jit(solution)/shard_map/ppermute | solution.py:50
  13.3 28.9 %collective-permute-start.3 = (bf16[48,768]{1,0:T(8,128)(2,1)}, bf16[48,768]{1,0:T(8,128)(2,1)S(1)}, u32[]{:S(2)}, u32[]{:S(2)}) collective-permute-start(bf16[48,768]{1,0:T(8,128)(2,1)} %get-tuple-element.50), channel_id=1, source_target_pairs={{0,2},{2,0},{4,6},{6,4},{1,3},{3,1},{5,7},{7,5},{8,10},{10,8},{12,... | collective-permute-start | bytes 221192 | tf_op jit(solution)/shard_map/ppermute | solution.py:50
  22.6 9.2 %collective-permute-start.1 = (bf16[2,1,2,64,768]{4,3,0,2,1:T(8,128)(2,1)S(1)}, bf16[2,1,2,64,768]{4,3,0,2,1:T(8,128)(2,1)S(1)}, u32[]{:S(2)}, u32[]{:S(2)}) collective-permute-start(bf16[2,1,2,64,768]{4,3,0,2,1:T(8,128)(2,1)S(1)} %pad_maximum_fusion.1), channel_id=1, source_target_pairs={{0,2},{2,0},{4,6},{6,4},{1,3},{3,1},{5,7},{7,5},{8,10},{10,8},{12,... | collective-permute-start | bytes 1179656 | tf_op jit(solution)/shard_map/ppermute | solution.py:50
  31.9 28.7 %collective-permute-start.2 = (bf16[2,1,256,768]{3,2,1,0:T(8,128)(2,1)S(1)}, bf16[2,1,256,768]{3,2,1,0:T(8,128)(2,1)}, u32[]{:S(2)}, u32[]{:S(2)}) collective-permute-start(bf16[2,1,256,768]{3,2,1,0:T(8,128)(2,1)S(1)} %bitcast.44), channel_id=1, source_target_pairs={{0,1},{1,0},{2,3},{3,2},{4,5},{5,4},{6,7},{7,6},{8,9},{9,8},{10,11... | collective-permute-start | bytes 2359304 | tf_op jit(solution)/shard_map/ppermute | solution.py:50
  35.0 7.2 %copy-start.37 = (bf16[48,768]{1,0:T(8,128)(2,1)S(1)}, bf16[48,768]{1,0:T(8,128)(2,1)}, u32[]{:S(2)}) copy-start(bf16[48,768]{1,0:T(8,128)(2,1)} %get-tuple-element.51) | copy-start | bytes 221188
  35.0 13.6 %copy-start.36 = (bf16[48,768]{1,0:T(8,128)(2,1)S(1)}, bf16[48,768]{1,0:T(8,128)(2,1)}, u32[]{:S(2)}) copy-start(bf16[48,768]{1,0:T(8,128)(2,1)} %get-tuple-element.52) | copy-start | bytes 221188
  38.0 20.5 %collective-permute-start.12 = (bf16[192,768]{1,0:T(8,128)(2,1)}, bf16[192,768]{1,0:T(8,128)(2,1)S(1)}, u32[]{:S(2)}, u32[]{:S(2)}) collective-permute-start(bf16[192,768]{1,0:T(8,128)(2,1)} %bitcast.49), channel_id=1, source_target_pairs={{0,8},{8,0},{16,24},{24,16},{1,9},{9,1},{17,25},{25,17},{2,10},{10... | collective-permute-start | bytes 884744 | tf_op jit(solution)/shard_map/ppermute | solution.py:50
  39.5 20.6 %collective-permute-start.13 = (bf16[192,768]{1,0:T(8,128)(2,1)}, bf16[192,768]{1,0:T(8,128)(2,1)S(1)}, u32[]{:S(2)}, u32[]{:S(2)}) collective-permute-start(bf16[192,768]{1,0:T(8,128)(2,1)} %bitcast.50), channel_id=1, source_target_pairs={{0,16},{8,24},{16,0},{24,8},{1,17},{9,25},{17,1},{25,9},{2,18},{10... | collective-permute-start | bytes 884744 | tf_op jit(solution)/shard_map/ppermute | solution.py:50
  41.1 19.5 %collective-permute-start.14 = (bf16[192,768]{1,0:T(8,128)(2,1)}, bf16[192,768]{1,0:T(8,128)(2,1)S(1)}, u32[]{:S(2)}, u32[]{:S(2)}) collective-permute-start(bf16[192,768]{1,0:T(8,128)(2,1)} %bitcast.51), channel_id=1, source_target_pairs={{0,24},{8,16},{16,8},{24,0},{1,25},{9,17},{17,9},{25,1},{2,26},{10... | collective-permute-start | bytes 884744 | tf_op jit(solution)/shard_map/ppermute | solution.py:50
  42.2 12.5 %copy-start.6 = (bf16[48,768]{1,0:T(8,128)(2,1)}, bf16[48,768]{1,0:T(8,128)(2,1)S(1)}, u32[]{:S(2)}) copy-start(bf16[48,768]{1,0:T(8,128)(2,1)S(1)} %collective-permute-done.3.refs_1_) | copy-start | bytes 221188
  42.2 6.4 %collective-permute-start.4 = (bf16[48,768]{1,0:T(8,128)(2,1)S(1)}, bf16[48,768]{1,0:T(8,128)(2,1)S(1)}, u32[]{:S(2)}, u32[]{:S(2)}) collective-permute-start(bf16[48,768]{1,0:T(8,128)(2,1)S(1)} %copy-done.37), channel_id=1, source_target_pairs={{0,4},{2,6},{4,0},{6,2},{1,5},{3,7},{5,1},{7,3},{8,12},{10,14},{12... | collective-permute-start | bytes 221192 | tf_op jit(solution)/shard_map/ppermute | solution.py:50
  48.5 6.2 %copy-start.11 = (bf16[48,768]{1,0:T(8,128)(2,1)}, bf16[48,768]{1,0:T(8,128)(2,1)S(1)}, u32[]{:S(2)}) copy-start(bf16[48,768]{1,0:T(8,128)(2,1)S(1)} %collective-permute-done.4.refs_2_) | copy-start | bytes 221188
  48.6 6.2 %collective-permute-start.5 = (bf16[48,768]{1,0:T(8,128)(2,1)S(1)}, bf16[48,768]{1,0:T(8,128)(2,1)S(1)}, u32[]{:S(2)}, u32[]{:S(2)}) collective-permute-start(bf16[48,768]{1,0:T(8,128)(2,1)S(1)} %copy-done.36), channel_id=1, source_target_pairs={{0,6},{2,4},{4,2},{6,0},{1,7},{3,5},{5,3},{7,1},{8,14},{10,12},{12... | collective-permute-start | bytes 221192 | tf_op jit(solution)/shard_map/ppermute | solution.py:50
  57.1 14.6 %collective-permute-start.6 = (bf16[192,768]{1,0:T(8,128)(2,1)}, bf16[192,768]{1,0:T(8,128)(2,1)S(1)}, u32[]{:S(2)}, u32[]{:S(2)}) collective-permute-start(bf16[192,768]{1,0:T(8,128)(2,1)} %bitcast.53), channel_id=1, source_target_pairs={{0,8},{8,0},{16,24},{24,16},{1,9},{9,1},{17,25},{25,17},{2,10},{10... | collective-permute-start | bytes 884744 | tf_op jit(solution)/shard_map/ppermute | solution.py:50
  58.6 13.6 %collective-permute-start.7 = (bf16[192,768]{1,0:T(8,128)(2,1)}, bf16[192,768]{1,0:T(8,128)(2,1)S(1)}, u32[]{:S(2)}, u32[]{:S(2)}) collective-permute-start(bf16[192,768]{1,0:T(8,128)(2,1)} %bitcast.54), channel_id=1, source_target_pairs={{0,16},{8,24},{16,0},{24,8},{1,17},{9,25},{17,1},{25,9},{2,18},{10... | collective-permute-start | bytes 884744 | tf_op jit(solution)/shard_map/ppermute | solution.py:50
  60.1 12.1 %collective-permute-start.8 = (bf16[192,768]{1,0:T(8,128)(2,1)}, bf16[192,768]{1,0:T(8,128)(2,1)S(1)}, u32[]{:S(2)}, u32[]{:S(2)}) collective-permute-start(bf16[192,768]{1,0:T(8,128)(2,1)} %bitcast.55), channel_id=1, source_target_pairs={{0,24},{8,16},{16,8},{24,0},{1,25},{9,17},{17,9},{25,1},{2,26},{10... | collective-permute-start | bytes 884744 | tf_op jit(solution)/shard_map/ppermute | solution.py:50
  81.1 1.2 collective-permute-start.23
  81.2 21.4 %collective-permute-start.19 = (f32[256,768]{1,0:T(8,128)}, f32[256,768]{1,0:T(8,128)S(1)}, u32[]{:S(2)}, u32[]{:S(2)}) collective-permute-start(f32[256,768]{1,0:T(8,128)} %get-tuple-element.60), channel_id=1, source_target_pairs={{0,1},{1,0},{2,3},{3,2},{4,5},{5,4},{6,7},{7,6},{8,9},{9,8},{10,11... | collective-permute-start | bytes 2359304 | tf_op jit(solution)/shard_map/ppermute | solution.py:50
  82.3 3.9 %collective-permute-start.24 = (f32[6528]{0:T(1024)S(1)}, f32[6528]{0:T(1024)S(1)}, u32[]{:S(2)}, u32[]{:S(2)}) collective-permute-start(f32[6528]{0:T(1024)S(1)} %pad_maximum_fusion.4), channel_id=1, source_target_pairs={{0,8},{8,0},{16,24},{24,16},{1,9},{9,1},{17,25},{25,17},{2,10},{10... | collective-permute-start | bytes 78344 | tf_op jit(solution)/shard_map/ppermute | solution.py:50
  83.5 38.8 %collective-permute-start.15 = (f32[256,768]{1,0:T(8,128)}, f32[256,768]{1,0:T(8,128)S(1)}, u32[]{:S(2)}, u32[]{:S(2)}) collective-permute-start(f32[256,768]{1,0:T(8,128)} %get-tuple-element.58), channel_id=1, source_target_pairs={{0,1},{1,0},{2,3},{3,2},{4,5},{5,4},{6,7},{7,6},{8,9},{9,8},{10,11... | collective-permute-start | bytes 2359304 | tf_op jit(solution)/shard_map/ppermute | solution.py:50
  86.3 3.9 %collective-permute-start.25 = (f32[6528]{0:T(1024)S(1)}, f32[6528]{0:T(1024)S(1)}, u32[]{:S(2)}, u32[]{:S(2)}) collective-permute-start(f32[6528]{0:T(1024)S(1)} %fusion.19), channel_id=1, source_target_pairs={{0,16},{8,24},{16,0},{24,8},{1,17},{9,25},{17,1},{25,9},{2,18},{10... | collective-permute-start | bytes 78344 | tf_op jit(solution)/shard_map/ppermute | solution.py:50
  87.9 13.6 %collective-permute-start.34 = (bf16[192,768]{1,0:T(8,128)(2,1)}, bf16[192,768]{1,0:T(8,128)(2,1)S(1)}, u32[]{:S(2)}, u32[]{:S(2)}) collective-permute-start(bf16[192,768]{1,0:T(8,128)(2,1)} %get-tuple-element.75), channel_id=1, source_target_pairs={{0,8},{8,0},{16,24},{24,16},{1,9},{9,1},{17,25},{25,17},{2,10},{10... | collective-permute-start | bytes 884744 | tf_op jit(solution)/shard_map/ppermute | solution.py:50
  89.0 13.3 %collective-permute-start.35 = (bf16[192,768]{1,0:T(8,128)(2,1)}, bf16[192,768]{1,0:T(8,128)(2,1)S(1)}, u32[]{:S(2)}, u32[]{:S(2)}) collective-permute-start(bf16[192,768]{1,0:T(8,128)(2,1)} %get-tuple-element.76), channel_id=1, source_target_pairs={{0,16},{8,24},{16,0},{24,8},{1,17},{9,25},{17,1},{25,9},{2,18},{10... | collective-permute-start | bytes 884744 | tf_op jit(solution)/shard_map/ppermute | solution.py:50
  90.2 3.9 %collective-permute-start.26 = (f32[6528]{0:T(1024)S(1)}, f32[6528]{0:T(1024)S(1)}, u32[]{:S(2)}, u32[]{:S(2)}) collective-permute-start(f32[6528]{0:T(1024)S(1)} %add.333), channel_id=1, source_target_pairs={{0,2},{2,0},{4,6},{6,4},{1,3},{3,1},{5,7},{7,5},{8,10},{10,8},{12,... | collective-permute-start | bytes 78344 | tf_op jit(solution)/shard_map/ppermute | solution.py:50
  94.2 4.8 %collective-permute-start.27 = (f32[6528]{0:T(1024)S(1)}, f32[6528]{0:T(1024)S(1)}, u32[]{:S(2)}, u32[]{:S(2)}) collective-permute-start(f32[6528]{0:T(1024)S(1)} %add.334), channel_id=1, source_target_pairs={{0,4},{2,6},{4,0},{6,2},{1,5},{3,7},{5,1},{7,3},{8,12},{10,14},{12... | collective-permute-start | bytes 78344 | tf_op jit(solution)/shard_map/ppermute | solution.py:50
  99.0 11.2 %collective-permute-start.36 = (bf16[192,768]{1,0:T(8,128)(2,1)}, bf16[192,768]{1,0:T(8,128)(2,1)}, u32[]{:S(2)}, u32[]{:S(2)}) collective-permute-start(bf16[192,768]{1,0:T(8,128)(2,1)} %get-tuple-element.77), channel_id=1, source_target_pairs={{0,24},{8,16},{16,8},{24,0},{1,25},{9,17},{17,9},{25,1},{2,26},{10... | collective-permute-start | bytes 884744 | tf_op jit(solution)/shard_map/ppermute | solution.py:50
  101.4 13.3 %collective-permute-start.28 = (bf16[192,768]{1,0:T(8,128)(2,1)}, bf16[192,768]{1,0:T(8,128)(2,1)S(1)}, u32[]{:S(2)}, u32[]{:S(2)}) collective-permute-start(bf16[192,768]{1,0:T(8,128)(2,1)} %get-tuple-element.65), channel_id=1, source_target_pairs={{0,8},{8,0},{16,24},{24,16},{1,9},{9,1},{17,25},{25,17},{2,10},{10... | collective-permute-start | bytes 884744 | tf_op jit(solution)/shard_map/ppermute | solution.py:50
  102.3 12.9 %collective-permute-start.29 = (bf16[192,768]{1,0:T(8,128)(2,1)}, bf16[192,768]{1,0:T(8,128)(2,1)}, u32[]{:S(2)}, u32[]{:S(2)}) collective-permute-start(bf16[192,768]{1,0:T(8,128)(2,1)} %get-tuple-element.66), channel_id=1, source_target_pairs={{0,16},{8,24},{16,0},{24,8},{1,17},{9,25},{17,1},{25,9},{2,18},{10... | collective-permute-start | bytes 884744 | tf_op jit(solution)/shard_map/ppermute | solution.py:50
  102.5 15.2 %collective-permute-start.30 = (bf16[192,768]{1,0:T(8,128)(2,1)}, bf16[192,768]{1,0:T(8,128)(2,1)}, u32[]{:S(2)}, u32[]{:S(2)}) collective-permute-start(bf16[192,768]{1,0:T(8,128)(2,1)} %get-tuple-element.67), channel_id=1, source_target_pairs={{0,24},{8,16},{16,8},{24,0},{1,25},{9,17},{17,9},{25,1},{2,26},{10... | collective-permute-start | bytes 884744 | tf_op jit(solution)/shard_map/ppermute | solution.py:50
  110.2 12.4 %collective-permute-start.20 = (bf16[1,2,64,768]{3,2,1,0:T(8,128)(2,1)S(1)}, bf16[1,2,64,768]{3,2,1,0:T(8,128)(2,1)S(1)}, u32[]{:S(2)}, u32[]{:S(2)}) collective-permute-start(bf16[1,2,64,768]{3,2,1,0:T(8,128)(2,1)S(1)} %split.62), channel_id=1, source_target_pairs={{0,2},{2,0},{4,6},{6,4},{1,3},{3,1},{5,7},{7,5},{8,10},{10,8},{12,... | collective-permute-start | bytes 589832 | tf_op jit(solution)/shard_map/ppermute | solution.py:50
  112.5 9.9 %copy-start.2 = (f32[256,768]{1,0:T(8,128)S(1)}, f32[256,768]{1,0:T(8,128)}, u32[]{:S(2)}) copy-start(f32[256,768]{1,0:T(8,128)} %get-tuple-element.57) | copy-start | bytes 2359300
  114.7 29.1 %collective-permute-start.37 = (bf16[48,768]{1,0:T(8,128)(2,1)}, bf16[48,768]{1,0:T(8,128)(2,1)S(1)}, u32[]{:S(2)}, u32[]{:S(2)}) collective-permute-start(bf16[48,768]{1,0:T(8,128)(2,1)} %get-tuple-element.79), channel_id=1, source_target_pairs={{0,2},{2,0},{4,6},{6,4},{1,3},{3,1},{5,7},{7,5},{8,10},{10,8},{12,... | collective-permute-start | bytes 221192 | tf_op jit(solution)/shard_map/ppermute | solution.py:50
  115.2 30.7 %collective-permute-start.38 = (bf16[48,768]{1,0:T(8,128)(2,1)}, bf16[48,768]{1,0:T(8,128)(2,1)S(1)}, u32[]{:S(2)}, u32[]{:S(2)}) collective-permute-start(bf16[48,768]{1,0:T(8,128)(2,1)} %get-tuple-element.80), channel_id=1, source_target_pairs={{0,4},{2,6},{4,0},{6,2},{1,5},{3,7},{5,1},{7,3},{8,12},{10,14},{12... | collective-permute-start | bytes 221192 | tf_op jit(solution)/shard_map/ppermute | solution.py:50
  117.7 30.0 %collective-permute-start.39 = (bf16[48,768]{1,0:T(8,128)(2,1)}, bf16[48,768]{1,0:T(8,128)(2,1)S(1)}, u32[]{:S(2)}, u32[]{:S(2)}) collective-permute-start(bf16[48,768]{1,0:T(8,128)(2,1)} %get-tuple-element.81), channel_id=1, source_target_pairs={{0,6},{2,4},{4,2},{6,0},{1,7},{3,5},{5,3},{7,1},{8,14},{10,12},{12... | collective-permute-start | bytes 221192 | tf_op jit(solution)/shard_map/ppermute | solution.py:50
  122.4 27.9 %collective-permute-start.31 = (bf16[48,768]{1,0:T(8,128)(2,1)}, bf16[48,768]{1,0:T(8,128)(2,1)S(1)}, u32[]{:S(2)}, u32[]{:S(2)}) collective-permute-start(bf16[48,768]{1,0:T(8,128)(2,1)} %get-tuple-element.69), channel_id=1, source_target_pairs={{0,2},{2,0},{4,6},{6,4},{1,3},{3,1},{5,7},{7,5},{8,10},{10,8},{12,... | collective-permute-start | bytes 221192 | tf_op jit(solution)/shard_map/ppermute | solution.py:50
  122.6 7.6 %collective-permute-start.16 = (bf16[1,2,64,768]{3,2,1,0:T(8,128)(2,1)S(1)}, bf16[1,2,64,768]{3,2,1,0:T(8,128)(2,1)S(1)}, u32[]{:S(2)}, u32[]{:S(2)}) collective-permute-start(bf16[1,2,64,768]{3,2,1,0:T(8,128)(2,1)S(1)} %split.63), channel_id=1, source_target_pairs={{0,2},{2,0},{4,6},{6,4},{1,3},{3,1},{5,7},{7,5},{8,10},{10,8},{12,... | collective-permute-start | bytes 589832 | tf_op jit(solution)/shard_map/ppermute | solution.py:50
  130.1 6.4 %collective-permute-start.21 = (bf16[1,1,64,768]{3,2,1,0:T(8,128)(2,1)S(1)}, bf16[1,1,64,768]{3,2,1,0:T(8,128)(2,1)S(1)}, u32[]{:S(2)}, u32[]{:S(2)}) collective-permute-start(bf16[1,1,64,768]{3,2,1,0:T(8,128)(2,1)S(1)} %split.64), channel_id=1, source_target_pairs={{0,4},{2,6},{4,0},{6,2},{1,5},{3,7},{5,1},{7,3},{8,12},{10,14},{12... | collective-permute-start | bytes 294920 | tf_op jit(solution)/shard_map/ppermute | solution.py:50
  136.5 7.2 %collective-permute-start.17 = (bf16[1,1,64,768]{3,2,1,0:T(8,128)(2,1)S(1)}, bf16[1,1,64,768]{3,2,1,0:T(8,128)(2,1)S(1)}, u32[]{:S(2)}, u32[]{:S(2)}) collective-permute-start(bf16[1,1,64,768]{3,2,1,0:T(8,128)(2,1)S(1)} %split.65), channel_id=1, source_target_pairs={{0,4},{2,6},{4,0},{6,2},{1,5},{3,7},{5,1},{7,3},{8,12},{10,14},{12... | collective-permute-start | bytes 294920 | tf_op jit(solution)/shard_map/ppermute | solution.py:50
  136.8 7.0 %copy-start.39 = (bf16[48,768]{1,0:T(8,128)(2,1)S(1)}, bf16[48,768]{1,0:T(8,128)(2,1)}, u32[]{:S(2)}) copy-start(bf16[48,768]{1,0:T(8,128)(2,1)} %get-tuple-element.70) | copy-start | bytes 221188
  143.7 6.6 %collective-permute-start.32 = (bf16[48,768]{1,0:T(8,128)(2,1)S(1)}, bf16[48,768]{1,0:T(8,128)(2,1)S(1)}, u32[]{:S(2)}, u32[]{:S(2)}) collective-permute-start(bf16[48,768]{1,0:T(8,128)(2,1)S(1)} %copy-done.39), channel_id=1, source_target_pairs={{0,4},{2,6},{4,0},{6,2},{1,5},{3,7},{5,1},{7,3},{8,12},{10,14},{12... | collective-permute-start | bytes 221192 | tf_op jit(solution)/shard_map/ppermute | solution.py:50
  144.6 6.2 %collective-permute-start.33 = (bf16[48,768]{1,0:T(8,128)(2,1)S(1)}, bf16[48,768]{1,0:T(8,128)(2,1)S(1)}, u32[]{:S(2)}, u32[]{:S(2)}) collective-permute-start(bf16[48,768]{1,0:T(8,128)(2,1)S(1)} %copy-done.38), channel_id=1, source_target_pairs={{0,6},{2,4},{4,2},{6,0},{1,7},{3,5},{5,3},{7,1},{8,14},{10,12},{12... | collective-permute-start | bytes 221192 | tf_op jit(solution)/shard_map/ppermute | solution.py:50
  145.9 7.4 %collective-permute-start.18 = (bf16[1,64,768]{2,1,0:T(8,128)(2,1)S(1)}, bf16[1,64,768]{2,1,0:T(8,128)(2,1)S(1)}, u32[]{:S(2)}, u32[]{:S(2)}) collective-permute-start(bf16[1,64,768]{2,1,0:T(8,128)(2,1)S(1)} %get-tuple-element.95), channel_id=1, source_target_pairs={{0,1},{1,0},{2,3},{3,2},{4,5},{5,4},{6,7},{7,6},{8,9},{9,8},{10,11... | collective-permute-start | bytes 294920 | tf_op jit(solution)/shard_map/ppermute | solution.py:50
  146.5 9.0 %copy-start.19 = (f32[768]{0:T(1024)}, f32[768]{0:T(1024)S(1)}, u32[]{:S(2)}) copy-start(f32[768]{0:T(1024)S(1)} %get-tuple-element.135) | copy-start | bytes 9220
  153.2 1.4 collective-permute-start.22
  (32 other events, 52.1 us)
where the time goes:
time: 157 us; the launch traced here: 156 us
  waiting for transfers between devices  55.1 us (35%)
  starting transfers between devices  44.3 us (28%)
  Pallas kernels  31.1 us (20%)
  local copies, waits for them, and re-layouts  17.1 us (11%)
  other arithmetic  7.25 us (5%)
    ppermute x40, waiting for transfers between devices, swap(): lax.ppermute(value, axis, [(i, i ^ bit) for i in range(lax.axis_size(axis...  55.1 us
    ppermute x40, starting transfers between devices, swap(): lax.ppermute(value, axis, [(i, i ^ bit) for i in range(lax.axis_size(axis...  44.3 us
    unnamed x82, local copies, waits for them, and re-layouts  9.11 us
    pallas_call x1, Pallas kernels, on_device(): local_kernel(functools.partial(attention_kernel, fsdp_count, tp_count, ne...  8.91 us
    pallas_call x1, Pallas kernels, on_device(): local_kernel(functools.partial(mlp_kernel, fsdp_count, tp_count, near, he...  7.32 us
    pallas_call x2, Pallas kernels, scatter_weights(): local_kernel(functools.partial(sum_blocks_kernel, fsdp_count), [shaped((r...  4.22 us
    pallas_call x2, Pallas kernels, own_rows(): local_kernel(ordered_kernel, shaped(shape, bf16))(*parts)  3.5 us
  transfers between devices with their start and end apart: 40, of which 17 were waited for; matrix products, arithmetic and copies ran while one was open for 9% of the time, Pallas kernels for 14%

commit v1 on v0

--- a/solution.py
+++ b/solution.py
@@ -121,6 +121,7 @@
 
 VMEM_LIMIT = 60 * 1024 * 1024
 LANES = 128
+SUBLANES = 16
 
 
 def local_kernel(body, out_shapes, scratch=(), flops=0, moved=0):
@@ -181,25 +182,22 @@
         out[...] = part
 
 
-def ordered_kernel(*refs):
-    parts, out = refs[:-1], refs[-1]
-    for r, part in enumerate(swapped([part[...] for part in parts], lax.axis_index("ctx"))):
-        out[r] = part
-
-
-def place_weight(parts, weight):
-    at = lax.axis_index("fsdp")
-    block = parts[0].shape[0]
+def place_weight(parts, weight, count):
+    fsdp_at, ctx_at = lax.axis_index("fsdp"), lax.axis_index("ctx")
+    rows = parts[0].shape[0] // count
     for k, part in enumerate(parts):
-        start = pl.multiple_of((at ^ k) * block, 16)
-        weight[pl.ds(start, block), :] = part[...]
+        for j in range(count):
+            place = (fsdp_at ^ k) * count + ((ctx_at ^ j) if count > 1 else 0)
+            weight[pl.ds(pl.multiple_of(place * rows, SUBLANES), rows), :] = part[
+                j * rows : (j + 1) * rows, :
+            ]
 
 
 def send_blocks(total, outs):
     at = lax.axis_index("fsdp")
     block = outs[0].shape[0]
     for k, out in enumerate(outs):
-        start = pl.multiple_of((at ^ k) * block, 16)
+        start = pl.multiple_of((at ^ k) * block, SUBLANES)
         out[...] = total[pl.ds(start, block), :].astype(out.dtype)
 
 
@@ -211,6 +209,7 @@
     own_heads,
     copies,
     seqs,
+    row_blocks,
     *refs,
 ):
     row_refs = refs[:core_count]
@@ -220,9 +219,9 @@
     ]
     gain, shift = norms[0:1, :], norms[1:2, :]
     outs = refs[core_count + fsdp_count + 6 :]
-    branch, norm_out, sums = outs[:3]
-    grad_outs = outs[3 : 3 + fsdp_count]
-    weight, grads, mixed, total = outs[3 + fsdp_count :]
+    branch, norm_out, sums, bias_out = outs[:4]
+    grad_outs = outs[4 : 4 + fsdp_count]
+    weight, grads, mixed, total = outs[4 + fsdp_count :]
     cols = weight.shape[1]
     features = own_heads * HD
     qkv_cols = 3 * features
@@ -231,7 +230,7 @@
     seq_at = lax.rem(lax.div(ctx_at, head_groups), seqs)
     core = lax.div(seq_at, near) ^ lax.axis_index("tp")
     inner = lax.rem(seq_at, near)
-    place_weight(parts, weight)
+    place_weight(parts, weight, row_blocks)
     seq_tokens, seq_grads = row_refs[0][0, inner], row_refs[0][1, inner]
     for j in range(1, core_count):
         seq_tokens = jnp.where(core == j, row_refs[j][0, inner], seq_tokens)
@@ -293,30 +292,28 @@
         [
             jnp.sum(norm_grad * centred, axis=0, keepdims=True),
             jnp.sum(norm_grad, axis=0, keepdims=True),
-            jnp.sum(proj_grad, axis=0, keepdims=True),
         ],
         axis=0,
     )
-
-
-def mlp_kernel(fsdp_count, core_count, near, head_groups, seqs, padded, *refs):
+    bias_out[...] = jnp.sum(proj_grad, axis=0, keepdims=True)
+
+
+def mlp_kernel(fsdp_count, core_count, near, head_groups, seqs, padded, row_blocks, *refs):
     row_refs = refs[:core_count]
     parts = refs[core_count : core_count + fsdp_count]
-    norm_ref, bias, attn_branch, attn_norm = refs[
-        core_count + fsdp_count : core_count + fsdp_count + 4
+    norm_ref, bias, attn_branch, attn_norm, attn_sums = refs[
+        core_count + fsdp_count : core_count + fsdp_count + 5
     ]
     gain, shift = norm_ref[2:3, :], norm_ref[3:4, :]
-    outs = refs[core_count + fsdp_count + 4 :]
-    branches = outs[:core_count]
-    norms = outs[core_count : 2 * core_count]
-    sums, bias_out = outs[2 * core_count : 2 * core_count + 2]
-    grad_outs = outs[2 * core_count + 2 : 2 * core_count + 2 + fsdp_count]
-    weight, total = outs[2 * core_count + 2 + fsdp_count :]
+    outs = refs[core_count + fsdp_count + 5 :]
+    both, bias_out = outs[:core_count], outs[core_count]
+    grad_outs = outs[core_count + 1 : core_count + 1 + fsdp_count]
+    weight, total = outs[core_count + 1 + fsdp_count :]
     size = attn_branch.shape[0]
     seq_at = lax.rem(lax.div(lax.axis_index("ctx"), head_groups), seqs)
     core = lax.div(seq_at, near) ^ lax.axis_index("tp")
     inner = lax.rem(seq_at, near)
-    place_weight(parts, weight)
+    place_weight(parts, weight, row_blocks)
     up, down = weight[:, :padded], weight[:, padded:]
     gain_sum = shift_sum = bias_sum = 0.0
     for j in range(core_count):
@@ -347,10 +344,15 @@
         for i in range(near):
             here = (core == j) & (inner == i)
             span = slice(i * size, (i + 1) * size)
-            branches[j][span, :] = branch[span] + jnp.where(here, attn_branch[...], 0.0)
-            norms[j][span, :] = norm_grad[span] + jnp.where(here, attn_norm[...], 0.0)
+            both[j][span, :] = branch[span] + jnp.where(here, attn_branch[...], 0.0)
+            span_norm = slice((near + i) * size, (near + i + 1) * size)
+            both[j][span_norm, :] = norm_grad[span] + jnp.where(here, attn_norm[...], 0.0)
     send_blocks(total, grad_outs)
-    sums[...] = jnp.concatenate([gain_sum, shift_sum], axis=0)
+    for j in range(core_count):
+        both[j][2 * near * size : 2 * near * size + 2, :] = attn_sums[...]
+        both[j][2 * near * size + 2 : 2 * near * size + 3, :] = gain_sum
+        both[j][2 * near * size + 3 : 2 * near * size + 4, :] = shift_sum
+        both[j][2 * near * size + 4 :, :] = jnp.zeros((4, width), jnp.float32)
     bias_out[...] = bias_sum
 
 
@@ -446,9 +448,10 @@
     chunks = gather_chunks(message[:, :, None], "ctx", 2)
     chunks = chunks.reshape(2, near, size, width)
 
+    loose = rows_here % SUBLANES == 0
+
     def own_rows(parts):
-        shape = (ctx_count, rows_here, parts[0].shape[1])
-        return local_kernel(ordered_kernel, shaped(shape, bf16))(*parts).reshape(block_rows, -1)
+        return jnp.concatenate(parts if loose else swapped(parts, ctx_at), axis=0)
 
     early_parts = spread(own_rows(early_rows), "fsdp")
     late_parts = spread(own_rows(late_rows), "fsdp")
@@ -463,6 +466,7 @@
     cos_table, sin_table = rotary_tables(position)
     place = position.astype(f32)
     norms = jnp.stack([attn_gain, attn_shift, mlp_gain, mlp_shift])
+    column_sums = jnp.sum(out_grad, axis=(0, 1))
 
     def row(vector):
         return vector.reshape(1, -1)
@@ -477,11 +481,21 @@
             shaped((block_rows, columns), bf16 if k else f32) for k in range(fsdp_count)
         ]
 
-    attn_branch, attn_norm, attn_sums, *early_grads = local_kernel(
+    row_blocks = ctx_count if loose else 1
+    attn_branch, attn_norm, attn_sums, qkv_bias_part, *early_grads = local_kernel(
         functools.partial(
-            attention_kernel, fsdp_count, tp_count, near, head_groups, own_heads, copies, seqs
+            attention_kernel,
+            fsdp_count,
+            tp_count,
+            near,
+            head_groups,
+            own_heads,
+            copies,
+            seqs,
+            row_blocks,
         ),
-        [shaped((size, width), f32), shaped((size, width), f32), shaped((3, cols), f32)]
+        [shaped((size, width), f32)] * 2
+        + [shaped((2, width), f32), shaped((1, cols), f32)]
         + grad_blocks(cols),
         [
             pltpu.VMEM((width, cols), bf16),
@@ -502,9 +516,11 @@
         row(place),
     )
     outs = local_kernel(
-        functools.partial(mlp_kernel, fsdp_count, tp_count, near, head_groups, seqs, padded),
-        [shaped((near_rows, width), f32)] * (2 * tp_count)
-        + [shaped((2, width), f32), shaped((1, padded), f32)]
+        functools.partial(
+            mlp_kernel, fsdp_count, tp_count, near, head_groups, seqs, padded, row_blocks
+        ),
+        [shaped((2 * near_rows + 8, width), f32)] * tp_count
+        + [shaped((1, padded), f32)]
         + grad_blocks(2 * padded),
         [pltpu.VMEM((width, 2 * padded), bf16), pltpu.VMEM((width, 2 * padded), f32)],
         flops=12 * seqs * size * width * padded,
@@ -516,14 +532,15 @@
         row(up_own),
         attn_branch,
         attn_norm,
-    )
-    branch_parts, norm_parts = outs[:tp_count], outs[tp_count : 2 * tp_count]
-    mlp_sums, up_bias_part = outs[2 * tp_count : 2 * tp_count + 2]
-    late_grads = outs[2 * tp_count + 2 :]
-
-    def scatter_rows(parts):
-        half = sum(exchange(parts, "tp")).reshape(near, ctx_count, length, width)
-        return scatter_chunks(half, "ctx", 1).reshape(near, length, width)
+        attn_sums,
+    )
+    row_parts, up_bias_part = outs[:tp_count], outs[tp_count]
+    late_grads = outs[tp_count + 1 :]
+    row_sums = sum(exchange(row_parts, "tp"))
+    gain_parts = row_sums[2 * near_rows : 2 * near_rows + 4].reshape(-1)
+    row_sums = row_sums[: 2 * near_rows].reshape(2, near, ctx_count, length, width)
+    row_sums = scatter_chunks(row_sums, "ctx", 2).reshape(2, near, length, width)
+    branches, inner = row_sums[0], row_sums[1]
 
     def both_cores(half):
         return jnp.concatenate(swapped(spread(half, "tp"), tp_at), axis=0)
@@ -539,8 +556,6 @@
 
     early_pieces = scatter_weights(early_grads)
     late_pieces = scatter_weights(late_grads)
-    branches = scatter_rows(branch_parts)
-    inner = scatter_rows(norm_parts)
     block_half = own_tokens.astype(f32) + branches + (dense_bias + down_bias)
     block_out = both_cores(block_half.astype(bf16))
     own_centred, own_inverse = normed_rows(own_tokens.astype(f32))
@@ -559,15 +574,14 @@
         [shaped(up_weight.shape, f32), shaped(down_weight.shape[::-1], f32)],
     )(*late_pieces)
 
-    gain_parts = jnp.concatenate([attn_sums[:2].reshape(-1), mlp_sums.reshape(-1)])
     bias_parts = jnp.concatenate(
         [
-            jnp.sum(out_grad, axis=(0, 1)),
-            one_hot_slots(attn_sums[2, :qkv_cols], head_at, head_groups),
+            column_sums,
+            one_hot_slots(qkv_bias_part[0, :qkv_cols], head_at, head_groups),
             one_hot_slots(up_bias_part[0, :ff], ctx_at, ctx_count),
         ]
     )
-    small = jnp.concatenate([butterfly(gain_parts, "tp"), bias_parts])
+    small = jnp.concatenate([gain_parts, bias_parts])
     small = butterfly(butterfly(small, "fsdp"), "ctx")
     cuts = []
     start = 0

time: 157 us -> 138 us (0.88)
  waiting for transfers between devices: 55.1 us -> 37.7 us
  local copies, waits for them, and re-layouts: 17.1 us -> 10 us
  starting transfers between devices: 44.3 us -> 49.5 us
  other arithmetic: 7.25 us -> 11.1 us
  Pallas kernels: 31.1 us -> 27.9 us
    ppermute x40 -> x36, waiting for transfers between devices: 55.1 us -> 37.7 us  [swap(): lax.ppermute(value, axis, [(i, i ^ bit) for i in range(lax.axis_size(axis...]
    ppermute x40 -> x36, starting transfers between devices: 44.3 us -> 49.5 us  [swap(): lax.ppermute(value, axis, [(i, i ^ bit) for i in range(lax.axis_size(axis...]
    unnamed x82 -> x79, local copies, waits for them, and re-layouts: 9.11 us -> 4.07 us
    pallas_call x2 -> x0, Pallas kernels: 3.5 us -> none  [own_rows(): local_kernel(ordered_kernel, shaped(shape, bf16))(*parts)]
  transfers between devices with their start and end apart: 40 -> 36, of which waited for: 17 -> 13; matrix products, arithmetic and copies ran while one was open for 9% -> 12% of each run, Pallas kernels for 14% -> 14%
where the time goes in v1:
time: 138 us
  starting transfers between devices  49.5 us (36%)
  waiting for transfers between devices  37.7 us (27%)
  Pallas kernels  27.9 us (20%)
  other arithmetic  11.1 us (8%)
  local copies, waits for them, and re-layouts  10 us (7%)
    ppermute x36, starting transfers between devices, swap(): lax.ppermute(value, axis, [(i, i ^ bit) for i in range(lax.axis_size(axis...  49.5 us
    ppermute x36, waiting for transfers between devices, swap(): lax.ppermute(value, axis, [(i, i ^ bit) for i in range(lax.axis_size(axis...  37.7 us
    pallas_call x1, Pallas kernels, on_device(): local_kernel(functools.partial(attention_kernel, fsdp_count, tp_count, ne...  8.97 us
    pallas_call x1, Pallas kernels, on_device(): local_kernel(functools.partial(mlp_kernel, fsdp_count, tp_count, near, he...  7.5 us
    pallas_call x2, Pallas kernels, scatter_weights(): local_kernel(functools.partial(sum_blocks_kernel, fsdp_count), [shaped((r...  4.24 us
    unnamed x79, local copies, waits for them, and re-layouts  4.07 us
  transfers between devices with their start and end apart: 36, of which 13 were waited for; matrix products, arithmetic and copies ran while one was open for 12% of the time, Pallas kernels for 14%

profile of v1, /device:TPU:0, one launch (start us, length us, event | category | flops | bytes accessed | tf_op | source)
XLA Modules:
  0.0 137.6 jit_solution(10475064657278654979)
XLA Ops:
  0.7 1.7 %shard_map.255 = (bf16[48,768]{1,0:T(8,128)(2,1)}, bf16[48,768]{1,0:T(8,128)(2,1)}) custom-call(bf16[48,1152]{1,0:T(8,128)(2,1)} %qkv_ref.1, bf16[48,384]{1,0:T(8,128)(2,1)} %bitcast.51), custom_call_target="tpu_custom_call" | custom-call | tf_op jit(solution)/shard_map/pallas_call | solution.py:430
  2.4 5.1 %collective-permute-start.11 = (bf16[48,768]{1,0:T(8,128)(2,1)}, bf16[48,768]{1,0:T(8,128)(2,1)S(1)}, u32[]{:S(2)}, u32[]{:S(2)}) collective-permute-start(bf16[48,768]{1,0:T(8,128)(2,1)} %get-tuple-element.52), channel_id=1, source_target_pairs={{0,6},{2,4},{4,2},{6,0},{1,7},{3,5},{5,3},{7,1},{8,14},{10,12},{12... | collective-permute-start | bytes 221192 | tf_op jit(solution)/shard_map/ppermute | solution.py:50
  8.0 1.0 convert_bitcast_fusion
  9.1 1.1 convert_reduce_fusion
  10.2 2.4 %collective-permute-start = (bf16[2,1,1,64,768]{4,3,0,2,1:T(8,128)(2,1)S(1)}, bf16[2,1,1,64,768]{4,3,0,2,1:T(8,128)(2,1)S(1)}, u32[]{:S(2)}, u32[]{:S(2)}) collective-permute-start(bf16[2,1,1,64,768]{4,3,0,2,1:T(8,128)(2,1)S(1)} %maximum_bitcast_fusion), channel_id=1, source_target_pairs={{0,4},{2,6},{4,0},{6,2},{1,5},{3,7},{5,1},{7,3},{8,12},{10,14},{12... | collective-permute-start | bytes 589832 | tf_op jit(solution)/shard_map/ppermute | solution.py:50
  12.6 1.7 %shard_map.254 = (bf16[48,768]{1,0:T(8,128)(2,1)}, bf16[48,768]{1,0:T(8,128)(2,1)}, bf16[48,768]{1,0:T(8,128)(2,1)}, bf16[48,768]{1,0:T(8,128)(2,1)}) custom-call(bf16[48,1536]{1,0:T(8,128)(2,1)} %up_ref.1, bf16[48,1536]{1,0:T(8,128)(2,1)} %bitcast.50), custom_call_target="tpu_custom_call" | custom-call | tf_op jit(solution)/shard_map/pallas_call | solution.py:434
  14.3 2.0 %collective-permute-start.3 = (bf16[48,768]{1,0:T(8,128)(2,1)}, bf16[48,768]{1,0:T(8,128)(2,1)S(1)}, u32[]{:S(2)}, u32[]{:S(2)}) collective-permute-start(bf16[48,768]{1,0:T(8,128)(2,1)} %get-tuple-element.48), channel_id=1, source_target_pairs={{0,2},{2,0},{4,6},{6,4},{1,3},{3,1},{5,7},{7,5},{8,10},{10,8},{12,... | collective-permute-start | bytes 221192 | tf_op jit(solution)/shard_map/ppermute | solution.py:50
  16.4 0.7 select_reduce_fusion.3
  17.2 0.8 slice_select_fusion.2
  18.7 4.0 %collective-permute-done = bf16[2,1,1,64,768]{4,3,0,2,1:T(8,128)(2,1)S(1)} collective-permute-done((bf16[2,1,1,64,768]{4,3,0,2,1:T(8,128)(2,1)S(1)}, bf16[2,1,1,64,768]{4,3,0,2,1:T(8,128)(2,1)S(1)}, u32[]{:S(2)}, u32[]{:S(2)}) %collective-permute-start) | collective-permute-done | bytes 196640 | tf_op jit(solution)/shard_map/ppermute | solution.py:50
  24.1 0.8 copy.46.refs_10_
  24.9 0.9 concatenate.75.refs_8_
  25.8 0.9 concatenate.76.refs_9_
  27.4 6.1 %collective-permute-done.1 = bf16[2,1,2,64,768]{4,3,0,2,1:T(8,128)(2,1)S(1)} collective-permute-done((bf16[2,1,2,64,768]{4,3,0,2,1:T(8,128)(2,1)S(1)}, bf16[2,1,2,64,768]{4,3,0,2,1:T(8,128)(2,1)S(1)}, u32[]{:S(2)}, u32[]{:S(2)}) %collective-permute-start.1) | collective-permute-done | bytes 393248 | tf_op jit(solution)/shard_map/ppermute | solution.py:50
  33.5 1.7 %collective-permute-start.4 = (bf16[48,768]{1,0:T(8,128)(2,1)S(1)}, bf16[48,768]{1,0:T(8,128)(2,1)S(1)}, u32[]{:S(2)}, u32[]{:S(2)}) collective-permute-start(bf16[48,768]{1,0:T(8,128)(2,1)S(1)} %copy-done.34), channel_id=1, source_target_pairs={{0,4},{2,6},{4,0},{6,2},{1,5},{3,7},{5,1},{7,3},{8,12},{10,14},{12... | collective-permute-start | bytes 221192 | tf_op jit(solution)/shard_map/ppermute | solution.py:50
  35.4 1.8 %collective-permute-start.5 = (bf16[48,768]{1,0:T(8,128)(2,1)S(1)}, bf16[48,768]{1,0:T(8,128)(2,1)S(1)}, u32[]{:S(2)}, u32[]{:S(2)}) collective-permute-start(bf16[48,768]{1,0:T(8,128)(2,1)S(1)} %copy-done.33), channel_id=1, source_target_pairs={{0,6},{2,4},{4,2},{6,0},{1,7},{3,5},{5,3},{7,1},{8,14},{10,12},{12... | collective-permute-start | bytes 221192 | tf_op jit(solution)/shard_map/ppermute | solution.py:50
  37.2 2.5 %collective-permute-start.14 = (bf16[192,768]{1,0:T(8,128)(2,1)S(1)}, bf16[192,768]{1,0:T(8,128)(2,1)S(1)}, u32[]{:S(2)}, u32[]{:S(2)}) collective-permute-start(bf16[192,768]{1,0:T(8,128)(2,1)S(1)} %constant_dynamic-update-slice_fusion.4.refs_2_), channel_id=1, source_target_pairs={{0,24},{8,16},{16,8},{24,0},{1,25},{9,17},{17,9},{25,1},{2,26},{10... | collective-permute-start | bytes 884744 | tf_op jit(solution)/shard_map/ppermute | solution.py:50
  40.9 1.1 collective-permute-done.5
  42.0 2.5 %collective-permute-start.8 = (bf16[192,768]{1,0:T(8,128)(2,1)S(1)}, bf16[192,768]{1,0:T(8,128)(2,1)S(1)}, u32[]{:S(2)}, u32[]{:S(2)}) collective-permute-start(bf16[192,768]{1,0:T(8,128)(2,1)S(1)} %constant_dynamic-update-slice_fusion.refs_2_), channel_id=1, source_target_pairs={{0,24},{8,16},{16,8},{24,0},{1,25},{9,17},{17,9},{25,1},{2,26},{10... | collective-permute-start | bytes 884744 | tf_op jit(solution)/shard_map/ppermute | solution.py:50
  44.5 3.6 %collective-permute-done.14.refs_5_ = bf16[192,768]{1,0:T(8,128)(2,1)S(1)} collective-permute-done((bf16[192,768]{1,0:T(8,128)(2,1)S(1)}, bf16[192,768]{1,0:T(8,128)(2,1)S(1)}, u32[]{:S(2)}, u32[]{:S(2)}) %collective-permute-start.14) | collective-permute-done | bytes 294944 | tf_op jit(solution)/shard_map/ppermute | solution.py:50
  48.1 1.5 %collective-permute-start.7 = (bf16[192,768]{1,0:T(8,128)(2,1)S(1)}, bf16[192,768]{1,0:T(8,128)(2,1)S(1)}, u32[]{:S(2)}, u32[]{:S(2)}) collective-permute-start(bf16[192,768]{1,0:T(8,128)(2,1)S(1)} %constant_dynamic-update-slice_fusion.refs_2_), channel_id=1, source_target_pairs={{0,16},{8,24},{16,0},{24,8},{1,17},{9,25},{17,1},{25,9},{2,18},{10... | collective-permute-start | bytes 884744 | tf_op jit(solution)/shard_map/ppermute | solution.py:50
  49.6 4.9 %collective-permute-done.13.refs_4_ = bf16[192,768]{1,0:T(8,128)(2,1)S(1)} collective-permute-done((bf16[192,768]{1,0:T(8,128)(2,1)S(1)}, bf16[192,768]{1,0:T(8,128)(2,1)S(1)}, u32[]{:S(2)}, u32[]{:S(2)}) %collective-permute-start.13) | collective-permute-done | bytes 294944 | tf_op jit(solution)/shard_map/ppermute | solution.py:50
  54.5 1.5 %collective-permute-start.6 = (bf16[192,768]{1,0:T(8,128)(2,1)S(1)}, bf16[192,768]{1,0:T(8,128)(2,1)S(1)}, u32[]{:S(2)}, u32[]{:S(2)}) collective-permute-start(bf16[192,768]{1,0:T(8,128)(2,1)S(1)} %constant_dynamic-update-slice_fusion.refs_2_), channel_id=1, source_target_pairs={{0,8},{8,0},{16,24},{24,16},{1,9},{9,1},{17,25},{25,17},{2,10},{10... | collective-permute-start | bytes 884744 | tf_op jit(solution)/shard_map/ppermute | solution.py:50
  57.3 9.0 %shard_map.256 = (f32[256,768]{1,0:T(8,128)}, f32[256,768]{1,0:T(8,128)}, f32[2,768]{1,0:T(2,128)}, f32[1,768]{1,0:T(1,128)}, f32[192,768]{1,0:T(8,128)}, /*inde...) custom-call(bf16[2,1,256,768]{3,2,1,0:T(8,128)(2,1)} %bitcast.42, ...), custom_call_target="tpu_custom_call" | custom-call | flops 2415919104 | bytes 3145728 | tf_op jit(solution)/shard_map/pallas_call | solution.py:485
  67.2 7.5 %shard_map.257 = (f32[520,768]{1,0:T(8,128)}, f32[520,768]{1,0:T(8,128)}, f32[1,384]{1,0:T(1,128)}, f32[192,768]{1,0:T(8,128)}, bf16[192,768]{1,0:T(8,128)(2,1)}...) custom-call(bf16[2,1,256,768]{3,2,1,0:T(8,128)(2,1)} %bitcast.43, ...), custom_call_target="tpu_custom_call" | custom-call | flops 1811939328 | bytes 6291456 | tf_op jit(solution)/shard_map/pallas_call | solution.py:518
  75.0 0.8 collective-permute-start.24
  75.9 1.2 collective-permute-start.25
  78.4 1.1 copy-done.2
  79.5 2.1 %add.306 = f32[520,768]{1,0:T(8,128)S(1)} add(f32[520,768]{1,0:T(8,128)} %get-tuple-element.56, f32[520,768]{1,0:T(8,128)} %copy-done.2) | non-fusion elementwise | flops 399360 | bytes 4792320 | tf_op jit(solution)/shard_map/add | solution.py:539
  81.7 1.1 collective-permute-start.20
  82.8 2.0 %collective-permute-start.26 = (bf16[192,768]{1,0:T(8,128)(2,1)}, bf16[192,768]{1,0:T(8,128)(2,1)}, u32[]{:S(2)}, u32[]{:S(2)}) collective-permute-start(bf16[192,768]{1,0:T(8,128)(2,1)} %get-tuple-element.63), channel_id=1, source_target_pairs={{0,24},{8,16},{16,8},{24,0},{1,25},{9,17},{17,9},{25,1},{2,26},{10... | collective-permute-start | bytes 884744 | tf_op jit(solution)/shard_map/ppermute | solution.py:50
  85.8 1.8 %collective-permute-start.21 = (f32[6528]{0:T(1024)S(1)}, f32[6528]{0:T(1024)S(1)}, u32[]{:S(2)}, u32[]{:S(2)}) collective-permute-start(f32[6528]{0:T(1024)S(1)} %fusion.17), channel_id=1, source_target_pairs={{0,16},{8,24},{16,0},{24,8},{1,17},{9,25},{17,1},{25,9},{2,18},{10... | collective-permute-start | bytes 78344 | tf_op jit(solution)/shard_map/ppermute | solution.py:50
  87.9 0.9 collective-permute-start.31
  88.8 4.7 %collective-permute-done.21 = f32[6528]{0:T(1024)S(1)} collective-permute-done((f32[6528]{0:T(1024)S(1)}, f32[6528]{0:T(1024)S(1)}, u32[]{:S(2)}, u32[]{:S(2)}) %collective-permute-start.21) | collective-permute-done | bytes 26144 | tf_op jit(solution)/shard_map/ppermute | solution.py:50
  93.5 1.5 %collective-permute-start.32 = (bf16[192,768]{1,0:T(8,128)(2,1)}, bf16[192,768]{1,0:T(8,128)(2,1)}, u32[]{:S(2)}, u32[]{:S(2)}) collective-permute-start(bf16[192,768]{1,0:T(8,128)(2,1)} %get-tuple-element.73), channel_id=1, source_target_pairs={{0,24},{8,16},{16,8},{24,0},{1,25},{9,17},{17,9},{25,1},{2,26},{10... | collective-permute-start | bytes 884744 | tf_op jit(solution)/shard_map/ppermute | solution.py:50
  95.5 2.1 %shard_map.258 = (f32[48,768]{1,0:T(8,128)}, bf16[48,768]{1,0:T(8,128)(2,1)}, bf16[48,768]{1,0:T(8,128)(2,1)}, bf16[48,768]{1,0:T(8,128)(2,1)}) custom-call(f32[4,48,768]{2,1,0:T(8,128)} %bitcast.45, bf16[4,48,768]{2,1,0:T(8,128)(2,1)} %bitcast.46, bf16[4,48,768]{2,1,0:T(8,128)(2,1)} %bitcast.47, bf16[4,48,768]{2,1,0:T(8,128)(2,1)} %bitcast.22.refs_3_), custom_call_target="tpu_custom_call" | custom-call | tf_op jit(solution)/shard_map/pallas_call | solution.py:551
  97.6 2.3 %collective-permute-done.30 = bf16[192,768]{1,0:T(8,128)(2,1)S(1)} collective-permute-done((bf16[192,768]{1,0:T(8,128)(2,1)}, bf16[192,768]{1,0:T(8,128)(2,1)S(1)}, u32[]{:S(2)}, u32[]{:S(2)}) %collective-permute-start.30) | collective-permute-done | bytes 294944 | tf_op jit(solution)/shard_map/ppermute | solution.py:50
  100.3 5.9 %collective-permute-done.31 = bf16[192,768]{1,0:T(8,128)(2,1)S(1)} collective-permute-done((bf16[192,768]{1,0:T(8,128)(2,1)}, bf16[192,768]{1,0:T(8,128)(2,1)S(1)}, u32[]{:S(2)}, u32[]{:S(2)}) %collective-permute-start.31) | collective-permute-done | bytes 294944 | tf_op jit(solution)/shard_map/ppermute | solution.py:50
  106.2 1.7 %collective-permute-start.28 = (bf16[48,768]{1,0:T(8,128)(2,1)}, bf16[48,768]{1,0:T(8,128)(2,1)S(1)}, u32[]{:S(2)}, u32[]{:S(2)}) collective-permute-start(bf16[48,768]{1,0:T(8,128)(2,1)} %get-tuple-element.66), channel_id=1, source_target_pairs={{0,4},{2,6},{4,0},{6,2},{1,5},{3,7},{5,1},{7,3},{8,12},{10,14},{12... | collective-permute-start | bytes 221192 | tf_op jit(solution)/shard_map/ppermute | solution.py:50
  107.9 1.2 collective-permute-start.29
  109.1 2.1 %shard_map.260 = (f32[48,768]{1,0:T(8,128)}, bf16[48,768]{1,0:T(8,128)(2,1)}, bf16[48,768]{1,0:T(8,128)(2,1)}, bf16[48,768]{1,0:T(8,128)(2,1)}) custom-call(f32[4,48,768]{2,1,0:T(8,128)} %bitcast.44, bf16[4,48,768]{2,1,0:T(8,128)(2,1)} %bitcast.48, bf16[4,48,768]{2,1,0:T(8,128)(2,1)} %bitcast.49, bf16[4,48,768]{2,1,0:T(8,128)(2,1)} %bitcast.27.refs_3_), custom_call_target="tpu_custom_call" | custom-call | tf_op jit(solution)/shard_map/pallas_call | solution.py:551
  111.9 2.7 %collective-permute-start.34 = (bf16[48,768]{1,0:T(8,128)(2,1)}, bf16[48,768]{1,0:T(8,128)(2,1)S(1)}, u32[]{:S(2)}, u32[]{:S(2)}) collective-permute-start(bf16[48,768]{1,0:T(8,128)(2,1)} %get-tuple-element.76), channel_id=1, source_target_pairs={{0,4},{2,6},{4,0},{6,2},{1,5},{3,7},{5,1},{7,3},{8,12},{10,14},{12... | collective-permute-start | bytes 221192 | tf_op jit(solution)/shard_map/ppermute | solution.py:50
  114.7 1.3 collective-permute-start.35
  116.6 7.4 %collective-permute-start.17 = (bf16[2,1,1,64,768]{4,3,2,1,0:T(8,128)(2,1)S(1)}, bf16[2,1,1,64,768]{4,3,2,1,0:T(8,128)(2,1)S(1)}, u32[]{:S(2)}, u32[]{:S(2)}) collective-permute-start(bf16[2,1,1,64,768]{4,3,2,1,0:T(8,128)(2,1)S(1)} %split.27), channel_id=1, source_target_pairs={{0,4},{2,6},{4,0},{6,2},{1,5},{3,7},{5,1},{7,3},{8,12},{10,14},{12... | collective-permute-start | bytes 589832 | tf_op jit(solution)/shard_map/ppermute | solution.py:50
  124.0 1.8 %shard_map.259 = (f32[48,1152]{1,0:T(8,128)}, f32[48,384]{1,0:T(8,128)}) custom-call(f32[48,768]{1,0:T(8,128)} %get-tuple-element.64.refs_0_, bf16[48,768]{1,0:T(8,128)(2,1)} %copy-done.10, bf16[48,768]{1,0:T(8,128)(2,1)} %copy-done.11, bf16[48,768]{1,0:T(8,128)(2,1)} %copy-done.13), custom_call_target="tpu_custom_call" | custom-call | tf_op jit(solution)/shard_map/pallas_call | solution.py:568
  126.6 1.9 %shard_map.261 = (f32[48,1536]{1,0:T(8,128)}, f32[48,1536]{1,0:T(8,128)}) custom-call(f32[48,768]{1,0:T(8,128)} %get-tuple-element.74.refs_0_, bf16[48,768]{1,0:T(8,128)(2,1)} %copy-done.12, bf16[48,768]{1,0:T(8,128)(2,1)} %copy-done.14, bf16[48,768]{1,0:T(8,128)(2,1)} %copy-done.15), custom_call_target="tpu_custom_call" | custom-call | tf_op jit(solution)/shard_map/pallas_call | solution.py:572
  128.6 3.7 %collective-permute-done.17 = bf16[2,1,1,64,768]{4,3,2,1,0:T(8,128)(2,1)S(1)} collective-permute-done((bf16[2,1,1,64,768]{4,3,2,1,0:T(8,128)(2,1)S(1)}, bf16[2,1,1,64,768]{4,3,2,1,0:T(8,128)(2,1)S(1)}, u32[]{:S(2)}, u32[]{:S(2)}) %collective-permute-start.17) | collective-permute-done | bytes 196640 | tf_op jit(solution)/shard_map/ppermute | solution.py:50
  136.2 0.8 pad_maximum_fusion.2
  (184 shorter events, 17.3 us)
Async XLA Ops:
  0.6 18.0 %copy-start.19 = (f32[1536]{0:T(1024)S(1)}, f32[1536]{0:T(1024)}, u32[]{:S(2)}) copy-start(f32[1536]{0:T(1024)} %param.26) | copy-start | bytes 18436
  0.7 22.8 %copy-start.22 = (f32[768]{0:T(1024)S(1)}, f32[768]{0:T(1024)}, u32[]{:S(2)}) copy-start(f32[768]{0:T(1024)} %param.17) | copy-start | bytes 9220
  0.7 22.8 %copy-start.23 = (f32[768]{0:T(1024)S(1)}, f32[768]{0:T(1024)}, u32[]{:S(2)}) copy-start(f32[768]{0:T(1024)} %param.18) | copy-start | bytes 9220
  0.7 22.8 %copy-start.24 = (f32[768]{0:T(1024)S(1)}, f32[768]{0:T(1024)}, u32[]{:S(2)}) copy-start(f32[768]{0:T(1024)} %param.23) | copy-start | bytes 9220
  0.7 22.8 %copy-start.25 = (f32[768]{0:T(1024)S(1)}, f32[768]{0:T(1024)}, u32[]{:S(2)}) copy-start(f32[768]{0:T(1024)} %param.24) | copy-start | bytes 9220
  2.4 34.8 %collective-permute-start.11 = (bf16[48,768]{1,0:T(8,128)(2,1)}, bf16[48,768]{1,0:T(8,128)(2,1)S(1)}, u32[]{:S(2)}, u32[]{:S(2)}) collective-permute-start(bf16[48,768]{1,0:T(8,128)(2,1)} %get-tuple-element.52), channel_id=1, source_target_pairs={{0,6},{2,4},{4,2},{6,0},{1,7},{3,5},{5,3},{7,1},{8,14},{10,12},{12... | collective-permute-start | bytes 221192 | tf_op jit(solution)/shard_map/ppermute | solution.py:50
  7.5 27.8 %collective-permute-start.9 = (bf16[48,768]{1,0:T(8,128)(2,1)}, bf16[48,768]{1,0:T(8,128)(2,1)S(1)}, u32[]{:S(2)}, u32[]{:S(2)}) collective-permute-start(bf16[48,768]{1,0:T(8,128)(2,1)} %get-tuple-element.52), channel_id=1, source_target_pairs={{0,2},{2,0},{4,6},{6,4},{1,3},{3,1},{5,7},{7,5},{8,10},{10,8},{12,... | collective-permute-start | bytes 221192 | tf_op jit(solution)/shard_map/ppermute | solution.py:50
  7.5 27.9 %collective-permute-start.10 = (bf16[48,768]{1,0:T(8,128)(2,1)}, bf16[48,768]{1,0:T(8,128)(2,1)S(1)}, u32[]{:S(2)}, u32[]{:S(2)}) collective-permute-start(bf16[48,768]{1,0:T(8,128)(2,1)} %get-tuple-element.51), channel_id=1, source_target_pairs={{0,4},{2,6},{4,0},{6,2},{1,5},{3,7},{5,1},{7,3},{8,12},{10,14},{12... | collective-permute-start | bytes 221192 | tf_op jit(solution)/shard_map/ppermute | solution.py:50
  10.2 12.5 %collective-permute-start = (bf16[2,1,1,64,768]{4,3,0,2,1:T(8,128)(2,1)S(1)}, bf16[2,1,1,64,768]{4,3,0,2,1:T(8,128)(2,1)S(1)}, u32[]{:S(2)}, u32[]{:S(2)}) collective-permute-start(bf16[2,1,1,64,768]{4,3,0,2,1:T(8,128)(2,1)S(1)} %maximum_bitcast_fusion), channel_id=1, source_target_pairs={{0,4},{2,6},{4,0},{6,2},{1,5},{3,7},{5,1},{7,3},{8,12},{10,14},{12... | collective-permute-start | bytes 589832 | tf_op jit(solution)/shard_map/ppermute | solution.py:50
  14.3 25.4 %collective-permute-start.3 = (bf16[48,768]{1,0:T(8,128)(2,1)}, bf16[48,768]{1,0:T(8,128)(2,1)S(1)}, u32[]{:S(2)}, u32[]{:S(2)}) collective-permute-start(bf16[48,768]{1,0:T(8,128)(2,1)} %get-tuple-element.48), channel_id=1, source_target_pairs={{0,2},{2,0},{4,6},{6,4},{1,3},{3,1},{5,7},{7,5},{8,10},{10,8},{12,... | collective-permute-start | bytes 221192 | tf_op jit(solution)/shard_map/ppermute | solution.py:50
  18.7 14.8 %copy-start.34 = (bf16[48,768]{1,0:T(8,128)(2,1)S(1)}, bf16[48,768]{1,0:T(8,128)(2,1)}, u32[]{:S(2)}) copy-start(bf16[48,768]{1,0:T(8,128)(2,1)} %get-tuple-element.49) | copy-start | bytes 221188
  22.7 10.7 %collective-permute-start.1 = (bf16[2,1,2,64,768]{4,3,0,2,1:T(8,128)(2,1)S(1)}, bf16[2,1,2,64,768]{4,3,0,2,1:T(8,128)(2,1)S(1)}, u32[]{:S(2)}, u32[]{:S(2)}) collective-permute-start(bf16[2,1,2,64,768]{4,3,0,2,1:T(8,128)(2,1)S(1)} %pad_maximum_fusion.1), channel_id=1, source_target_pairs={{0,2},{2,0},{4,6},{6,4},{1,3},{3,1},{5,7},{7,5},{8,10},{10,8},{12,... | collective-permute-start | bytes 1179656 | tf_op jit(solution)/shard_map/ppermute | solution.py:50
  33.5 6.8 %collective-permute-start.4 = (bf16[48,768]{1,0:T(8,128)(2,1)S(1)}, bf16[48,768]{1,0:T(8,128)(2,1)S(1)}, u32[]{:S(2)}, u32[]{:S(2)}) collective-permute-start(bf16[48,768]{1,0:T(8,128)(2,1)S(1)} %copy-done.34), channel_id=1, source_target_pairs={{0,4},{2,6},{4,0},{6,2},{1,5},{3,7},{5,1},{7,3},{8,12},{10,14},{12... | collective-permute-start | bytes 221192 | tf_op jit(solution)/shard_map/ppermute | solution.py:50
  35.3 21.4 %copy-start.3 = (bf16[2,1,4,64,768]{4,3,2,0,1:T(8,128)(2,1)}, bf16[2,1,4,64,768]{4,3,2,0,1:T(8,128)(2,1)S(1)}, u32[]{:S(2)}) copy-start(bf16[2,1,4,64,768]{4,3,2,0,1:T(8,128)(2,1)S(1)} %copy.44) | copy-start | bytes 2359300
  35.3 21.3 %collective-permute-start.2 = (bf16[2,1,256,768]{3,2,1,0:T(8,128)(2,1)S(1)}, bf16[2,1,256,768]{3,2,1,0:T(8,128)(2,1)}, u32[]{:S(2)}, u32[]{:S(2)}) collective-permute-start(bf16[2,1,256,768]{3,2,1,0:T(8,128)(2,1)S(1)} %bitcast.41), channel_id=1, source_target_pairs={{0,1},{1,0},{2,3},{3,2},{4,5},{5,4},{6,7},{7,6},{8,9},{9,8},{10,11... | collective-permute-start | bytes 2359304 | tf_op jit(solution)/shard_map/ppermute | solution.py:50
  35.4 6.6 %collective-permute-start.5 = (bf16[48,768]{1,0:T(8,128)(2,1)S(1)}, bf16[48,768]{1,0:T(8,128)(2,1)S(1)}, u32[]{:S(2)}, u32[]{:S(2)}) collective-permute-start(bf16[48,768]{1,0:T(8,128)(2,1)S(1)} %copy-done.33), channel_id=1, source_target_pairs={{0,6},{2,4},{4,2},{6,0},{1,7},{3,5},{5,3},{7,1},{8,14},{10,12},{12... | collective-permute-start | bytes 221192 | tf_op jit(solution)/shard_map/ppermute | solution.py:50
  37.2 19.4 %copy-start.17 = (bf16[192,768]{1,0:T(8,128)(2,1)}, bf16[192,768]{1,0:T(8,128)(2,1)S(1)}, u32[]{:S(2)}) copy-start(bf16[192,768]{1,0:T(8,128)(2,1)S(1)} %constant_dynamic-update-slice_fusion.4.refs_2_) | copy-start | bytes 884740
  37.2 10.9 %collective-permute-start.14 = (bf16[192,768]{1,0:T(8,128)(2,1)S(1)}, bf16[192,768]{1,0:T(8,128)(2,1)S(1)}, u32[]{:S(2)}, u32[]{:S(2)}) collective-permute-start(bf16[192,768]{1,0:T(8,128)(2,1)S(1)} %constant_dynamic-update-slice_fusion.4.refs_2_), channel_id=1, source_target_pairs={{0,24},{8,16},{16,8},{24,0},{1,25},{9,17},{17,9},{25,1},{2,26},{10... | collective-permute-start | bytes 884744 | tf_op jit(solution)/shard_map/ppermute | solution.py:50
  39.7 14.8 %collective-permute-start.13 = (bf16[192,768]{1,0:T(8,128)(2,1)S(1)}, bf16[192,768]{1,0:T(8,128)(2,1)S(1)}, u32[]{:S(2)}, u32[]{:S(2)}) collective-permute-start(bf16[192,768]{1,0:T(8,128)(2,1)S(1)} %constant_dynamic-update-slice_fusion.4.refs_2_), channel_id=1, source_target_pairs={{0,16},{8,24},{16,0},{24,8},{1,17},{9,25},{17,1},{25,9},{2,18},{10... | collective-permute-start | bytes 884744 | tf_op jit(solution)/shard_map/ppermute | solution.py:50
  40.3 16.4 %collective-permute-start.12 = (bf16[192,768]{1,0:T(8,128)(2,1)S(1)}, bf16[192,768]{1,0:T(8,128)(2,1)S(1)}, u32[]{:S(2)}, u32[]{:S(2)}) collective-permute-start(bf16[192,768]{1,0:T(8,128)(2,1)S(1)} %constant_dynamic-update-slice_fusion.4.refs_2_), channel_id=1, source_target_pairs={{0,8},{8,0},{16,24},{24,16},{1,9},{9,1},{17,25},{25,17},{2,10},{10... | collective-permute-start | bytes 884744 | tf_op jit(solution)/shard_map/ppermute | solution.py:50
  42.0 24.3 %copy-start.16 = (bf16[192,768]{1,0:T(8,128)(2,1)}, bf16[192,768]{1,0:T(8,128)(2,1)S(1)}, u32[]{:S(2)}) copy-start(bf16[192,768]{1,0:T(8,128)(2,1)S(1)} %constant_dynamic-update-slice_fusion.refs_2_) | copy-start | bytes 884740
  42.0 24.3 %collective-permute-start.8 = (bf16[192,768]{1,0:T(8,128)(2,1)S(1)}, bf16[192,768]{1,0:T(8,128)(2,1)S(1)}, u32[]{:S(2)}, u32[]{:S(2)}) collective-permute-start(bf16[192,768]{1,0:T(8,128)(2,1)S(1)} %constant_dynamic-update-slice_fusion.refs_2_), channel_id=1, source_target_pairs={{0,24},{8,16},{16,8},{24,0},{1,25},{9,17},{17,9},{25,1},{2,26},{10... | collective-permute-start | bytes 884744 | tf_op jit(solution)/shard_map/ppermute | solution.py:50
  48.1 18.2 %collective-permute-start.7 = (bf16[192,768]{1,0:T(8,128)(2,1)S(1)}, bf16[192,768]{1,0:T(8,128)(2,1)S(1)}, u32[]{:S(2)}, u32[]{:S(2)}) collective-permute-start(bf16[192,768]{1,0:T(8,128)(2,1)S(1)} %constant_dynamic-update-slice_fusion.refs_2_), channel_id=1, source_target_pairs={{0,16},{8,24},{16,0},{24,8},{1,17},{9,25},{17,1},{25,9},{2,18},{10... | collective-permute-start | bytes 884744 | tf_op jit(solution)/shard_map/ppermute | solution.py:50
  54.5 11.9 %collective-permute-start.6 = (bf16[192,768]{1,0:T(8,128)(2,1)S(1)}, bf16[192,768]{1,0:T(8,128)(2,1)S(1)}, u32[]{:S(2)}, u32[]{:S(2)}) collective-permute-start(bf16[192,768]{1,0:T(8,128)(2,1)S(1)} %constant_dynamic-update-slice_fusion.refs_2_), channel_id=1, source_target_pairs={{0,8},{8,0},{16,24},{24,16},{1,9},{9,1},{17,25},{25,17},{2,10},{10... | collective-permute-start | bytes 884744 | tf_op jit(solution)/shard_map/ppermute | solution.py:50
  74.7 3.7 %collective-permute-start.15 = (f32[520,768]{1,0:T(8,128)}, f32[520,768]{1,0:T(8,128)S(1)}, u32[]{:S(2)}, u32[]{:S(2)}) collective-permute-start(f32[520,768]{1,0:T(8,128)} %get-tuple-element.57), channel_id=1, source_target_pairs={{0,1},{1,0},{2,3},{3,2},{4,5},{5,4},{6,7},{7,6},{8,9},{9,8},{10,11... | collective-permute-start | bytes 4792328 | tf_op jit(solution)/shard_map/ppermute | solution.py:50
  75.0 12.6 %collective-permute-start.24 = (bf16[192,768]{1,0:T(8,128)(2,1)}, bf16[192,768]{1,0:T(8,128)(2,1)S(1)}, u32[]{:S(2)}, u32[]{:S(2)}) collective-permute-start(bf16[192,768]{1,0:T(8,128)(2,1)} %get-tuple-element.61), channel_id=1, source_target_pairs={{0,8},{8,0},{16,24},{24,16},{1,9},{9,1},{17,25},{25,17},{2,10},{10... | collective-permute-start | bytes 884744 | tf_op jit(solution)/shard_map/ppermute | solution.py:50
  75.9 12.1 %collective-permute-start.25 = (bf16[192,768]{1,0:T(8,128)(2,1)}, bf16[192,768]{1,0:T(8,128)(2,1)S(1)}, u32[]{:S(2)}, u32[]{:S(2)}) collective-permute-start(bf16[192,768]{1,0:T(8,128)(2,1)} %get-tuple-element.62), channel_id=1, source_target_pairs={{0,16},{8,24},{16,0},{24,8},{1,17},{9,25},{17,1},{25,9},{2,18},{10... | collective-permute-start | bytes 884744 | tf_op jit(solution)/shard_map/ppermute | solution.py:50
  81.7 4.1 %collective-permute-start.20 = (f32[6528]{0:T(1024)S(1)}, f32[6528]{0:T(1024)S(1)}, u32[]{:S(2)}, u32[]{:S(2)}) collective-permute-start(f32[6528]{0:T(1024)S(1)} %pad_maximum_fusion.4), channel_id=1, source_target_pairs={{0,8},{8,0},{16,24},{24,16},{1,9},{9,1},{17,25},{25,17},{2,10},{10... | collective-permute-start | bytes 78344 | tf_op jit(solution)/shard_map/ppermute | solution.py:50
  82.8 12.2 %collective-permute-start.26 = (bf16[192,768]{1,0:T(8,128)(2,1)}, bf16[192,768]{1,0:T(8,128)(2,1)}, u32[]{:S(2)}, u32[]{:S(2)}) collective-permute-start(bf16[192,768]{1,0:T(8,128)(2,1)} %get-tuple-element.63), channel_id=1, source_target_pairs={{0,24},{8,16},{16,8},{24,0},{1,25},{9,17},{17,9},{25,1},{2,26},{10... | collective-permute-start | bytes 884744 | tf_op jit(solution)/shard_map/ppermute | solution.py:50
  85.0 26.9 %collective-permute-start.16 = (bf16[2,1,2,64,768]{4,3,2,1,0:T(8,128)(2,1)S(1)}, bf16[2,1,2,64,768]{4,3,2,1,0:T(8,128)(2,1)S(1)}, u32[]{:S(2)}, u32[]{:S(2)}) collective-permute-start(bf16[2,1,2,64,768]{4,3,2,1,0:T(8,128)(2,1)S(1)} %split.26), channel_id=1, source_target_pairs={{0,2},{2,0},{4,6},{6,4},{1,3},{3,1},{5,7},{7,5},{8,10},{10,8},{12,... | collective-permute-start | bytes 1179656 | tf_op jit(solution)/shard_map/ppermute | solution.py:50
  85.8 7.7 %collective-permute-start.21 = (f32[6528]{0:T(1024)S(1)}, f32[6528]{0:T(1024)S(1)}, u32[]{:S(2)}, u32[]{:S(2)}) collective-permute-start(f32[6528]{0:T(1024)S(1)} %fusion.17), channel_id=1, source_target_pairs={{0,16},{8,24},{16,0},{24,8},{1,17},{9,25},{17,1},{25,9},{2,18},{10... | collective-permute-start | bytes 78344 | tf_op jit(solution)/shard_map/ppermute | solution.py:50
  87.7 12.2 %collective-permute-start.30 = (bf16[192,768]{1,0:T(8,128)(2,1)}, bf16[192,768]{1,0:T(8,128)(2,1)S(1)}, u32[]{:S(2)}, u32[]{:S(2)}) collective-permute-start(bf16[192,768]{1,0:T(8,128)(2,1)} %get-tuple-element.71), channel_id=1, source_target_pairs={{0,8},{8,0},{16,24},{24,16},{1,9},{9,1},{17,25},{25,17},{2,10},{10... | collective-permute-start | bytes 884744 | tf_op jit(solution)/shard_map/ppermute | solution.py:50
  87.9 18.3 %collective-permute-start.31 = (bf16[192,768]{1,0:T(8,128)(2,1)}, bf16[192,768]{1,0:T(8,128)(2,1)S(1)}, u32[]{:S(2)}, u32[]{:S(2)}) collective-permute-start(bf16[192,768]{1,0:T(8,128)(2,1)} %get-tuple-element.72), channel_id=1, source_target_pairs={{0,16},{8,24},{16,0},{24,8},{1,17},{9,25},{17,1},{25,9},{2,18},{10... | collective-permute-start | bytes 884744 | tf_op jit(solution)/shard_map/ppermute | solution.py:50
  93.5 14.5 %collective-permute-start.32 = (bf16[192,768]{1,0:T(8,128)(2,1)}, bf16[192,768]{1,0:T(8,128)(2,1)}, u32[]{:S(2)}, u32[]{:S(2)}) collective-permute-start(bf16[192,768]{1,0:T(8,128)(2,1)} %get-tuple-element.73), channel_id=1, source_target_pairs={{0,24},{8,16},{16,8},{24,0},{1,25},{9,17},{17,9},{25,1},{2,26},{10... | collective-permute-start | bytes 884744 | tf_op jit(solution)/shard_map/ppermute | solution.py:50
  95.0 16.3 %collective-permute-start.22 = (f32[6528]{0:T(1024)S(1)}, f32[6528]{0:T(1024)S(1)}, u32[]{:S(2)}, u32[]{:S(2)}) collective-permute-start(f32[6528]{0:T(1024)S(1)} %add.317), channel_id=1, source_target_pairs={{0,2},{2,0},{4,6},{6,4},{1,3},{3,1},{5,7},{7,5},{8,10},{10,8},{12,... | collective-permute-start | bytes 78344 | tf_op jit(solution)/shard_map/ppermute | solution.py:50
  99.9 14.8 %collective-permute-start.27 = (bf16[48,768]{1,0:T(8,128)(2,1)}, bf16[48,768]{1,0:T(8,128)(2,1)S(1)}, u32[]{:S(2)}, u32[]{:S(2)}) collective-permute-start(bf16[48,768]{1,0:T(8,128)(2,1)} %get-tuple-element.65), channel_id=1, source_target_pairs={{0,2},{2,0},{4,6},{6,4},{1,3},{3,1},{5,7},{7,5},{8,10},{10,8},{12,... | collective-permute-start | bytes 221192 | tf_op jit(solution)/shard_map/ppermute | solution.py:50
  106.2 9.8 %collective-permute-start.28 = (bf16[48,768]{1,0:T(8,128)(2,1)}, bf16[48,768]{1,0:T(8,128)(2,1)S(1)}, u32[]{:S(2)}, u32[]{:S(2)}) collective-permute-start(bf16[48,768]{1,0:T(8,128)(2,1)} %get-tuple-element.66), channel_id=1, source_target_pairs={{0,4},{2,6},{4,0},{6,2},{1,5},{3,7},{5,1},{7,3},{8,12},{10,14},{12... | collective-permute-start | bytes 221192 | tf_op jit(solution)/shard_map/ppermute | solution.py:50
  107.9 8.7 %collective-permute-start.29 = (bf16[48,768]{1,0:T(8,128)(2,1)}, bf16[48,768]{1,0:T(8,128)(2,1)S(1)}, u32[]{:S(2)}, u32[]{:S(2)}) collective-permute-start(bf16[48,768]{1,0:T(8,128)(2,1)} %get-tuple-element.67), channel_id=1, source_target_pairs={{0,6},{2,4},{4,2},{6,0},{1,7},{3,5},{5,3},{7,1},{8,14},{10,12},{12... | collective-permute-start | bytes 221192 | tf_op jit(solution)/shard_map/ppermute | solution.py:50
  109.1 14.8 %copy-start.20 = (f32[768]{0:T(1024)S(1)}, f32[768]{0:T(1024)}, u32[]{:S(2)}) copy-start(f32[768]{0:T(1024)} %param.22) | copy-start | bytes 9220
  109.1 14.8 %copy-start.21 = (f32[768]{0:T(1024)S(1)}, f32[768]{0:T(1024)}, u32[]{:S(2)}) copy-start(f32[768]{0:T(1024)} %param.28) | copy-start | bytes 9220
  111.3 14.6 %collective-permute-start.33 = (bf16[48,768]{1,0:T(8,128)(2,1)}, bf16[48,768]{1,0:T(8,128)(2,1)S(1)}, u32[]{:S(2)}, u32[]{:S(2)}) collective-permute-start(bf16[48,768]{1,0:T(8,128)(2,1)} %get-tuple-element.75), channel_id=1, source_target_pairs={{0,2},{2,0},{4,6},{6,4},{1,3},{3,1},{5,7},{7,5},{8,10},{10,8},{12,... | collective-permute-start | bytes 221192 | tf_op jit(solution)/shard_map/ppermute | solution.py:50
  111.9 14.0 %collective-permute-start.34 = (bf16[48,768]{1,0:T(8,128)(2,1)}, bf16[48,768]{1,0:T(8,128)(2,1)S(1)}, u32[]{:S(2)}, u32[]{:S(2)}) collective-permute-start(bf16[48,768]{1,0:T(8,128)(2,1)} %get-tuple-element.76), channel_id=1, source_target_pairs={{0,4},{2,6},{4,0},{6,2},{1,5},{3,7},{5,1},{7,3},{8,12},{10,14},{12... | collective-permute-start | bytes 221192 | tf_op jit(solution)/shard_map/ppermute | solution.py:50
  114.7 17.9 %copy-start.1 = (f32[2,64,768]{2,1,0:T(8,128)S(1)}, f32[2,64,768]{2,1,0:T(8,128)}, u32[]{:S(2)}) copy-start(f32[2,64,768]{2,1,0:T(8,128)} %param.29) | copy-start | bytes 1179652
  114.7 11.2 %collective-permute-start.35 = (bf16[48,768]{1,0:T(8,128)(2,1)S(1)}, bf16[48,768]{1,0:T(8,128)(2,1)S(1)}, u32[]{:S(2)}, u32[]{:S(2)}) collective-permute-start(bf16[48,768]{1,0:T(8,128)(2,1)S(1)} %copy-done.35), channel_id=1, source_target_pairs={{0,6},{2,4},{4,2},{6,0},{1,7},{3,5},{5,3},{7,1},{8,14},{10,12},{12... | collective-permute-start | bytes 221192 | tf_op jit(solution)/shard_map/ppermute | solution.py:50
  116.0 12.5 %collective-permute-start.23 = (f32[6528]{0:T(1024)S(1)}, f32[6528]{0:T(1024)S(1)}, u32[]{:S(2)}, u32[]{:S(2)}) collective-permute-start(f32[6528]{0:T(1024)S(1)} %add.318), channel_id=1, source_target_pairs={{0,4},{2,6},{4,0},{6,2},{1,5},{3,7},{5,1},{7,3},{8,12},{10,14},{12... | collective-permute-start | bytes 78344 | tf_op jit(solution)/shard_map/ppermute | solution.py:50
  116.6 15.6 %collective-permute-start.17 = (bf16[2,1,1,64,768]{4,3,2,1,0:T(8,128)(2,1)S(1)}, bf16[2,1,1,64,768]{4,3,2,1,0:T(8,128)(2,1)S(1)}, u32[]{:S(2)}, u32[]{:S(2)}) collective-permute-start(bf16[2,1,1,64,768]{4,3,2,1,0:T(8,128)(2,1)S(1)} %split.27), channel_id=1, source_target_pairs={{0,4},{2,6},{4,0},{6,2},{1,5},{3,7},{5,1},{7,3},{8,12},{10,14},{12... | collective-permute-start | bytes 589832 | tf_op jit(solution)/shard_map/ppermute | solution.py:50
  132.7 2.4 %collective-permute-start.18 = (bf16[1,64,768]{2,1,0:T(8,128)(2,1)S(1)}, bf16[1,64,768]{2,1,0:T(8,128)(2,1)S(1)}, u32[]{:S(2)}, u32[]{:S(2)}) collective-permute-start(bf16[1,64,768]{2,1,0:T(8,128)(2,1)S(1)} %get-tuple-element.87), channel_id=1, source_target_pairs={{0,1},{1,0},{2,3},{3,2},{4,5},{5,4},{6,7},{7,6},{8,9},{9,8},{10,11... | collective-permute-start | bytes 294920 | tf_op jit(solution)/shard_map/ppermute | solution.py:50
  134.6 1.6 %collective-permute-start.19 = (f32[1,64,768]{2,1,0:T(8,128)S(1)}, f32[1,64,768]{2,1,0:T(8,128)S(1)}, u32[]{:S(2)}, u32[]{:S(2)}) collective-permute-start(f32[1,64,768]{2,1,0:T(8,128)S(1)} %get-tuple-element.86), channel_id=1, source_target_pairs={{0,1},{1,0},{2,3},{3,2},{4,5},{5,4},{6,7},{7,6},{8,9},{9,8},{10,11... | collective-permute-start | bytes 589832 | tf_op jit(solution)/shard_map/ppermute | solution.py:50
  (24 other events, 111.0 us)

commit v2 on v1

--- a/solution.py
+++ b/solution.py
@@ -20,13 +20,6 @@
 INV_ROOT_TWO_PI = 0.3989422804014327
 CONTRACT_LAST = (((1,), (1,)), ((), ()))
 CONTRACT_FIRST = (((0,), (0,)), ((), ()))
-
-
-def angle_tables(position):
-    half = ROT // 2
-    frequency = 1.0 / 10000.0 ** (jnp.arange(half, dtype=jnp.float32) * (2.0 / ROT))
-    phase = position.astype(jnp.float32)[:, None] * frequency[None, :]
-    return (jnp.cos(phase), jnp.sin(phase))
 
 
 def positions(order, start, count):
@@ -86,20 +79,6 @@
     return value
 
 
-def butterfly(value, axis):
-    bit = 1
-    while bit < lax.axis_size(axis):
-        other = swap(value, axis, bit)
-        value = value + other
-        bit *= 2
-    return value
-
-
-def one_hot_slots(value, index, count):
-    slots = jnp.arange(count, dtype=jnp.int32)[:, None] == index
-    return jnp.where(slots, value[None, :], 0.0).reshape(-1)
-
-
 def dot(left, right):
     return jnp.dot(left, right, preferred_element_type=jnp.float32)
 
@@ -141,12 +120,34 @@
 
 
 def rotary_tables(position):
-    cosine, sine = angle_tables(position)
-    rest = jnp.ones((position.shape[0], HD - ROT), jnp.float32)
-    none = jnp.zeros((position.shape[0], HD - ROT), jnp.float32)
-    cos_head = jnp.concatenate([cosine, cosine, rest], axis=1)
-    sin_head = jnp.concatenate([-sine, sine, none], axis=1)
-    return jnp.concatenate([cos_head] * 2, axis=1), jnp.concatenate([sin_head] * 2, axis=1)
+    lane = jnp.arange(LANES, dtype=jnp.int32) % HD
+    half = ROT // 2
+    frequency = 1.0 / 10000.0 ** ((lane % half).astype(jnp.float32) * (2.0 / ROT))
+    phase = position * jnp.where(lane < ROT, frequency, 0.0)[None, :]
+    return jnp.cos(phase), jnp.where(lane < half, -1.0, 1.0)[None, :] * jnp.sin(phase)
+
+
+def tiled(vector):
+    return vector.reshape(-1, LANES)
+
+
+def row_of(ref):
+    return jnp.concatenate([ref[i : i + 1, :] for i in range(ref.shape[0])], axis=1)
+
+
+def put_row(ref, value):
+    for i in range(ref.shape[0]):
+        ref[i : i + 1, :] = value[:, i * LANES : (i + 1) * LANES]
+
+
+def tree_sum(parts):
+    while len(parts) > 1:
+        parts = [parts[i] + parts[i + 1] for i in range(0, len(parts), 2)]
+    return parts[0]
+
+
+def folded(value, columns):
+    return [value[:, i : i + columns] for i in range(0, value.shape[1], columns)]
 
 
 def early_message_kernel(groups, qkv_cols, features, qkv_ref, dense_ref, *outs):
@@ -193,12 +194,16 @@
             ]
 
 
-def send_blocks(total, outs):
+def send_blocks(total, outs, block, extra=()):
     at = lax.axis_index("fsdp")
-    block = outs[0].shape[0]
     for k, out in enumerate(outs):
         start = pl.multiple_of((at ^ k) * block, SUBLANES)
-        out[...] = total[pl.ds(start, block), :].astype(out.dtype)
+        out[:block, :] = total[pl.ds(start, block), :].astype(out.dtype)
+        for i, row in enumerate(extra):
+            out[block + i : block + i + 1, :] = row.astype(out.dtype)
+        rest = out.shape[0] - block - len(extra)
+        if rest:
+            out[block + len(extra) :, :] = jnp.zeros((rest, out.shape[1]), out.dtype)
 
 
 def attention_kernel(
@@ -214,17 +219,19 @@
 ):
     row_refs = refs[:core_count]
     parts = refs[core_count : core_count + fsdp_count]
-    (norms, bias, cos_ref, sin_ref, pos_col, pos_row) = refs[
-        core_count + fsdp_count : core_count + fsdp_count + 6
+    (gain_ref, shift_ref, bias_ref, cos_ref, sin_ref, pos_col, pos_row) = refs[
+        core_count + fsdp_count : core_count + fsdp_count + 7
     ]
-    gain, shift = norms[0:1, :], norms[1:2, :]
-    outs = refs[core_count + fsdp_count + 6 :]
+    gain, shift = row_of(gain_ref), row_of(shift_ref)
+    outs = refs[core_count + fsdp_count + 7 :]
     branch, norm_out, sums, bias_out = outs[:4]
     grad_outs = outs[4 : 4 + fsdp_count]
     weight, grads, mixed, total = outs[4 + fsdp_count :]
     cols = weight.shape[1]
     features = own_heads * HD
     qkv_cols = 3 * features
+    low_cols = qkv_cols // LANES * LANES
+    high_cols = -(-qkv_cols // LANES) * LANES
     scale = 1.0 / math.sqrt(HD)
     ctx_at = lax.axis_index("ctx")
     seq_at = lax.rem(lax.div(ctx_at, head_groups), seqs)
@@ -237,21 +244,26 @@
         seq_grads = jnp.where(core == j, row_refs[j][1, inner], seq_grads)
     centred, _ = normed_rows(seq_tokens.astype(jnp.float32))
     attn_in = (centred * gain + shift).astype(jnp.bfloat16)
-    lane = lax.broadcasted_iota(jnp.int32, (1, cols), 1)
+    bias_all = row_of(bias_ref)
+    biases = [bias_all[:, g * qkv_cols : (g + 1) * qkv_cols] for g in range(head_groups)]
+    bias = swapped(biases, lax.rem(ctx_at, head_groups))[0]
+    if high_cols > qkv_cols:
+        bias = jnp.concatenate([bias, jnp.zeros((1, high_cols - qkv_cols), jnp.float32)], axis=1)
+    lane = lax.broadcasted_iota(jnp.int32, (1, high_cols), 1)
     rotated = (lane < qkv_cols) & (lane % (3 * HD) < 2 * HD)
     first = lane % HD < ROT // 2
-    repeat = cols // LANES
+    repeat = high_cols // LANES
     cos_all = jnp.where(rotated, jnp.concatenate([cos_ref[...]] * repeat, axis=1), 1.0)
     sin_all = jnp.where(rotated, jnp.concatenate([sin_ref[...]] * repeat, axis=1), 0.0)
 
     def turn(values, sine):
-        ahead = pltpu.roll(values, cols - ROT // 2, 1)
+        ahead = pltpu.roll(values, high_cols - ROT // 2, 1)
         behind = pltpu.roll(values, ROT // 2, 1)
         return values * cos_all + jnp.where(first, ahead, behind) * sine
 
-    projected = dot(attn_in, weight[...]) + bias[...]
+    projected = dot(attn_in, weight[:, :high_cols]) + bias
     turned = turn(projected, sin_all).astype(jnp.bfloat16)
-    ctx_low = dot(seq_grads, weight[:, qkv_cols:]).astype(jnp.bfloat16)
+    ctx_low = dot(seq_grads, weight[:, low_cols:]).astype(jnp.bfloat16)
     allowed = pos_row[...] <= pos_col[...]
     keep = None
     if copies > 1:
@@ -263,7 +275,8 @@
         query = turned[:, at : at + HD]
         key = turned[:, at + HD : at + 2 * HD]
         value = turned[:, at + 2 * HD : at + 3 * HD]
-        low = ctx_low[:, head * HD : (head + 1) * HD]
+        spot = qkv_cols - low_cols + head * HD
+        low = ctx_low[:, spot : spot + HD]
         scores = jnp.where(allowed, dot_last(query, key) * scale, NEGATIVE)
         peak = jnp.max(scores, axis=-1, keepdims=True)
         weights = jnp.where(allowed, jnp.exp(scores - peak), 0.0)
@@ -280,13 +293,16 @@
         grads[:, at : at + HD] = dot(score_low, key) * scale
         grads[:, at + HD : at + 2 * HD] = dot_first(score_low, query) * scale
         grads[:, at + 2 * HD : at + 3 * HD] = dot_first(probs_low, low)
-        mixed[:, qkv_cols + head * HD : qkv_cols + (head + 1) * HD] = attended.astype(jnp.bfloat16)
+        mixed[:, spot : spot + HD] = attended.astype(jnp.bfloat16)
     proj_grad = turn(grads[...], -sin_all)
     proj_low = proj_grad.astype(jnp.bfloat16)
-    total[...] = dot_first(attn_in, proj_low) + dot_first(seq_grads, mixed[...])
-    send_blocks(total, grad_outs)
-    branch[...] = dot_last(mixed[...], weight[...])
-    norm_grad = dot_last(proj_low, weight[...])
+    total[:, :high_cols] = dot_first(attn_in, proj_low)
+    if cols > high_cols:
+        total[:, high_cols:] = jnp.zeros((weight.shape[0], cols - high_cols), jnp.float32)
+    total[:, low_cols:] += dot_first(seq_grads, mixed[...])
+    send_blocks(total, grad_outs, grad_outs[0].shape[0])
+    branch[...] = dot_last(mixed[...], weight[:, low_cols:])
+    norm_grad = dot_last(proj_low, weight[:, :high_cols])
     norm_out[...] = norm_grad * gain
     sums[...] = jnp.concatenate(
         [
@@ -295,76 +311,95 @@
         ],
         axis=0,
     )
-    bias_out[...] = jnp.sum(proj_grad, axis=0, keepdims=True)
-
-
-def mlp_kernel(fsdp_count, core_count, near, head_groups, seqs, padded, row_blocks, *refs):
+    bias_out[:, :high_cols] = jnp.sum(proj_grad, axis=0, keepdims=True)
+    if cols > high_cols:
+        bias_out[:, high_cols:] = jnp.zeros((1, cols - high_cols), jnp.float32)
+
+
+def mlp_kernel(fsdp_count, core_count, near, head_groups, seqs, ff, row_blocks, *refs):
     row_refs = refs[:core_count]
     parts = refs[core_count : core_count + fsdp_count]
-    norm_ref, bias, attn_branch, attn_norm, attn_sums = refs[
-        core_count + fsdp_count : core_count + fsdp_count + 5
-    ]
-    gain, shift = norm_ref[2:3, :], norm_ref[3:4, :]
-    outs = refs[core_count + fsdp_count + 5 :]
-    both, bias_out = outs[:core_count], outs[core_count]
-    grad_outs = outs[core_count + 1 : core_count + 1 + fsdp_count]
-    weight, total = outs[core_count + 1 + fsdp_count :]
-    size = attn_branch.shape[0]
-    seq_at = lax.rem(lax.div(lax.axis_index("ctx"), head_groups), seqs)
+    (
+        gain_ref,
+        shift_ref,
+        bias_ref,
+        columns_ref,
+        attn_branch,
+        attn_norm,
+        attn_sums,
+        attn_bias,
+    ) = refs[core_count + fsdp_count : core_count + fsdp_count + 8]
+    outs = refs[core_count + fsdp_count + 8 :]
+    both = outs[:core_count]
+    grad_outs = outs[core_count : core_count + fsdp_count]
+    weight, total = outs[core_count + fsdp_count :]
+    gain, shift = row_of(gain_ref), row_of(shift_ref)
+    size, width = attn_branch.shape
+    both_cols = weight.shape[1]
+    padded = both_cols // 2
+    ctx_at = lax.axis_index("ctx")
+    bias_all = row_of(bias_ref)
+    count = bias_all.shape[1] // ff
+    bias = swapped([bias_all[:, r * ff : (r + 1) * ff] for r in range(count)], ctx_at)[0]
+    if padded > ff:
+        bias = jnp.concatenate([bias, jnp.zeros((1, padded - ff), jnp.float32)], axis=1)
+    seq_at = lax.rem(lax.div(ctx_at, head_groups), seqs)
     core = lax.div(seq_at, near) ^ lax.axis_index("tp")
     inner = lax.rem(seq_at, near)
     place_weight(parts, weight, row_blocks)
     up, down = weight[:, :padded], weight[:, padded:]
-    gain_sum = shift_sum = bias_sum = 0.0
+    rows = jnp.concatenate([ref[0].reshape(near * size, width) for ref in row_refs], axis=0)
+    grad_rows = jnp.concatenate([ref[1].reshape(near * size, width) for ref in row_refs], axis=0)
+    centred, _ = normed_rows(rows.astype(jnp.float32))
+    mlp_in = (centred * gain + shift).astype(jnp.bfloat16)
+    pre_act = dot(mlp_in, up) + bias
+    normal = 0.5 * (1.0 + lax.erf(pre_act * ROOT_HALF))
+    hidden = (pre_act * normal).astype(jnp.bfloat16)
+    slope = normal + pre_act * jnp.exp(-0.5 * pre_act * pre_act) * INV_ROOT_TWO_PI
+    pre_grad = dot(grad_rows, down) * slope
+    pre_low = pre_grad.astype(jnp.bfloat16)
+    total[:, :padded] = dot_first(mlp_in, pre_low)
+    total[:, padded:] = dot_first(grad_rows, hidden)
+    norm_grad = dot_last(pre_low, up)
+    bias_sum = jnp.concatenate(
+        [jnp.sum(pre_grad, axis=0, keepdims=True), jnp.zeros((1, padded), jnp.float32)], axis=1
+    )
+    vectors = [
+        attn_sums[0:1, :],
+        attn_sums[1:2, :],
+        jnp.sum(norm_grad * centred, axis=0, keepdims=True),
+        jnp.sum(norm_grad, axis=0, keepdims=True),
+        row_of(columns_ref),
+        attn_bias[...],
+    ]
+    extra = [piece for vector in vectors for piece in folded(vector, both_cols)] + [bias_sum]
+    send_blocks(total, grad_outs, width // fsdp_count, extra)
+    norm_grad = norm_grad * gain
+    branch = dot_last(hidden, down)
     for j in range(core_count):
-        width = weight.shape[0]
-        rows = row_refs[j][0].reshape(near * size, width)
-        grad_rows = row_refs[j][1].reshape(near * size, width)
-        centred, _ = normed_rows(rows.astype(jnp.float32))
-        mlp_in = (centred * gain + shift).astype(jnp.bfloat16)
-        pre_act = dot(mlp_in, up) + bias[...]
-        normal = 0.5 * (1.0 + lax.erf(pre_act * ROOT_HALF))
-        hidden = (pre_act * normal).astype(jnp.bfloat16)
-        slope = normal + pre_act * jnp.exp(-0.5 * pre_act * pre_act) * INV_ROOT_TWO_PI
-        pre_grad = dot(grad_rows, down) * slope
-        pre_low = pre_grad.astype(jnp.bfloat16)
-        up_part, down_part = dot_first(mlp_in, pre_low), dot_first(grad_rows, hidden)
-        if j:
-            total[:, :padded] += up_part
-            total[:, padded:] += down_part
-        else:
-            total[:, :padded] = up_part
-            total[:, padded:] = down_part
-        norm_grad = dot_last(pre_low, up)
-        gain_sum = gain_sum + jnp.sum(norm_grad * centred, axis=0, keepdims=True)
-        shift_sum = shift_sum + jnp.sum(norm_grad, axis=0, keepdims=True)
-        bias_sum = bias_sum + jnp.sum(pre_grad, axis=0, keepdims=True)
-        norm_grad = norm_grad * gain
-        branch = dot_last(hidden, down)
         for i in range(near):
             here = (core == j) & (inner == i)
-            span = slice(i * size, (i + 1) * size)
-            both[j][span, :] = branch[span] + jnp.where(here, attn_branch[...], 0.0)
-            span_norm = slice((near + i) * size, (near + i + 1) * size)
-            both[j][span_norm, :] = norm_grad[span] + jnp.where(here, attn_norm[...], 0.0)
-    send_blocks(total, grad_outs)
-    for j in range(core_count):
-        both[j][2 * near * size : 2 * near * size + 2, :] = attn_sums[...]
-        both[j][2 * near * size + 2 : 2 * near * size + 3, :] = gain_sum
-        both[j][2 * near * size + 3 : 2 * near * size + 4, :] = shift_sum
-        both[j][2 * near * size + 4 :, :] = jnp.zeros((4, width), jnp.float32)
-    bias_out[...] = bias_sum
-
-
-def sum_blocks_kernel(fsdp_count, *refs):
+            at = (j * near + i) * size
+            out = both[j]
+            out[0, i] = branch[at : at + size] + jnp.where(here, attn_branch[...], 0.0)
+            out[1, i] = norm_grad[at : at + size] + jnp.where(here, attn_norm[...], 0.0)
+
+
+def sum_blocks_kernel(fsdp_count, ctx_count, rows_here, *refs):
     parts, outs = refs[:fsdp_count], refs[fsdp_count:]
-    at = lax.axis_index("ctx")
-    for k, out in enumerate(outs):
-        rank = at ^ k
-        block = parts[0][rank]
-        for part in parts[1:]:
-            block = block + part[rank].astype(jnp.float32)
-        out[...] = block.astype(out.dtype)
+    block = ctx_count * rows_here
+    total = parts[0][:block, :]
+    for part in parts[1:]:
+        total = total + part[:block, :].astype(jnp.float32)
+    pieces = [total[r * rows_here : (r + 1) * rows_here] for r in range(ctx_count)]
+    for out, piece in zip(outs, swapped(pieces, lax.axis_index("ctx"))):
+        out[:rows_here, :] = piece.astype(out.dtype)
+    if outs[0].shape[0] > rows_here:
+        vectors = tree_sum(
+            [part[block:, :].astype(jnp.bfloat16).astype(jnp.float32) for part in parts]
+        ).astype(jnp.bfloat16)
+        for out in outs:
+            out[rows_here:, :] = vectors.astype(out.dtype)
 
 
 def early_end_kernel(count, groups, qkv_cols, features, *refs):
@@ -372,21 +407,41 @@
     at = lax.rem(lax.axis_index("ctx"), groups)
     sums = []
     for g in range(groups):
-        block = parts[g][...].astype(jnp.float32)
-        for part in parts[g + groups :: groups]:
-            block = block + part[...].astype(jnp.float32)
-        sums.append(block)
+        sums.append(tree_sum([part[...].astype(jnp.float32) for part in parts[g::groups]]))
     for g, block in enumerate(swapped(sums, at)):
         qkv_out[:, g * qkv_cols : (g + 1) * qkv_cols] = block[:, :qkv_cols]
         dense_out[:, g * features : (g + 1) * features] = block[:, qkv_cols:]
 
 
-def late_end_kernel(count, ff, padded, *refs):
-    parts, (up_out, down_out) = refs[:count], refs[count:]
-    blocks = [part[...].astype(jnp.float32) for part in parts]
-    for r, block in enumerate(swapped(blocks, lax.axis_index("ctx"))):
+def late_end_kernel(count, groups, ff, padded, qkv_cols, cols, *refs):
+    parts, outs = refs[:count], refs[count:]
+    up_out, down_out, gains_out, columns_out, qkv_bias_out, up_bias_out = outs
+    rows, width = up_out.shape[0], LANES * columns_out.shape[0]
+    both_cols = 2 * padded
+    ctx_at = lax.axis_index("ctx")
+    blocks = [part[:rows, :].astype(jnp.float32) for part in parts]
+    for r, block in enumerate(swapped(blocks, ctx_at)):
         up_out[:, r * ff : (r + 1) * ff] = block[:, :ff]
         down_out[:, r * ff : (r + 1) * ff] = block[:, padded : padded + ff]
+    vectors = [part[rows:, :].astype(jnp.float32) for part in parts]
+
+    def unfolded(block, start, extent):
+        n = extent // both_cols
+        return jnp.concatenate([block[start + i : start + i + 1] for i in range(n)], axis=1)
+
+    summed = tree_sum(vectors)
+    step = width // both_cols
+    gains = jnp.concatenate([unfolded(summed, i * step, width) for i in range(4)], axis=1)
+    put_row(gains_out, gains)
+    put_row(columns_out, unfolded(summed, 4 * step, width))
+    sums = [tree_sum(vectors[g::groups]) for g in range(groups)]
+    sums = [unfolded(block, 5 * step, cols)[:, :qkv_cols] for block in sums]
+    put_row(
+        qkv_bias_out, jnp.concatenate(swapped(sums, lax.rem(ctx_at, groups)), axis=1)
+    )
+    last = 5 * step + cols // both_cols
+    ups = [block[last : last + 1, :ff] for block in vectors]
+    put_row(up_bias_out, jnp.concatenate(swapped(ups, ctx_at), axis=1))
 
 
 def on_device(
@@ -420,12 +475,12 @@
     features = own_heads * HD
     qkv_cols = 3 * features
     cols = qkv_cols + features
+    low_cols = qkv_cols // LANES * LANES
+    high_cols = -(-qkv_cols // LANES) * LANES
     ff = hidden_all // ctx_count
     padded = -(-ff // LANES) * LANES
-    head_at = ctx_at % head_groups
     near = seqs // tp_count
     size = ctx_count * length
-    near_rows = near * size
 
     early = local_kernel(
         functools.partial(early_message_kernel, head_groups, qkv_cols, features),
@@ -462,24 +517,17 @@
             positions(group_order, (ctx_at ^ k) * length, length)
             for k in gather_order(ctx_count)
         ]
-    )
-    cos_table, sin_table = rotary_tables(position)
-    place = position.astype(f32)
-    norms = jnp.stack([attn_gain, attn_shift, mlp_gain, mlp_shift])
+    ).astype(f32)
+    cos_table, sin_table = rotary_tables(position[:, None])
     column_sums = jnp.sum(out_grad, axis=(0, 1))
 
-    def row(vector):
-        return vector.reshape(1, -1)
-
-    qkv_parts = [qkv_bias[g * qkv_cols : (g + 1) * qkv_cols] for g in range(head_groups)]
-    qkv_own = jnp.pad(swapped(qkv_parts, head_at)[0], (0, features))
-    up_parts = [up_bias[r * ff : (r + 1) * ff] for r in range(ctx_count)]
-    up_own = jnp.pad(swapped(up_parts, ctx_at)[0], (0, padded - ff))
-
-    def grad_blocks(columns):
+    def grad_blocks(columns, extra=0):
         return [
-            shaped((block_rows, columns), bf16 if k else f32) for k in range(fsdp_count)
+            shaped((block_rows + extra, columns), bf16 if k else f32) for k in range(fsdp_count)
         ]
+
+    vector_rows = (5 * width + cols) // (2 * padded) + 1
+    vector_rows = -(-vector_rows // SUBLANES) * SUBLANES
 
     row_blocks = ctx_count if loose else 1
     attn_branch, attn_norm, attn_sums, qkv_bias_part, *early_grads = local_kernel(
@@ -499,8 +547,8 @@
         + grad_blocks(cols),
         [
             pltpu.VMEM((width, cols), bf16),
-            pltpu.VMEM((size, cols), f32),
-            pltpu.VMEM((size, cols), bf16),
+            pltpu.VMEM((size, high_cols), f32),
+            pltpu.VMEM((size, cols - low_cols), bf16),
             pltpu.VMEM((width, cols), f32),
         ],
         flops=16 * size * width * cols,
@@ -508,50 +556,51 @@
     )(
         *by_core,
         *early_parts,
-        norms,
-        row(qkv_own),
+        tiled(attn_gain),
+        tiled(attn_shift),
+        tiled(qkv_bias),
         cos_table,
         sin_table,
-        place.reshape(-1, 1),
-        row(place),
+        position.reshape(-1, 1),
+        position.reshape(1, -1),
     )
     outs = local_kernel(
         functools.partial(
-            mlp_kernel, fsdp_count, tp_count, near, head_groups, seqs, padded, row_blocks
+            mlp_kernel, fsdp_count, tp_count, near, head_groups, seqs, ff, row_blocks
         ),
-        [shaped((2 * near_rows + 8, width), f32)] * tp_count
-        + [shaped((1, padded), f32)]
-        + grad_blocks(2 * padded),
+        [shaped((2, near, size, width), f32)] * tp_count + grad_blocks(2 * padded, vector_rows),
         [pltpu.VMEM((width, 2 * padded), bf16), pltpu.VMEM((width, 2 * padded), f32)],
         flops=12 * seqs * size * width * padded,
         moved=32 * size * width,
     )(
         *by_core,
         *late_parts,
-        norms,
-        row(up_own),
+        tiled(mlp_gain),
+        tiled(mlp_shift),
+        tiled(up_bias),
+        tiled(column_sums),
         attn_branch,
         attn_norm,
         attn_sums,
-    )
-    row_parts, up_bias_part = outs[:tp_count], outs[tp_count]
-    late_grads = outs[tp_count + 1 :]
+        qkv_bias_part,
+    )
+    row_parts, late_grads = outs[:tp_count], outs[tp_count:]
     row_sums = sum(exchange(row_parts, "tp"))
-    gain_parts = row_sums[2 * near_rows : 2 * near_rows + 4].reshape(-1)
-    row_sums = row_sums[: 2 * near_rows].reshape(2, near, ctx_count, length, width)
+    row_sums = row_sums.reshape(2, near, ctx_count, length, width)
     row_sums = scatter_chunks(row_sums, "ctx", 2).reshape(2, near, length, width)
     branches, inner = row_sums[0], row_sums[1]
 
     def both_cores(half):
-        return jnp.concatenate(swapped(spread(half, "tp"), tp_at), axis=0)
+        halves = spread(half, "tp")
+        return jnp.concatenate(swapped(halves, tp_at), axis=0)
 
     def scatter_weights(parts):
         columns = parts[0].shape[1]
-        received = [part.reshape(ctx_count, rows_here, columns) for part in exchange(parts, "fsdp")]
+        rows = parts[0].shape[0] - block_rows + rows_here
         pieces = local_kernel(
-            functools.partial(sum_blocks_kernel, fsdp_count),
-            [shaped((rows_here, columns), bf16 if k else f32) for k in range(ctx_count)],
-        )(*received)
+            functools.partial(sum_blocks_kernel, fsdp_count, ctx_count, rows_here),
+            [shaped((rows, columns), bf16 if k else f32) for k in range(ctx_count)],
+        )(*exchange(parts, "fsdp"))
         return exchange(pieces, "ctx")
 
     early_pieces = scatter_weights(early_grads)
@@ -569,40 +618,38 @@
         functools.partial(early_end_kernel, ctx_count, head_groups, qkv_cols, features),
         [shaped(qkv_weight.shape, f32), shaped(dense_weight.shape[::-1], f32)],
     )(*early_pieces)
-    up_weight_grad, down_weight_grad = local_kernel(
-        functools.partial(late_end_kernel, ctx_count, ff, padded),
-        [shaped(up_weight.shape, f32), shaped(down_weight.shape[::-1], f32)],
-    )(*late_pieces)
-
-    bias_parts = jnp.concatenate(
-        [
-            column_sums,
-            one_hot_slots(qkv_bias_part[0, :qkv_cols], head_at, head_groups),
-            one_hot_slots(up_bias_part[0, :ff], ctx_at, ctx_count),
-        ]
-    )
-    small = jnp.concatenate([gain_parts, bias_parts])
-    small = butterfly(butterfly(small, "fsdp"), "ctx")
-    cuts = []
-    start = 0
-    for extent in [width] * 5 + [3 * HD * heads, hidden_all]:
-        cuts.append(small[start : start + extent])
-        start += extent
+    up_weight_grad, down_weight_grad, gains, column_grad, qkv_bias_grad, up_bias_grad = (
+        local_kernel(
+            functools.partial(
+                late_end_kernel, ctx_count, head_groups, ff, padded, qkv_cols, cols
+            ),
+            [
+                shaped(up_weight.shape, f32),
+                shaped(down_weight.shape[::-1], f32),
+                shaped((4 * width // LANES, LANES), f32),
+                shaped((width // LANES, LANES), f32),
+                shaped((3 * HD * heads // LANES, LANES), f32),
+                shaped((hidden_all // LANES, LANES), f32),
+            ],
+        )(*late_pieces)
+    )
+    gains = sum(spread(gains, "tp")).reshape(4, width)
+    column_grad = column_grad.reshape(width)
     return (
         block_out,
         tokens_grad,
-        cuts[0],
-        cuts[1],
+        gains[0],
+        gains[1],
         qkv_weight_grad,
-        cuts[5],
+        qkv_bias_grad.reshape(3 * HD * heads),
         dense_weight_grad.T,
-        cuts[4],
-        cuts[2],
-        cuts[3],
+        column_grad,
+        gains[2],
+        gains[3],
         up_weight_grad,
-        cuts[6],
+        up_bias_grad.reshape(hidden_all),
         down_weight_grad.T,
-        cuts[4],
+        column_grad,
     )
 
 

time: 138 us -> 134 us (0.971)
  waiting for transfers between devices: 37.7 us -> 50.1 us
  starting transfers between devices: 49.5 us -> 37.7 us
  local copies, waits for them, and re-layouts: 10 us -> 6.93 us
  other arithmetic: 11.1 us -> 9.64 us
    ppermute x36 -> x33, waiting for transfers between devices: 37.7 us -> 50.1 us  [swap(): lax.ppermute(value, axis, [(i, i ^ bit) for i in range(lax.axis_size(axis...]
    ppermute x36 -> x33, starting transfers between devices: 49.5 us -> 37.7 us  [swap(): lax.ppermute(value, axis, [(i, i ^ bit) for i in range(lax.axis_size(axis...]
    slice x6 -> x0, local copies, waits for them, and re-layouts: 1.93 us -> none  [the longest x3 1.81 us: on_device(): cuts.append(small[start:start + extent])]
    concatenate x2 -> x0, local copies, waits for them, and re-layouts: 1.79 us -> none  [the longest x1 0.89 us: rotary_tables(): jnp.concatenate([cos_head] * 2, axis=1)]
    unnamed x79 -> x59, local copies, waits for them, and re-layouts: 4.07 us -> 5.36 us
  transfers between devices with their start and end apart: 36 -> 33, of which waited for: 13 -> 13; matrix products, arithmetic and copies ran while one was open for 12% -> 8% of each run, Pallas kernels for 14% -> 14%
where the time goes in v2:
time: 134 us; the launch traced here: 133 us
  waiting for transfers between devices  50.1 us (37%)
  starting transfers between devices  37.7 us (28%)
  Pallas kernels  27.8 us (21%)
  other arithmetic  9.64 us (7%)
  local copies, waits for them, and re-layouts  6.93 us (5%)
    ppermute x33, waiting for transfers between devices, swap(): lax.ppermute(value, axis, [(i, i ^ bit) for i in range(lax.axis_size(axis...  50.1 us
    ppermute x33, starting transfers between devices, swap(): lax.ppermute(value, axis, [(i, i ^ bit) for i in range(lax.axis_size(axis...  37.7 us
    pallas_call x1, Pallas kernels, on_device(): local_kernel(functools.partial(attention_kernel, fsdp_count, tp_count, ne...  8.65 us
    pallas_call x1, Pallas kernels, on_device(): local_kernel(functools.partial(mlp_kernel, fsdp_count, tp_count, near, he...  7.42 us
    unnamed x59, local copies, waits for them, and re-layouts  5.36 us
    pallas_call x2, Pallas kernels, scatter_weights(): local_kernel(functools.partial(sum_blocks_kernel, fsdp_count, ctx_count,...  4.47 us
  transfers between devices with their start and end apart: 33, of which 13 were waited for; matrix products, arithmetic and copies ran while one was open for 8% of the time, Pallas kernels for 14%

profile of v2, /device:TPU:0, one launch (start us, length us, event | category | flops | bytes accessed | tf_op | source)
XLA Modules:
  0.0 133.2 jit_solution(17573574401043924447)
XLA Ops:
  0.7 1.7 %shard_map.255 = (bf16[48,768]{1,0:T(8,128)(2,1)}, bf16[48,768]{1,0:T(8,128)(2,1)}) custom-call(bf16[48,1152]{1,0:T(8,128)(2,1)} %qkv_ref.1, bf16[48,384]{1,0:T(8,128)(2,1)} %bitcast.55), custom_call_target="tpu_custom_call" | custom-call | tf_op jit(solution)/shard_map/pallas_call | solution.py:485
  2.4 3.1 %collective-permute-start.9 = (bf16[48,768]{1,0:T(8,128)(2,1)}, bf16[48,768]{1,0:T(8,128)(2,1)S(1)}, u32[]{:S(2)}, u32[]{:S(2)}) collective-permute-start(bf16[48,768]{1,0:T(8,128)(2,1)} %get-tuple-element.55), channel_id=1, source_target_pairs={{0,2},{2,0},{4,6},{6,4},{1,3},{3,1},{5,7},{7,5},{8,10},{10,8},{12,... | collective-permute-start | bytes 221192 | tf_op jit(solution)/shard_map/ppermute | solution.py:43
  5.4 2.5 %collective-permute-start.11 = (bf16[48,768]{1,0:T(8,128)(2,1)}, bf16[48,768]{1,0:T(8,128)(2,1)S(1)}, u32[]{:S(2)}, u32[]{:S(2)}) collective-permute-start(bf16[48,768]{1,0:T(8,128)(2,1)} %get-tuple-element.55), channel_id=1, source_target_pairs={{0,6},{2,4},{4,2},{6,0},{1,7},{3,5},{5,3},{7,1},{8,14},{10,12},{12... | collective-permute-start | bytes 221192 | tf_op jit(solution)/shard_map/ppermute | solution.py:43
  7.9 1.1 convert_reduce_fusion
  9.0 1.1 convert_bitcast_fusion
  10.2 2.8 %collective-permute-start.10 = (bf16[48,768]{1,0:T(8,128)(2,1)}, bf16[48,768]{1,0:T(8,128)(2,1)S(1)}, u32[]{:S(2)}, u32[]{:S(2)}) collective-permute-start(bf16[48,768]{1,0:T(8,128)(2,1)} %get-tuple-element.54), channel_id=1, source_target_pairs={{0,4},{2,6},{4,0},{6,2},{1,5},{3,7},{5,1},{7,3},{8,12},{10,14},{12... | collective-permute-start | bytes 221192 | tf_op jit(solution)/shard_map/ppermute | solution.py:43
  13.0 1.7 %shard_map.254 = (bf16[48,768]{1,0:T(8,128)(2,1)}, bf16[48,768]{1,0:T(8,128)(2,1)}, bf16[48,768]{1,0:T(8,128)(2,1)}, bf16[48,768]{1,0:T(8,128)(2,1)}) custom-call(bf16[48,1536]{1,0:T(8,128)(2,1)} %up_ref.1, bf16[48,1536]{1,0:T(8,128)(2,1)} %bitcast.54), custom_call_target="tpu_custom_call" | custom-call | tf_op jit(solution)/shard_map/pallas_call | solution.py:489
  15.6 0.7 select_reduce_fusion.3
  16.4 0.9 constant_dynamic-update-slice_fusion.7
  17.3 5.8 %collective-permute-done = bf16[2,1,1,64,768]{4,3,0,2,1:T(8,128)(2,1)S(1)} collective-permute-done((bf16[2,1,1,64,768]{4,3,0,2,1:T(8,128)(2,1)S(1)}, bf16[2,1,1,64,768]{4,3,0,2,1:T(8,128)(2,1)S(1)}, u32[]{:S(2)}, u32[]{:S(2)}) %collective-permute-start) | collective-permute-done | bytes 196640 | tf_op jit(solution)/shard_map/ppermute | solution.py:43
  23.3 0.8 copy.45.refs_11_
  24.8 1.2 fusion.11
  26.0 7.9 %collective-permute-done.1 = bf16[2,1,2,64,768]{4,3,0,2,1:T(8,128)(2,1)S(1)} collective-permute-done((bf16[2,1,2,64,768]{4,3,0,2,1:T(8,128)(2,1)S(1)}, bf16[2,1,2,64,768]{4,3,0,2,1:T(8,128)(2,1)S(1)}, u32[]{:S(2)}, u32[]{:S(2)}) %collective-permute-start.1) | collective-permute-done | bytes 393248 | tf_op jit(solution)/shard_map/ppermute | solution.py:43
  34.8 2.1 %collective-permute-start.5 = (bf16[48,768]{1,0:T(8,128)(2,1)S(1)}, bf16[48,768]{1,0:T(8,128)(2,1)S(1)}, u32[]{:S(2)}, u32[]{:S(2)}) collective-permute-start(bf16[48,768]{1,0:T(8,128)(2,1)S(1)} %copy-done.24), channel_id=1, source_target_pairs={{0,6},{2,4},{4,2},{6,0},{1,7},{3,5},{5,3},{7,1},{8,14},{10,12},{12... | collective-permute-start | bytes 221192 | tf_op jit(solution)/shard_map/ppermute | solution.py:43
  37.0 1.6 %collective-permute-start.12 = (bf16[192,768]{1,0:T(8,128)(2,1)S(1)}, bf16[192,768]{1,0:T(8,128)(2,1)S(1)}, u32[]{:S(2)}, u32[]{:S(2)}) collective-permute-start(bf16[192,768]{1,0:T(8,128)(2,1)S(1)} %constant_dynamic-update-slice_fusion.4.refs_2_), channel_id=1, source_target_pairs={{0,8},{8,0},{16,24},{24,16},{1,9},{9,1},{17,25},{25,17},{2,10},{10... | collective-permute-start | bytes 884744 | tf_op jit(solution)/shard_map/ppermute | solution.py:43
  38.5 1.5 %collective-permute-start.13 = (bf16[192,768]{1,0:T(8,128)(2,1)S(1)}, bf16[192,768]{1,0:T(8,128)(2,1)S(1)}, u32[]{:S(2)}, u32[]{:S(2)}) collective-permute-start(bf16[192,768]{1,0:T(8,128)(2,1)S(1)} %constant_dynamic-update-slice_fusion.4.refs_2_), channel_id=1, source_target_pairs={{0,16},{8,24},{16,0},{24,8},{1,17},{9,25},{17,1},{25,9},{2,18},{10... | collective-permute-start | bytes 884744 | tf_op jit(solution)/shard_map/ppermute | solution.py:43
  40.0 1.9 %collective-permute-done.4 = bf16[48,768]{1,0:T(8,128)(2,1)S(1)} collective-permute-done((bf16[48,768]{1,0:T(8,128)(2,1)S(1)}, bf16[48,768]{1,0:T(8,128)(2,1)S(1)}, u32[]{:S(2)}, u32[]{:S(2)}) %collective-permute-start.4) | collective-permute-done | bytes 73760 | tf_op jit(solution)/shard_map/ppermute | solution.py:43
  41.9 2.4 %collective-permute-start.14 = (bf16[192,768]{1,0:T(8,128)(2,1)S(1)}, bf16[192,768]{1,0:T(8,128)(2,1)S(1)}, u32[]{:S(2)}, u32[]{:S(2)}) collective-permute-start(bf16[192,768]{1,0:T(8,128)(2,1)S(1)} %constant_dynamic-update-slice_fusion.4.refs_2_), channel_id=1, source_target_pairs={{0,24},{8,16},{16,8},{24,0},{1,25},{9,17},{17,9},{25,1},{2,26},{10... | collective-permute-start | bytes 884744 | tf_op jit(solution)/shard_map/ppermute | solution.py:43
  45.0 1.9 %collective-permute-done.12.refs_3_ = bf16[192,768]{1,0:T(8,128)(2,1)S(1)} collective-permute-done((bf16[192,768]{1,0:T(8,128)(2,1)S(1)}, bf16[192,768]{1,0:T(8,128)(2,1)S(1)}, u32[]{:S(2)}, u32[]{:S(2)}) %collective-permute-start.12) | collective-permute-done | bytes 294944 | tf_op jit(solution)/shard_map/ppermute | solution.py:43
  46.9 1.5 %collective-permute-start.7 = (bf16[192,768]{1,0:T(8,128)(2,1)S(1)}, bf16[192,768]{1,0:T(8,128)(2,1)S(1)}, u32[]{:S(2)}, u32[]{:S(2)}) collective-permute-start(bf16[192,768]{1,0:T(8,128)(2,1)S(1)} %constant_dynamic-update-slice_fusion.refs_2_), channel_id=1, source_target_pairs={{0,16},{8,24},{16,0},{24,8},{1,17},{9,25},{17,1},{25,9},{2,18},{10... | collective-permute-start | bytes 884744 | tf_op jit(solution)/shard_map/ppermute | solution.py:43
  48.4 5.3 %collective-permute-done.13.refs_4_ = bf16[192,768]{1,0:T(8,128)(2,1)S(1)} collective-permute-done((bf16[192,768]{1,0:T(8,128)(2,1)S(1)}, bf16[192,768]{1,0:T(8,128)(2,1)S(1)}, u32[]{:S(2)}, u32[]{:S(2)}) %collective-permute-start.13) | collective-permute-done | bytes 294944 | tf_op jit(solution)/shard_map/ppermute | solution.py:43
  53.8 1.3 %collective-permute-start.8 = (bf16[192,768]{1,0:T(8,128)(2,1)S(1)}, bf16[192,768]{1,0:T(8,128)(2,1)}, u32[]{:S(2)}, u32[]{:S(2)}) collective-permute-start(bf16[192,768]{1,0:T(8,128)(2,1)S(1)} %constant_dynamic-update-slice_fusion.refs_2_), channel_id=1, source_target_pairs={{0,24},{8,16},{16,8},{24,0},{1,25},{9,17},{17,9},{25,1},{2,26},{10... | collective-permute-start | bytes 884744 | tf_op jit(solution)/shard_map/ppermute | solution.py:43
  55.8 0.9 copy-done.18
  56.7 8.7 %shard_map.256 = (f32[256,768]{1,0:T(8,128)}, f32[256,768]{1,0:T(8,128)}, f32[2,768]{1,0:T(2,128)}, f32[1,768]{1,0:T(1,128)}, f32[192,768]{1,0:T(8,128)}, /*inde...) custom-call(bf16[2,1,256,768]{3,2,1,0:T(8,128)(2,1)} %bitcast.52, ...), custom_call_target="tpu_custom_call" | custom-call | flops 2415919104 | bytes 3145728 | tf_op jit(solution)/shard_map/pallas_call | solution.py:533
  65.4 0.9 collective-permute-done.7.refs_4_
  67.0 7.4 %shard_map.257 = (f32[2,1,256,768]{3,2,1,0:T(8,128)}, f32[2,1,256,768]{3,2,1,0:T(8,128)}, f32[208,768]{1,0:T(8,128)}, bf16[208,768]{1,0:T(8,128)(2,1)}, bf16[208...) custom-call(bf16[2,1,256,768]{3,2,1,0:T(8,128)(2,1)} %bitcast.53, bf16[2,1,256,768]{3,2,1,0:T(8,128)(2,1)} %copy-done.18, ...), custom_call_target="tpu_custom_call" | custom-call | flops 1811939328 | bytes 6291456 | tf_op jit(solution)/shard_map/pallas_call | solution.py:567
  74.5 1.9 %collective-permute-start.20 = (bf16[208,768]{1,0:T(8,128)(2,1)}, bf16[208,768]{1,0:T(8,128)(2,1)S(1)}, u32[]{:S(2)}, u32[]{:S(2)}) collective-permute-start(bf16[208,768]{1,0:T(8,128)(2,1)} %get-tuple-element.63), channel_id=1, source_target_pairs={{0,8},{8,0},{16,24},{24,16},{1,9},{9,1},{17,25},{25,17},{2,10},{10... | collective-permute-start | bytes 958472 | tf_op jit(solution)/shard_map/ppermute | solution.py:43
  76.6 1.4 %collective-permute-start.22 = (bf16[208,768]{1,0:T(8,128)(2,1)}, bf16[208,768]{1,0:T(8,128)(2,1)S(1)}, u32[]{:S(2)}, u32[]{:S(2)}) collective-permute-start(bf16[208,768]{1,0:T(8,128)(2,1)} %get-tuple-element.65), channel_id=1, source_target_pairs={{0,24},{8,16},{16,8},{24,0},{1,25},{9,17},{17,9},{25,1},{2,26},{10... | collective-permute-start | bytes 958472 | tf_op jit(solution)/shard_map/ppermute | solution.py:43
  78.0 1.8 %collective-permute-start.27 = (bf16[192,768]{1,0:T(8,128)(2,1)}, bf16[192,768]{1,0:T(8,128)(2,1)}, u32[]{:S(2)}, u32[]{:S(2)}) collective-permute-start(bf16[192,768]{1,0:T(8,128)(2,1)} %get-tuple-element.72), channel_id=1, source_target_pairs={{0,8},{8,0},{16,24},{24,16},{1,9},{9,1},{17,25},{25,17},{2,10},{10... | collective-permute-start | bytes 884744 | tf_op jit(solution)/shard_map/ppermute | solution.py:43
  80.1 1.6 %add.315 = f32[2,1,256,768]{3,2,1,0:T(8,128)S(1)} add(f32[2,1,256,768]{3,2,1,0:T(8,128)} %get-tuple-element.60, f32[2,1,256,768]{3,2,1,0:T(8,128)S(1)} %collective-permute-done.15) | non-fusion elementwise | flops 393216 | bytes 4718592 | tf_op jit(solution)/shard_map/add | solution.py:588
  81.7 3.4 %collective-permute-done.20.refs_1_ = bf16[208,768]{1,0:T(8,128)(2,1)S(1)} collective-permute-done((bf16[208,768]{1,0:T(8,128)(2,1)}, bf16[208,768]{1,0:T(8,128)(2,1)S(1)}, u32[]{:S(2)}, u32[]{:S(2)}) %collective-permute-start.20) | collective-permute-done | bytes 319520 | tf_op jit(solution)/shard_map/ppermute | solution.py:43
  85.2 0.8 collective-permute-start.16
  86.0 7.8 %collective-permute-done.21.refs_2_ = bf16[208,768]{1,0:T(8,128)(2,1)S(1)} collective-permute-done((bf16[208,768]{1,0:T(8,128)(2,1)}, bf16[208,768]{1,0:T(8,128)(2,1)S(1)}, u32[]{:S(2)}, u32[]{:S(2)}) %collective-permute-start.21) | collective-permute-done | bytes 319520 | tf_op jit(solution)/shard_map/ppermute | solution.py:43
  93.8 1.2 collective-permute-start.29
  95.0 0.7 copy-done.4
  95.7 2.3 %shard_map.258 = (f32[64,768]{1,0:T(8,128)}, bf16[64,768]{1,0:T(8,128)(2,1)}, bf16[64,768]{1,0:T(8,128)(2,1)}, bf16[64,768]{1,0:T(8,128)(2,1)}) custom-call(f32[208,768]{1,0:T(8,128)} %get-tuple-element.62.refs_0_, bf16[208,768]{1,0:T(8,128)(2,1)} %copy-done.2, bf16[208,768]{1,0:T(8,128)(2,1)} %copy-done.3, bf16[208,768]{1,0:T(8,128)(2,1)} %copy-done.4), custom_call_target="tpu_custom_call" | custom-call | tf_op jit(solution)/shard_map/pallas_call | solution.py:600
  98.0 0.8 collective-permute-start.23
  98.8 1.4 %collective-permute-start.24 = (bf16[64,768]{1,0:T(8,128)(2,1)}, bf16[64,768]{1,0:T(8,128)(2,1)S(1)}, u32[]{:S(2)}, u32[]{:S(2)}) collective-permute-start(bf16[64,768]{1,0:T(8,128)(2,1)} %get-tuple-element.68), channel_id=1, source_target_pairs={{0,4},{2,6},{4,0},{6,2},{1,5},{3,7},{5,1},{7,3},{8,12},{10,14},{12... | collective-permute-start | bytes 294920 | tf_op jit(solution)/shard_map/ppermute | solution.py:43
  100.3 5.5 %collective-permute-done.28.refs_2_ = bf16[192,768]{1,0:T(8,128)(2,1)} collective-permute-done((bf16[192,768]{1,0:T(8,128)(2,1)}, bf16[192,768]{1,0:T(8,128)(2,1)}, u32[]{:S(2)}, u32[]{:S(2)}) %collective-permute-start.28) | collective-permute-done | bytes 294944 | tf_op jit(solution)/shard_map/ppermute | solution.py:43
  105.7 1.7 %collective-permute-start.25 = (bf16[64,768]{1,0:T(8,128)(2,1)}, bf16[64,768]{1,0:T(8,128)(2,1)S(1)}, u32[]{:S(2)}, u32[]{:S(2)}) collective-permute-start(bf16[64,768]{1,0:T(8,128)(2,1)} %get-tuple-element.69), channel_id=1, source_target_pairs={{0,6},{2,4},{4,2},{6,0},{1,7},{3,5},{5,3},{7,1},{8,14},{10,12},{12... | collective-permute-start | bytes 294920 | tf_op jit(solution)/shard_map/ppermute | solution.py:43
  107.6 2.2 %shard_map.260 = (f32[48,768]{1,0:T(8,128)}, bf16[48,768]{1,0:T(8,128)(2,1)}, bf16[48,768]{1,0:T(8,128)(2,1)}, bf16[48,768]{1,0:T(8,128)(2,1)}) custom-call(f32[192,768]{1,0:T(8,128)} %get-tuple-element.71.refs_0_, bf16[192,768]{1,0:T(8,128)(2,1)} %collective-permute-done.27.refs_1_, bf16[192,768]{1,0:T(8,128)(2,1)} %collective-permute-done.28.refs_2_, ...), custom_call_target="tpu_custom_call" | custom-call | tf_op jit(solution)/shard_map/pallas_call | solution.py:600
  109.9 2.6 %collective-permute-start.31 = (bf16[48,768]{1,0:T(8,128)(2,1)}, bf16[48,768]{1,0:T(8,128)(2,1)S(1)}, u32[]{:S(2)}, u32[]{:S(2)}) collective-permute-start(bf16[48,768]{1,0:T(8,128)(2,1)} %get-tuple-element.77), channel_id=1, source_target_pairs={{0,4},{2,6},{4,0},{6,2},{1,5},{3,7},{5,1},{7,3},{8,12},{10,14},{12... | collective-permute-start | bytes 221192 | tf_op jit(solution)/shard_map/ppermute | solution.py:43
  112.6 1.7 %collective-permute-start.32 = (bf16[48,768]{1,0:T(8,128)(2,1)}, bf16[48,768]{1,0:T(8,128)(2,1)S(1)}, u32[]{:S(2)}, u32[]{:S(2)}) collective-permute-start(bf16[48,768]{1,0:T(8,128)(2,1)} %get-tuple-element.78), channel_id=1, source_target_pairs={{0,6},{2,4},{4,2},{6,0},{1,7},{3,5},{5,3},{7,1},{8,14},{10,12},{12... | collective-permute-start | bytes 221192 | tf_op jit(solution)/shard_map/ppermute | solution.py:43
  114.9 2.0 %shard_map.259 = (f32[48,1536]{1,0:T(8,128)}, f32[48,1536]{1,0:T(8,128)}, f32[24,128]{1,0:T(8,128)}, f32[6,128]{1,0:T(8,128)}, f32[9,128]{1,0:T(8,128)}, /*index=5*/f32[12,128]{1,0:T(8,128)}) custom-call(f32[64,768]{1,0:T(8,128)} %get-tuple-element.66.refs_0_, bf16[64,768]{1,0:T(8,128)(2,1)} %copy-done.5, bf16[64,768]{1,0:T(8,128)(2,1)} %copy-done.6, ...), custom_call_target="tpu_custom_call" | custom-call | tf_op jit(solution)/shard_map/pallas_call | solution.py:622
  117.3 1.7 %collective-permute-done.32.refs_3_ = bf16[48,768]{1,0:T(8,128)(2,1)S(1)} collective-permute-done((bf16[48,768]{1,0:T(8,128)(2,1)}, bf16[48,768]{1,0:T(8,128)(2,1)S(1)}, u32[]{:S(2)}, u32[]{:S(2)}) %collective-permute-start.32) | collective-permute-done | bytes 73760 | tf_op jit(solution)/shard_map/ppermute | solution.py:43
  119.6 1.8 %shard_map.261 = (f32[48,1152]{1,0:T(8,128)}, f32[48,384]{1,0:T(8,128)}) custom-call(f32[48,768]{1,0:T(8,128)} %get-tuple-element.75.refs_0_, bf16[48,768]{1,0:T(8,128)(2,1)} %copy-done.9, bf16[48,768]{1,0:T(8,128)(2,1)} %copy-done.10, bf16[48,768]{1,0:T(8,128)(2,1)} %copy-done.11), custom_call_target="tpu_custom_call" | custom-call | tf_op jit(solution)/shard_map/pallas_call | solution.py:617
  121.4 7.6 %collective-permute-done.17 = bf16[2,1,1,64,768]{4,3,2,1,0:T(8,128)(2,1)S(1)} collective-permute-done((bf16[2,1,1,64,768]{4,3,2,1,0:T(8,128)(2,1)S(1)}, bf16[2,1,1,64,768]{4,3,2,1,0:T(8,128)(2,1)S(1)}, u32[]{:S(2)}, u32[]{:S(2)}) %collective-permute-start.17) | collective-permute-done | bytes 196640 | tf_op jit(solution)/shard_map/ppermute | solution.py:43
  131.9 0.8 pad_maximum_fusion.2
  (127 shorter events, 10.5 us)
Async XLA Ops:
  0.6 23.5 %copy-start = (f32[2,64,768]{2,1,0:T(8,128)S(1)}, f32[2,64,768]{2,1,0:T(8,128)}, u32[]{:S(2)}) copy-start(f32[2,64,768]{2,1,0:T(8,128)} %param.29) | copy-start | bytes 1179652
  2.4 32.2 %collective-permute-start.9 = (bf16[48,768]{1,0:T(8,128)(2,1)}, bf16[48,768]{1,0:T(8,128)(2,1)S(1)}, u32[]{:S(2)}, u32[]{:S(2)}) collective-permute-start(bf16[48,768]{1,0:T(8,128)(2,1)} %get-tuple-element.55), channel_id=1, source_target_pairs={{0,2},{2,0},{4,6},{6,4},{1,3},{3,1},{5,7},{7,5},{8,10},{10,8},{12,... | collective-permute-start | bytes 221192 | tf_op jit(solution)/shard_map/ppermute | solution.py:43
  5.4 31.5 %collective-permute-start.11 = (bf16[48,768]{1,0:T(8,128)(2,1)}, bf16[48,768]{1,0:T(8,128)(2,1)S(1)}, u32[]{:S(2)}, u32[]{:S(2)}) collective-permute-start(bf16[48,768]{1,0:T(8,128)(2,1)} %get-tuple-element.55), channel_id=1, source_target_pairs={{0,6},{2,4},{4,2},{6,0},{1,7},{3,5},{5,3},{7,1},{8,14},{10,12},{12... | collective-permute-start | bytes 221192 | tf_op jit(solution)/shard_map/ppermute | solution.py:43
  10.1 13.0 %collective-permute-start = (bf16[2,1,1,64,768]{4,3,0,2,1:T(8,128)(2,1)S(1)}, bf16[2,1,1,64,768]{4,3,0,2,1:T(8,128)(2,1)S(1)}, u32[]{:S(2)}, u32[]{:S(2)}) collective-permute-start(bf16[2,1,1,64,768]{4,3,0,2,1:T(8,128)(2,1)S(1)} %maximum_bitcast_fusion), channel_id=1, source_target_pairs={{0,4},{2,6},{4,0},{6,2},{1,5},{3,7},{5,1},{7,3},{8,12},{10,14},{12... | collective-permute-start | bytes 589832 | tf_op jit(solution)/shard_map/ppermute | solution.py:43
  10.2 24.5 %collective-permute-start.10 = (bf16[48,768]{1,0:T(8,128)(2,1)}, bf16[48,768]{1,0:T(8,128)(2,1)S(1)}, u32[]{:S(2)}, u32[]{:S(2)}) collective-permute-start(bf16[48,768]{1,0:T(8,128)(2,1)} %get-tuple-element.54), channel_id=1, source_target_pairs={{0,4},{2,6},{4,0},{6,2},{1,5},{3,7},{5,1},{7,3},{8,12},{10,14},{12... | collective-permute-start | bytes 221192 | tf_op jit(solution)/shard_map/ppermute | solution.py:43
  14.8 10.0 %copy-start.8 = (bf16[48,768]{1,0:T(8,128)(2,1)S(1)}, bf16[48,768]{1,0:T(8,128)(2,1)}, u32[]{:S(2)}) copy-start(bf16[48,768]{1,0:T(8,128)(2,1)} %get-tuple-element.50) | copy-start | bytes 221188
  14.8 19.2 %copy-start.25 = (bf16[48,768]{1,0:T(8,128)(2,1)S(1)}, bf16[48,768]{1,0:T(8,128)(2,1)}, u32[]{:S(2)}) copy-start(bf16[48,768]{1,0:T(8,128)(2,1)} %get-tuple-element.52) | copy-start | bytes 221188
  14.8 23.8 %collective-permute-start.3 = (bf16[48,768]{1,0:T(8,128)(2,1)}, bf16[48,768]{1,0:T(8,128)(2,1)S(1)}, u32[]{:S(2)}, u32[]{:S(2)}) collective-permute-start(bf16[48,768]{1,0:T(8,128)(2,1)} %get-tuple-element.51), channel_id=1, source_target_pairs={{0,2},{2,0},{4,6},{6,4},{1,3},{3,1},{5,7},{7,5},{8,10},{10,8},{12,... | collective-permute-start | bytes 221192 | tf_op jit(solution)/shard_map/ppermute | solution.py:43
  23.1 10.8 %collective-permute-start.1 = (bf16[2,1,2,64,768]{4,3,0,2,1:T(8,128)(2,1)S(1)}, bf16[2,1,2,64,768]{4,3,0,2,1:T(8,128)(2,1)S(1)}, u32[]{:S(2)}, u32[]{:S(2)}) collective-permute-start(bf16[2,1,2,64,768]{4,3,0,2,1:T(8,128)(2,1)S(1)} %pad_maximum_fusion.1), channel_id=1, source_target_pairs={{0,2},{2,0},{4,6},{6,4},{1,3},{3,1},{5,7},{7,5},{8,10},{10,8},{12,... | collective-permute-start | bytes 1179656 | tf_op jit(solution)/shard_map/ppermute | solution.py:43
  33.9 8.0 %collective-permute-start.4 = (bf16[48,768]{1,0:T(8,128)(2,1)S(1)}, bf16[48,768]{1,0:T(8,128)(2,1)S(1)}, u32[]{:S(2)}, u32[]{:S(2)}) collective-permute-start(bf16[48,768]{1,0:T(8,128)(2,1)S(1)} %copy-done.25), channel_id=1, source_target_pairs={{0,4},{2,6},{4,0},{6,2},{1,5},{3,7},{5,1},{7,3},{8,12},{10,14},{12... | collective-permute-start | bytes 221192 | tf_op jit(solution)/shard_map/ppermute | solution.py:43
  34.6 22.1 %copy-start.1 = (bf16[2,1,4,64,768]{4,3,2,0,1:T(8,128)(2,1)}, bf16[2,1,4,64,768]{4,3,2,0,1:T(8,128)(2,1)S(1)}, u32[]{:S(2)}) copy-start(bf16[2,1,4,64,768]{4,3,2,0,1:T(8,128)(2,1)S(1)} %copy.44) | copy-start | bytes 2359300
  34.6 21.1 %collective-permute-start.2 = (bf16[2,1,256,768]{3,2,1,0:T(8,128)(2,1)S(1)}, bf16[2,1,256,768]{3,2,1,0:T(8,128)(2,1)S(1)}, u32[]{:S(2)}, u32[]{:S(2)}) collective-permute-start(bf16[2,1,256,768]{3,2,1,0:T(8,128)(2,1)S(1)} %bitcast.51), channel_id=1, source_target_pairs={{0,1},{1,0},{2,3},{3,2},{4,5},{5,4},{6,7},{7,6},{8,9},{9,8},{10,11... | collective-permute-start | bytes 2359304 | tf_op jit(solution)/shard_map/ppermute | solution.py:43
  34.8 9.6 %collective-permute-start.5 = (bf16[48,768]{1,0:T(8,128)(2,1)S(1)}, bf16[48,768]{1,0:T(8,128)(2,1)S(1)}, u32[]{:S(2)}, u32[]{:S(2)}) collective-permute-start(bf16[48,768]{1,0:T(8,128)(2,1)S(1)} %copy-done.24), channel_id=1, source_target_pairs={{0,6},{2,4},{4,2},{6,0},{1,7},{3,5},{5,3},{7,1},{8,14},{10,12},{12... | collective-permute-start | bytes 221192 | tf_op jit(solution)/shard_map/ppermute | solution.py:43
  36.9 19.7 %copy-start.13 = (bf16[192,768]{1,0:T(8,128)(2,1)}, bf16[192,768]{1,0:T(8,128)(2,1)S(1)}, u32[]{:S(2)}) copy-start(bf16[192,768]{1,0:T(8,128)(2,1)S(1)} %constant_dynamic-update-slice_fusion.4.refs_2_) | copy-start | bytes 884740
  37.0 9.9 %collective-permute-start.12 = (bf16[192,768]{1,0:T(8,128)(2,1)S(1)}, bf16[192,768]{1,0:T(8,128)(2,1)S(1)}, u32[]{:S(2)}, u32[]{:S(2)}) collective-permute-start(bf16[192,768]{1,0:T(8,128)(2,1)S(1)} %constant_dynamic-update-slice_fusion.4.refs_2_), channel_id=1, source_target_pairs={{0,8},{8,0},{16,24},{24,16},{1,9},{9,1},{17,25},{25,17},{2,10},{10... | collective-permute-start | bytes 884744 | tf_op jit(solution)/shard_map/ppermute | solution.py:43
  38.5 15.2 %collective-permute-start.13 = (bf16[192,768]{1,0:T(8,128)(2,1)S(1)}, bf16[192,768]{1,0:T(8,128)(2,1)S(1)}, u32[]{:S(2)}, u32[]{:S(2)}) collective-permute-start(bf16[192,768]{1,0:T(8,128)(2,1)S(1)} %constant_dynamic-update-slice_fusion.4.refs_2_), channel_id=1, source_target_pairs={{0,16},{8,24},{16,0},{24,8},{1,17},{9,25},{17,1},{25,9},{2,18},{10... | collective-permute-start | bytes 884744 | tf_op jit(solution)/shard_map/ppermute | solution.py:43
  41.9 13.8 %collective-permute-start.14 = (bf16[192,768]{1,0:T(8,128)(2,1)S(1)}, bf16[192,768]{1,0:T(8,128)(2,1)S(1)}, u32[]{:S(2)}, u32[]{:S(2)}) collective-permute-start(bf16[192,768]{1,0:T(8,128)(2,1)S(1)} %constant_dynamic-update-slice_fusion.4.refs_2_), channel_id=1, source_target_pairs={{0,24},{8,16},{16,8},{24,0},{1,25},{9,17},{17,9},{25,1},{2,26},{10... | collective-permute-start | bytes 884744 | tf_op jit(solution)/shard_map/ppermute | solution.py:43
  44.4 21.0 %copy-start.12 = (bf16[192,768]{1,0:T(8,128)(2,1)}, bf16[192,768]{1,0:T(8,128)(2,1)S(1)}, u32[]{:S(2)}) copy-start(bf16[192,768]{1,0:T(8,128)(2,1)S(1)} %constant_dynamic-update-slice_fusion.refs_2_) | copy-start | bytes 884740
  44.4 21.0 %collective-permute-start.6 = (bf16[192,768]{1,0:T(8,128)(2,1)S(1)}, bf16[192,768]{1,0:T(8,128)(2,1)S(1)}, u32[]{:S(2)}, u32[]{:S(2)}) collective-permute-start(bf16[192,768]{1,0:T(8,128)(2,1)S(1)} %constant_dynamic-update-slice_fusion.refs_2_), channel_id=1, source_target_pairs={{0,8},{8,0},{16,24},{24,16},{1,9},{9,1},{17,25},{25,17},{2,10},{10... | collective-permute-start | bytes 884744 | tf_op jit(solution)/shard_map/ppermute | solution.py:43
  46.9 9.8 %copy-start.19 = (bf16[192,768]{1,0:T(8,128)(2,1)}, bf16[192,768]{1,0:T(8,128)(2,1)S(1)}, u32[]{:S(2)}) copy-start(bf16[192,768]{1,0:T(8,128)(2,1)S(1)} %collective-permute-done.12.refs_3_) | copy-start | bytes 884740
  46.9 19.4 %collective-permute-start.7 = (bf16[192,768]{1,0:T(8,128)(2,1)S(1)}, bf16[192,768]{1,0:T(8,128)(2,1)S(1)}, u32[]{:S(2)}, u32[]{:S(2)}) collective-permute-start(bf16[192,768]{1,0:T(8,128)(2,1)S(1)} %constant_dynamic-update-slice_fusion.refs_2_), channel_id=1, source_target_pairs={{0,16},{8,24},{16,0},{24,8},{1,17},{9,25},{17,1},{25,9},{2,18},{10... | collective-permute-start | bytes 884744 | tf_op jit(solution)/shard_map/ppermute | solution.py:43
  53.8 2.9 %copy-start.20 = (bf16[192,768]{1,0:T(8,128)(2,1)}, bf16[192,768]{1,0:T(8,128)(2,1)S(1)}, u32[]{:S(2)}) copy-start(bf16[192,768]{1,0:T(8,128)(2,1)S(1)} %collective-permute-done.13.refs_4_) | copy-start | bytes 884740
  53.8 12.6 %collective-permute-start.8 = (bf16[192,768]{1,0:T(8,128)(2,1)S(1)}, bf16[192,768]{1,0:T(8,128)(2,1)}, u32[]{:S(2)}, u32[]{:S(2)}) collective-permute-start(bf16[192,768]{1,0:T(8,128)(2,1)S(1)} %constant_dynamic-update-slice_fusion.refs_2_), channel_id=1, source_target_pairs={{0,24},{8,16},{16,8},{24,0},{1,25},{9,17},{17,9},{25,1},{2,26},{10... | collective-permute-start | bytes 884744 | tf_op jit(solution)/shard_map/ppermute | solution.py:43
  74.5 5.4 %collective-permute-start.15 = (f32[2,1,256,768]{3,2,1,0:T(8,128)}, f32[2,1,256,768]{3,2,1,0:T(8,128)S(1)}, u32[]{:S(2)}, u32[]{:S(2)}) collective-permute-start(f32[2,1,256,768]{3,2,1,0:T(8,128)} %get-tuple-element.61), channel_id=1, source_target_pairs={{0,1},{1,0},{2,3},{3,2},{4,5},{5,4},{6,7},{7,6},{8,9},{9,8},{10,11... | collective-permute-start | bytes 4718600 | tf_op jit(solution)/shard_map/ppermute | solution.py:43
  74.5 10.7 %collective-permute-start.20 = (bf16[208,768]{1,0:T(8,128)(2,1)}, bf16[208,768]{1,0:T(8,128)(2,1)S(1)}, u32[]{:S(2)}, u32[]{:S(2)}) collective-permute-start(bf16[208,768]{1,0:T(8,128)(2,1)} %get-tuple-element.63), channel_id=1, source_target_pairs={{0,8},{8,0},{16,24},{24,16},{1,9},{9,1},{17,25},{25,17},{2,10},{10... | collective-permute-start | bytes 958472 | tf_op jit(solution)/shard_map/ppermute | solution.py:43
  76.3 17.5 %collective-permute-start.21 = (bf16[208,768]{1,0:T(8,128)(2,1)}, bf16[208,768]{1,0:T(8,128)(2,1)S(1)}, u32[]{:S(2)}, u32[]{:S(2)}) collective-permute-start(bf16[208,768]{1,0:T(8,128)(2,1)} %get-tuple-element.64), channel_id=1, source_target_pairs={{0,16},{8,24},{16,0},{24,8},{1,17},{9,25},{17,1},{25,9},{2,18},{10... | collective-permute-start | bytes 958472 | tf_op jit(solution)/shard_map/ppermute | solution.py:43
  76.6 18.4 %collective-permute-start.22 = (bf16[208,768]{1,0:T(8,128)(2,1)}, bf16[208,768]{1,0:T(8,128)(2,1)S(1)}, u32[]{:S(2)}, u32[]{:S(2)}) collective-permute-start(bf16[208,768]{1,0:T(8,128)(2,1)} %get-tuple-element.65), channel_id=1, source_target_pairs={{0,24},{8,16},{16,8},{24,0},{1,25},{9,17},{17,9},{25,1},{2,26},{10... | collective-permute-start | bytes 958472 | tf_op jit(solution)/shard_map/ppermute | solution.py:43
  78.0 20.8 %collective-permute-start.27 = (bf16[192,768]{1,0:T(8,128)(2,1)}, bf16[192,768]{1,0:T(8,128)(2,1)}, u32[]{:S(2)}, u32[]{:S(2)}) collective-permute-start(bf16[192,768]{1,0:T(8,128)(2,1)} %get-tuple-element.72), channel_id=1, source_target_pairs={{0,8},{8,0},{16,24},{24,16},{1,9},{9,1},{17,25},{25,17},{2,10},{10... | collective-permute-start | bytes 884744 | tf_op jit(solution)/shard_map/ppermute | solution.py:43
  79.8 25.9 %collective-permute-start.28 = (bf16[192,768]{1,0:T(8,128)(2,1)}, bf16[192,768]{1,0:T(8,128)(2,1)}, u32[]{:S(2)}, u32[]{:S(2)}) collective-permute-start(bf16[192,768]{1,0:T(8,128)(2,1)} %get-tuple-element.73), channel_id=1, source_target_pairs={{0,16},{8,24},{16,0},{24,8},{1,17},{9,25},{17,1},{25,9},{2,18},{10... | collective-permute-start | bytes 884744 | tf_op jit(solution)/shard_map/ppermute | solution.py:43
  85.1 9.9 %copy-start.2 = (bf16[208,768]{1,0:T(8,128)(2,1)}, bf16[208,768]{1,0:T(8,128)(2,1)S(1)}, u32[]{:S(2)}) copy-start(bf16[208,768]{1,0:T(8,128)(2,1)S(1)} %collective-permute-done.20.refs_1_) | copy-start | bytes 958468
  85.2 31.8 %collective-permute-start.16 = (bf16[2,1,2,64,768]{4,3,2,1,0:T(8,128)(2,1)S(1)}, bf16[2,1,2,64,768]{4,3,2,1,0:T(8,128)(2,1)S(1)}, u32[]{:S(2)}, u32[]{:S(2)}) collective-permute-start(bf16[2,1,2,64,768]{4,3,2,1,0:T(8,128)(2,1)S(1)} %split.26), channel_id=1, source_target_pairs={{0,2},{2,0},{4,6},{6,4},{1,3},{3,1},{5,7},{7,5},{8,10},{10,8},{12,... | collective-permute-start | bytes 1179656 | tf_op jit(solution)/shard_map/ppermute | solution.py:43
  93.8 13.8 %collective-permute-start.29 = (bf16[192,768]{1,0:T(8,128)(2,1)}, bf16[192,768]{1,0:T(8,128)(2,1)}, u32[]{:S(2)}, u32[]{:S(2)}) collective-permute-start(bf16[192,768]{1,0:T(8,128)(2,1)} %get-tuple-element.74), channel_id=1, source_target_pairs={{0,24},{8,16},{16,8},{24,0},{1,25},{9,17},{17,9},{25,1},{2,26},{10... | collective-permute-start | bytes 884744 | tf_op jit(solution)/shard_map/ppermute | solution.py:43
  98.0 11.9 %collective-permute-start.23 = (bf16[64,768]{1,0:T(8,128)(2,1)}, bf16[64,768]{1,0:T(8,128)(2,1)S(1)}, u32[]{:S(2)}, u32[]{:S(2)}) collective-permute-start(bf16[64,768]{1,0:T(8,128)(2,1)} %get-tuple-element.67), channel_id=1, source_target_pairs={{0,2},{2,0},{4,6},{6,4},{1,3},{3,1},{5,7},{7,5},{8,10},{10,8},{12,... | collective-permute-start | bytes 294920 | tf_op jit(solution)/shard_map/ppermute | solution.py:43
  98.8 13.7 %collective-permute-start.24 = (bf16[64,768]{1,0:T(8,128)(2,1)}, bf16[64,768]{1,0:T(8,128)(2,1)S(1)}, u32[]{:S(2)}, u32[]{:S(2)}) collective-permute-start(bf16[64,768]{1,0:T(8,128)(2,1)} %get-tuple-element.68), channel_id=1, source_target_pairs={{0,4},{2,6},{4,0},{6,2},{1,5},{3,7},{5,1},{7,3},{8,12},{10,14},{12... | collective-permute-start | bytes 294920 | tf_op jit(solution)/shard_map/ppermute | solution.py:43
  105.7 8.5 %collective-permute-start.25 = (bf16[64,768]{1,0:T(8,128)(2,1)}, bf16[64,768]{1,0:T(8,128)(2,1)S(1)}, u32[]{:S(2)}, u32[]{:S(2)}) collective-permute-start(bf16[64,768]{1,0:T(8,128)(2,1)} %get-tuple-element.69), channel_id=1, source_target_pairs={{0,6},{2,4},{4,2},{6,0},{1,7},{3,5},{5,3},{7,1},{8,14},{10,12},{12... | collective-permute-start | bytes 294920 | tf_op jit(solution)/shard_map/ppermute | solution.py:43
  109.8 7.4 %copy-start.15 = (f32[768]{0:T(1024)S(1)}, f32[768]{0:T(1024)}, u32[]{:S(2)}) copy-start(f32[768]{0:T(1024)} %param.22) | copy-start | bytes 9220
  109.8 7.4 %copy-start.16 = (f32[768]{0:T(1024)S(1)}, f32[768]{0:T(1024)}, u32[]{:S(2)}) copy-start(f32[768]{0:T(1024)} %param.28) | copy-start | bytes 9220
  109.8 7.4 %collective-permute-start.30 = (bf16[48,768]{1,0:T(8,128)(2,1)}, bf16[48,768]{1,0:T(8,128)(2,1)S(1)}, u32[]{:S(2)}, u32[]{:S(2)}) collective-permute-start(bf16[48,768]{1,0:T(8,128)(2,1)} %get-tuple-element.76), channel_id=1, source_target_pairs={{0,2},{2,0},{4,6},{6,4},{1,3},{3,1},{5,7},{7,5},{8,10},{10,8},{12,... | collective-permute-start | bytes 221192 | tf_op jit(solution)/shard_map/ppermute | solution.py:43
  109.9 4.4 %copy-start.5 = (bf16[64,768]{1,0:T(8,128)(2,1)}, bf16[64,768]{1,0:T(8,128)(2,1)S(1)}, u32[]{:S(2)}) copy-start(bf16[64,768]{1,0:T(8,128)(2,1)S(1)} %collective-permute-done.23.refs_1_) | copy-start | bytes 294916
  109.9 7.3 %collective-permute-start.31 = (bf16[48,768]{1,0:T(8,128)(2,1)}, bf16[48,768]{1,0:T(8,128)(2,1)S(1)}, u32[]{:S(2)}, u32[]{:S(2)}) collective-permute-start(bf16[48,768]{1,0:T(8,128)(2,1)} %get-tuple-element.77), channel_id=1, source_target_pairs={{0,4},{2,6},{4,0},{6,2},{1,5},{3,7},{5,1},{7,3},{8,12},{10,14},{12... | collective-permute-start | bytes 221192 | tf_op jit(solution)/shard_map/ppermute | solution.py:43
  112.6 1.7 %copy-start.6 = (bf16[64,768]{1,0:T(8,128)(2,1)}, bf16[64,768]{1,0:T(8,128)(2,1)S(1)}, u32[]{:S(2)}) copy-start(bf16[64,768]{1,0:T(8,128)(2,1)S(1)} %collective-permute-done.24.refs_2_) | copy-start | bytes 294916
  112.6 6.4 %collective-permute-start.32 = (bf16[48,768]{1,0:T(8,128)(2,1)}, bf16[48,768]{1,0:T(8,128)(2,1)S(1)}, u32[]{:S(2)}, u32[]{:S(2)}) collective-permute-start(bf16[48,768]{1,0:T(8,128)(2,1)} %get-tuple-element.78), channel_id=1, source_target_pairs={{0,6},{2,4},{4,2},{6,0},{1,7},{3,5},{5,3},{7,1},{8,14},{10,12},{12... | collective-permute-start | bytes 221192 | tf_op jit(solution)/shard_map/ppermute | solution.py:43
  116.9 4.5 %copy-start.14 = (f32[24,128]{1,0:T(8,128)S(1)}, f32[24,128]{1,0:T(8,128)}, u32[]{:S(2)}) copy-start(f32[24,128]{1,0:T(8,128)} %get-tuple-element.70) | copy-start | bytes 36868
  116.9 4.5 %collective-permute-start.26 = (f32[24,128]{1,0:T(8,128)}, f32[24,128]{1,0:T(8,128)S(1)}, u32[]{:S(2)}, u32[]{:S(2)}) collective-permute-start(f32[24,128]{1,0:T(8,128)} %get-tuple-element.70), channel_id=1, source_target_pairs={{0,1},{1,0},{2,3},{3,2},{4,5},{5,4},{6,7},{7,6},{8,9},{9,8},{10,11... | collective-permute-start | bytes 36872 | tf_op jit(solution)/shard_map/ppermute | solution.py:43
  117.1 11.9 %collective-permute-start.17 = (bf16[2,1,1,64,768]{4,3,2,1,0:T(8,128)(2,1)S(1)}, bf16[2,1,1,64,768]{4,3,2,1,0:T(8,128)(2,1)S(1)}, u32[]{:S(2)}, u32[]{:S(2)}) collective-permute-start(bf16[2,1,1,64,768]{4,3,2,1,0:T(8,128)(2,1)S(1)} %split.27), channel_id=1, source_target_pairs={{0,4},{2,6},{4,0},{6,2},{1,5},{3,7},{5,1},{7,3},{8,12},{10,14},{12... | collective-permute-start | bytes 589832 | tf_op jit(solution)/shard_map/ppermute | solution.py:43
  129.4 3.2 %copy-start.17 = (f32[6,128]{1,0:T(8,128)S(1)}, f32[6,128]{1,0:T(8,128)}, u32[]{:S(2)}) copy-start(f32[6,128]{1,0:T(8,128)} %get-tuple-element.82) | copy-start | bytes 9220
  129.6 1.4 %collective-permute-start.18 = (bf16[1,64,768]{2,1,0:T(8,128)(2,1)S(1)}, bf16[1,64,768]{2,1,0:T(8,128)(2,1)S(1)}, u32[]{:S(2)}, u32[]{:S(2)}) collective-permute-start(bf16[1,64,768]{2,1,0:T(8,128)(2,1)S(1)} %get-tuple-element.93), channel_id=1, source_target_pairs={{0,1},{1,0},{2,3},{3,2},{4,5},{5,4},{6,7},{7,6},{8,9},{9,8},{10,11... | collective-permute-start | bytes 294920 | tf_op jit(solution)/shard_map/ppermute | solution.py:43
  130.3 1.5 %collective-permute-start.19 = (f32[1,64,768]{2,1,0:T(8,128)S(1)}, f32[1,64,768]{2,1,0:T(8,128)S(1)}, u32[]{:S(2)}, u32[]{:S(2)}) collective-permute-start(f32[1,64,768]{2,1,0:T(8,128)S(1)} %get-tuple-element.92), channel_id=1, source_target_pairs={{0,1},{1,0},{2,3},{3,2},{4,5},{5,4},{6,7},{7,6},{8,9},{9,8},{10,11... | collective-permute-start | bytes 589832 | tf_op jit(solution)/shard_map/ppermute | solution.py:43
  (11 other events, 11.1 us)

commit v3 on v2

--- a/solution.py
+++ b/solution.py
@@ -101,6 +101,7 @@
 VMEM_LIMIT = 60 * 1024 * 1024
 LANES = 128
 SUBLANES = 16
+SCORES_AT_ONCE = 512 * 1024
 
 
 def local_kernel(body, out_shapes, scratch=(), flops=0, moved=0):
@@ -227,6 +228,7 @@
     branch, norm_out, sums, bias_out = outs[:4]
     grad_outs = outs[4 : 4 + fsdp_count]
     weight, grads, mixed, total = outs[4 + fsdp_count :]
+    size = pos_col.shape[0]
     cols = weight.shape[1]
     features = own_heads * HD
     qkv_cols = 3 * features
@@ -270,30 +272,40 @@
         keep = lax.div(ctx_at, head_groups * seqs) == 0
     grads[...] = jnp.zeros(grads.shape, jnp.float32)
     mixed[...] = jnp.zeros(mixed.shape, jnp.bfloat16)
-    for head in range(own_heads):
-        at = head * 3 * HD
-        query = turned[:, at : at + HD]
-        key = turned[:, at + HD : at + 2 * HD]
-        value = turned[:, at + 2 * HD : at + 3 * HD]
-        spot = qkv_cols - low_cols + head * HD
-        low = ctx_low[:, spot : spot + HD]
-        scores = jnp.where(allowed, dot_last(query, key) * scale, NEGATIVE)
-        peak = jnp.max(scores, axis=-1, keepdims=True)
-        weights = jnp.where(allowed, jnp.exp(scores - peak), 0.0)
-        probs = weights / jnp.sum(weights, axis=-1, keepdims=True)
-        probs_low = probs.astype(jnp.bfloat16)
-        attended = dot(probs_low, value)
-        delta = jnp.sum(low.astype(jnp.float32) * attended, axis=-1, keepdims=True)
-        score_grad = probs * (dot_last(low, value) - delta)
+    together = own_heads if own_heads * size * size <= SCORES_AT_ONCE else 1
+    for base in range(0, own_heads, together):
+        group = range(base, min(base + together, own_heads))
+        heads = range(len(group))
+        starts = [head * 3 * HD for head in group]
+        spots = [qkv_cols - low_cols + head * HD for head in group]
+        queries = [turned[:, at : at + HD] for at in starts]
+        keys = [turned[:, at + HD : at + 2 * HD] for at in starts]
+        values = [turned[:, at + 2 * HD : at + 3 * HD] for at in starts]
+        lows = [ctx_low[:, spot : spot + HD] for spot in spots]
+        scores = [
+            jnp.where(allowed, dot_last(queries[h], keys[h]) * scale, NEGATIVE) for h in heads
+        ]
+        weight_grads = [dot_last(lows[h], values[h]) for h in heads]
+        peaks = [jnp.max(scores[h], axis=-1, keepdims=True) for h in heads]
+        weights = [jnp.where(allowed, jnp.exp(scores[h] - peaks[h]), 0.0) for h in heads]
+        probs = [weights[h] / jnp.sum(weights[h], axis=-1, keepdims=True) for h in heads]
+        probs_low = [probs[h].astype(jnp.bfloat16) for h in heads]
+        attended = [dot(probs_low[h], values[h]) for h in heads]
+        deltas = [
+            jnp.sum(lows[h].astype(jnp.float32) * attended[h], axis=-1, keepdims=True) for h in heads
+        ]
+        score_grads = [probs[h] * (weight_grads[h] - deltas[h]) for h in heads]
         if copies > 1:
-            score_grad = jnp.where(keep, score_grad, 0.0)
-            probs_low = jnp.where(keep, probs_low, jnp.zeros_like(probs_low))
-            attended = jnp.where(keep, attended, 0.0)
-        score_low = score_grad.astype(jnp.bfloat16)
-        grads[:, at : at + HD] = dot(score_low, key) * scale
-        grads[:, at + HD : at + 2 * HD] = dot_first(score_low, query) * scale
-        grads[:, at + 2 * HD : at + 3 * HD] = dot_first(probs_low, low)
-        mixed[:, spot : spot + HD] = attended.astype(jnp.bfloat16)
+            score_grads = [jnp.where(keep, part, 0.0) for part in score_grads]
+            probs_low = [jnp.where(keep, part, jnp.zeros_like(part)) for part in probs_low]
+            attended = [jnp.where(keep, part, 0.0) for part in attended]
+        score_low = [part.astype(jnp.bfloat16) for part in score_grads]
+        for h in heads:
+            at, spot = starts[h], spots[h]
+            grads[:, at : at + HD] = dot(score_low[h], keys[h]) * scale
+            grads[:, at + HD : at + 2 * HD] = dot_first(score_low[h], queries[h]) * scale
+            grads[:, at + 2 * HD : at + 3 * HD] = dot_first(probs_low[h], lows[h])
+            mixed[:, spot : spot + HD] = attended[h].astype(jnp.bfloat16)
     proj_grad = turn(grads[...], -sin_all)
     proj_low = proj_grad.astype(jnp.bfloat16)
     total[:, :high_cols] = dot_first(attn_in, proj_low)
@@ -415,7 +427,7 @@
 
 def late_end_kernel(count, groups, ff, padded, qkv_cols, cols, *refs):
     parts, outs = refs[:count], refs[count:]
-    up_out, down_out, gains_out, columns_out, qkv_bias_out, up_bias_out = outs
+    up_out, down_out, gains_out, columns_out, columns_again, qkv_bias_out, up_bias_out = outs
     rows, width = up_out.shape[0], LANES * columns_out.shape[0]
     both_cols = 2 * padded
     ctx_at = lax.axis_index("ctx")
@@ -433,7 +445,9 @@
     step = width // both_cols
     gains = jnp.concatenate([unfolded(summed, i * step, width) for i in range(4)], axis=1)
     put_row(gains_out, gains)
-    put_row(columns_out, unfolded(summed, 4 * step, width))
+    columns = unfolded(summed, 4 * step, width)
+    put_row(columns_out, columns)
+    put_row(columns_again, columns)
     sums = [tree_sum(vectors[g::groups]) for g in range(groups)]
     sums = [unfolded(block, 5 * step, cols)[:, :qkv_cols] for block in sums]
     put_row(
@@ -442,6 +456,14 @@
     last = 5 * step + cols // both_cols
     ups = [block[last : last + 1, :ff] for block in vectors]
     put_row(up_bias_out, jnp.concatenate(swapped(ups, ctx_at), axis=1))
+
+
+def gains_end_kernel(count, *refs):
+    parts, outs = refs[:count], refs[count : count + 4]
+    total = tree_sum([part[...] for part in parts])
+    rows = total.shape[0] // 4
+    for i, out in enumerate(outs):
+        out[...] = total[i * rows : (i + 1) * rows]
 
 
 def on_device(
@@ -618,7 +640,7 @@
         functools.partial(early_end_kernel, ctx_count, head_groups, qkv_cols, features),
         [shaped(qkv_weight.shape, f32), shaped(dense_weight.shape[::-1], f32)],
     )(*early_pieces)
-    up_weight_grad, down_weight_grad, gains, column_grad, qkv_bias_grad, up_bias_grad = (
+    up_weight_grad, down_weight_grad, gains, column_grad, column_again, qkv_bias_grad, up_bias_grad = (
         local_kernel(
             functools.partial(
                 late_end_kernel, ctx_count, head_groups, ff, padded, qkv_cols, cols
@@ -628,13 +650,19 @@
                 shaped(down_weight.shape[::-1], f32),
                 shaped((4 * width // LANES, LANES), f32),
                 shaped((width // LANES, LANES), f32),
+                shaped((width // LANES, LANES), f32),
                 shaped((3 * HD * heads // LANES, LANES), f32),
                 shaped((hidden_all // LANES, LANES), f32),
             ],
         )(*late_pieces)
     )
-    gains = sum(spread(gains, "tp")).reshape(4, width)
-    column_grad = column_grad.reshape(width)
+    gains = [
+        part.reshape(width)
+        for part in local_kernel(
+            functools.partial(gains_end_kernel, tp_count),
+            [shaped((width // LANES, LANES), f32)] * 4,
+        )(*spread(gains, "tp"))
+    ]
     return (
         block_out,
         tokens_grad,
@@ -643,13 +671,13 @@
         qkv_weight_grad,
         qkv_bias_grad.reshape(3 * HD * heads),
         dense_weight_grad.T,
-        column_grad,
+        column_grad.reshape(width),
         gains[2],
         gains[3],
         up_weight_grad,
         up_bias_grad.reshape(hidden_all),
         down_weight_grad.T,
-        column_grad,
+        column_again.reshape(width),
     )
 
 

time: 134 us -> 131 us (0.978)
  waiting for transfers between devices: 50.1 us -> 47.3 us
    ppermute x33, waiting for transfers between devices: 50.1 us -> 47.3 us  [swap(): lax.ppermute(value, axis, [(i, i ^ bit) for i in range(lax.axis_size(axis...]
    unnamed x59 -> x68, local copies, waits for them, and re-layouts: 5.36 us -> 6.13 us
  transfers between devices with their start and end apart: 33 -> 33, of which waited for: 13 -> 12; matrix products, arithmetic and copies ran while one was open for 8% -> 7% of each run, Pallas kernels for 14% -> 15%
where the time goes in v3:
time: 131 us
  waiting for transfers between devices  47.3 us (36%)
  starting transfers between devices  37.6 us (29%)
  Pallas kernels  28.2 us (22%)
  other arithmetic  9.73 us (7%)
  local copies, waits for them, and re-layouts  7.07 us (5%)
    ppermute x33, waiting for transfers between devices, swap(): lax.ppermute(value, axis, [(i, i ^ bit) for i in range(lax.axis_size(axis...  47.3 us
    ppermute x33, starting transfers between devices, swap(): lax.ppermute(value, axis, [(i, i ^ bit) for i in range(lax.axis_size(axis...  37.6 us
    pallas_call x1, Pallas kernels, on_device(): local_kernel(functools.partial(attention_kernel, fsdp_count, tp_count, ne...  7.76 us
    pallas_call x1, Pallas kernels, on_device(): local_kernel(functools.partial(mlp_kernel, fsdp_count, tp_count, near, he...  7.38 us
    unnamed x68, local copies, waits for them, and re-layouts  6.13 us
    pallas_call x2, Pallas kernels, scatter_weights(): local_kernel(functools.partial(sum_blocks_kernel, fsdp_count, ctx_count,...  4.46 us
  transfers between devices with their start and end apart: 33, of which 12 were waited for; matrix products, arithmetic and copies ran while one was open for 7% of the time, Pallas kernels for 15%

profile of v3, /device:TPU:0, one launch (start us, length us, event | category | flops | bytes accessed | tf_op | source)
XLA Modules:
  0.0 130.9 jit_solution(15834997871745061134)
XLA Ops:
  0.7 1.7 %shard_map.255 = (bf16[48,768]{1,0:T(8,128)(2,1)}, bf16[48,768]{1,0:T(8,128)(2,1)}) custom-call(bf16[48,1152]{1,0:T(8,128)(2,1)} %qkv_ref.1, bf16[48,384]{1,0:T(8,128)(2,1)} %bitcast.52), custom_call_target="tpu_custom_call" | custom-call | tf_op jit(solution)/shard_map/pallas_call | solution.py:507
  2.4 3.1 %collective-permute-start.9 = (bf16[48,768]{1,0:T(8,128)(2,1)}, bf16[48,768]{1,0:T(8,128)(2,1)S(1)}, u32[]{:S(2)}, u32[]{:S(2)}) collective-permute-start(bf16[48,768]{1,0:T(8,128)(2,1)} %get-tuple-element.60), channel_id=1, source_target_pairs={{0,2},{2,0},{4,6},{6,4},{1,3},{3,1},{5,7},{7,5},{8,10},{10,8},{12,... | collective-permute-start | bytes 221192 | tf_op jit(solution)/shard_map/ppermute | solution.py:43
  5.4 2.5 %collective-permute-start.11 = (bf16[48,768]{1,0:T(8,128)(2,1)}, bf16[48,768]{1,0:T(8,128)(2,1)S(1)}, u32[]{:S(2)}, u32[]{:S(2)}) collective-permute-start(bf16[48,768]{1,0:T(8,128)(2,1)} %get-tuple-element.60), channel_id=1, source_target_pairs={{0,6},{2,4},{4,2},{6,0},{1,7},{3,5},{5,3},{7,1},{8,14},{10,12},{12... | collective-permute-start | bytes 221192 | tf_op jit(solution)/shard_map/ppermute | solution.py:43
  7.9 1.1 convert_reduce_fusion
  9.0 1.1 convert_bitcast_fusion
  10.2 2.8 %collective-permute-start.10 = (bf16[48,768]{1,0:T(8,128)(2,1)}, bf16[48,768]{1,0:T(8,128)(2,1)S(1)}, u32[]{:S(2)}, u32[]{:S(2)}) collective-permute-start(bf16[48,768]{1,0:T(8,128)(2,1)} %get-tuple-element.59), channel_id=1, source_target_pairs={{0,4},{2,6},{4,0},{6,2},{1,5},{3,7},{5,1},{7,3},{8,12},{10,14},{12... | collective-permute-start | bytes 221192 | tf_op jit(solution)/shard_map/ppermute | solution.py:43
  13.0 1.7 %shard_map.254 = (bf16[48,768]{1,0:T(8,128)(2,1)}, bf16[48,768]{1,0:T(8,128)(2,1)}, bf16[48,768]{1,0:T(8,128)(2,1)}, bf16[48,768]{1,0:T(8,128)(2,1)}) custom-call(bf16[48,1536]{1,0:T(8,128)(2,1)} %up_ref.1, bf16[48,1536]{1,0:T(8,128)(2,1)} %bitcast.51), custom_call_target="tpu_custom_call" | custom-call | tf_op jit(solution)/shard_map/pallas_call | solution.py:511
  16.4 0.9 constant_dynamic-update-slice_fusion.7
  17.3 5.8 %collective-permute-done = bf16[2,1,1,64,768]{4,3,0,2,1:T(8,128)(2,1)S(1)} collective-permute-done((bf16[2,1,1,64,768]{4,3,0,2,1:T(8,128)(2,1)S(1)}, bf16[2,1,1,64,768]{4,3,0,2,1:T(8,128)(2,1)S(1)}, u32[]{:S(2)}, u32[]{:S(2)}) %collective-permute-start) | collective-permute-done | bytes 196640 | tf_op jit(solution)/shard_map/ppermute | solution.py:43
  23.3 0.8 copy.45.refs_11_
  24.7 1.2 fusion.11
  26.0 7.9 %collective-permute-done.1 = bf16[2,1,2,64,768]{4,3,0,2,1:T(8,128)(2,1)S(1)} collective-permute-done((bf16[2,1,2,64,768]{4,3,0,2,1:T(8,128)(2,1)S(1)}, bf16[2,1,2,64,768]{4,3,0,2,1:T(8,128)(2,1)S(1)}, u32[]{:S(2)}, u32[]{:S(2)}) %collective-permute-start.1) | collective-permute-done | bytes 393248 | tf_op jit(solution)/shard_map/ppermute | solution.py:43
  34.8 2.1 %collective-permute-start.5 = (bf16[48,768]{1,0:T(8,128)(2,1)S(1)}, bf16[48,768]{1,0:T(8,128)(2,1)S(1)}, u32[]{:S(2)}, u32[]{:S(2)}) collective-permute-start(bf16[48,768]{1,0:T(8,128)(2,1)S(1)} %copy-done.29), channel_id=1, source_target_pairs={{0,6},{2,4},{4,2},{6,0},{1,7},{3,5},{5,3},{7,1},{8,14},{10,12},{12... | collective-permute-start | bytes 221192 | tf_op jit(solution)/shard_map/ppermute | solution.py:43
  36.9 1.6 %collective-permute-start.12 = (bf16[192,768]{1,0:T(8,128)(2,1)S(1)}, bf16[192,768]{1,0:T(8,128)(2,1)S(1)}, u32[]{:S(2)}, u32[]{:S(2)}) collective-permute-start(bf16[192,768]{1,0:T(8,128)(2,1)S(1)} %constant_dynamic-update-slice_fusion.4.refs_2_), channel_id=1, source_target_pairs={{0,8},{8,0},{16,24},{24,16},{1,9},{9,1},{17,25},{25,17},{2,10},{10... | collective-permute-start | bytes 884744 | tf_op jit(solution)/shard_map/ppermute | solution.py:43
  38.5 1.5 %collective-permute-start.13 = (bf16[192,768]{1,0:T(8,128)(2,1)S(1)}, bf16[192,768]{1,0:T(8,128)(2,1)S(1)}, u32[]{:S(2)}, u32[]{:S(2)}) collective-permute-start(bf16[192,768]{1,0:T(8,128)(2,1)S(1)} %constant_dynamic-update-slice_fusion.4.refs_2_), channel_id=1, source_target_pairs={{0,16},{8,24},{16,0},{24,8},{1,17},{9,25},{17,1},{25,9},{2,18},{10... | collective-permute-start | bytes 884744 | tf_op jit(solution)/shard_map/ppermute | solution.py:43
  40.0 1.9 %collective-permute-done.4 = bf16[48,768]{1,0:T(8,128)(2,1)S(1)} collective-permute-done((bf16[48,768]{1,0:T(8,128)(2,1)S(1)}, bf16[48,768]{1,0:T(8,128)(2,1)S(1)}, u32[]{:S(2)}, u32[]{:S(2)}) %collective-permute-start.4) | collective-permute-done | bytes 73760 | tf_op jit(solution)/shard_map/ppermute | solution.py:43
  41.9 2.4 %collective-permute-start.14 = (bf16[192,768]{1,0:T(8,128)(2,1)S(1)}, bf16[192,768]{1,0:T(8,128)(2,1)S(1)}, u32[]{:S(2)}, u32[]{:S(2)}) collective-permute-start(bf16[192,768]{1,0:T(8,128)(2,1)S(1)} %constant_dynamic-update-slice_fusion.4.refs_2_), channel_id=1, source_target_pairs={{0,24},{8,16},{16,8},{24,0},{1,25},{9,17},{17,9},{25,1},{2,26},{10... | collective-permute-start | bytes 884744 | tf_op jit(solution)/shard_map/ppermute | solution.py:43
  45.0 1.9 %collective-permute-done.12.refs_3_ = bf16[192,768]{1,0:T(8,128)(2,1)S(1)} collective-permute-done((bf16[192,768]{1,0:T(8,128)(2,1)S(1)}, bf16[192,768]{1,0:T(8,128)(2,1)S(1)}, u32[]{:S(2)}, u32[]{:S(2)}) %collective-permute-start.12) | collective-permute-done | bytes 294944 | tf_op jit(solution)/shard_map/ppermute | solution.py:43
  46.9 1.5 %collective-permute-start.7 = (bf16[192,768]{1,0:T(8,128)(2,1)S(1)}, bf16[192,768]{1,0:T(8,128)(2,1)}, u32[]{:S(2)}, u32[]{:S(2)}) collective-permute-start(bf16[192,768]{1,0:T(8,128)(2,1)S(1)} %constant_dynamic-update-slice_fusion.refs_2_), channel_id=1, source_target_pairs={{0,16},{8,24},{16,0},{24,8},{1,17},{9,25},{17,1},{25,9},{2,18},{10... | collective-permute-start | bytes 884744 | tf_op jit(solution)/shard_map/ppermute | solution.py:43
  48.4 5.3 %collective-permute-done.13.refs_4_ = bf16[192,768]{1,0:T(8,128)(2,1)S(1)} collective-permute-done((bf16[192,768]{1,0:T(8,128)(2,1)S(1)}, bf16[192,768]{1,0:T(8,128)(2,1)S(1)}, u32[]{:S(2)}, u32[]{:S(2)}) %collective-permute-start.13) | collective-permute-done | bytes 294944 | tf_op jit(solution)/shard_map/ppermute | solution.py:43
  53.8 1.3 %collective-permute-start.8 = (bf16[192,768]{1,0:T(8,128)(2,1)S(1)}, bf16[192,768]{1,0:T(8,128)(2,1)}, u32[]{:S(2)}, u32[]{:S(2)}) collective-permute-start(bf16[192,768]{1,0:T(8,128)(2,1)S(1)} %constant_dynamic-update-slice_fusion.refs_2_), channel_id=1, source_target_pairs={{0,24},{8,16},{16,8},{24,0},{1,25},{9,17},{17,9},{25,1},{2,26},{10... | collective-permute-start | bytes 884744 | tf_op jit(solution)/shard_map/ppermute | solution.py:43
  56.5 0.9 copy-done.20
  57.3 7.8 %shard_map.256 = (f32[256,768]{1,0:T(8,128)}, f32[256,768]{1,0:T(8,128)}, f32[2,768]{1,0:T(2,128)}, f32[1,768]{1,0:T(1,128)}, f32[192,768]{1,0:T(8,128)}, /*inde...) custom-call(bf16[2,1,256,768]{3,2,1,0:T(8,128)(2,1)} %bitcast.49, ...), custom_call_target="tpu_custom_call" | custom-call | flops 2415919104 | bytes 3145728 | tf_op jit(solution)/shard_map/pallas_call | solution.py:555
  65.1 1.3 collective-permute-done.7.refs_4_
  66.4 7.4 %shard_map.257 = (f32[2,1,256,768]{3,2,1,0:T(8,128)}, f32[2,1,256,768]{3,2,1,0:T(8,128)}, f32[208,768]{1,0:T(8,128)}, bf16[208,768]{1,0:T(8,128)(2,1)}, bf16[208...) custom-call(bf16[2,1,256,768]{3,2,1,0:T(8,128)(2,1)} %bitcast.50, bf16[2,1,256,768]{3,2,1,0:T(8,128)(2,1)} %copy-done.20, ...), custom_call_target="tpu_custom_call" | custom-call | flops 1811939328 | bytes 6291456 | tf_op jit(solution)/shard_map/pallas_call | solution.py:589
  73.8 3.6 %collective-permute-done.15 = f32[2,1,256,768]{3,2,1,0:T(8,128)S(1)} collective-permute-done((f32[2,1,256,768]{3,2,1,0:T(8,128)}, f32[2,1,256,768]{3,2,1,0:T(8,128)S(1)}, u32[]{:S(2)}, u32[]{:S(2)}) %collective-permute-start.15) | collective-permute-done | bytes 1572896 | tf_op jit(solution)/shard_map/ppermute | solution.py:43
  77.4 1.7 %add.312 = f32[2,1,256,768]{3,2,1,0:T(8,128)S(1)} add(f32[2,1,256,768]{3,2,1,0:T(8,128)} %get-tuple-element.65, f32[2,1,256,768]{3,2,1,0:T(8,128)S(1)} %collective-permute-done.15) | non-fusion elementwise | flops 393216 | bytes 4718592 | tf_op jit(solution)/shard_map/add | solution.py:610
  79.2 0.9 collective-permute-start.16
  80.3 2.1 %collective-permute-start.20 = (bf16[208,768]{1,0:T(8,128)(2,1)S(1)}, bf16[208,768]{1,0:T(8,128)(2,1)S(1)}, u32[]{:S(2)}, u32[]{:S(2)}) collective-permute-start(bf16[208,768]{1,0:T(8,128)(2,1)S(1)} %copy-done.23), channel_id=1, source_target_pairs={{0,8},{8,0},{16,24},{24,16},{1,9},{9,1},{17,25},{25,17},{2,10},{10... | collective-permute-start | bytes 958472 | tf_op jit(solution)/shard_map/ppermute | solution.py:43
  82.5 1.5 %collective-permute-start.22 = (bf16[208,768]{1,0:T(8,128)(2,1)S(1)}, bf16[208,768]{1,0:T(8,128)(2,1)S(1)}, u32[]{:S(2)}, u32[]{:S(2)}) collective-permute-start(bf16[208,768]{1,0:T(8,128)(2,1)S(1)} %copy-done.21), channel_id=1, source_target_pairs={{0,24},{8,16},{16,8},{24,0},{1,25},{9,17},{17,9},{25,1},{2,26},{10... | collective-permute-start | bytes 958472 | tf_op jit(solution)/shard_map/ppermute | solution.py:43
  84.0 6.5 %collective-permute-done.16 = bf16[2,1,2,64,768]{4,3,2,1,0:T(8,128)(2,1)S(1)} collective-permute-done((bf16[2,1,2,64,768]{4,3,2,1,0:T(8,128)(2,1)S(1)}, bf16[2,1,2,64,768]{4,3,2,1,0:T(8,128)(2,1)S(1)}, u32[]{:S(2)}, u32[]{:S(2)}) %collective-permute-start.16) | collective-permute-done | bytes 393248 | tf_op jit(solution)/shard_map/ppermute | solution.py:43
  90.5 1.1 collective-permute-start.17
  91.7 2.0 %collective-permute-start.27 = (bf16[192,768]{1,0:T(8,128)(2,1)}, bf16[192,768]{1,0:T(8,128)(2,1)S(1)}, u32[]{:S(2)}, u32[]{:S(2)}) collective-permute-start(bf16[192,768]{1,0:T(8,128)(2,1)} %get-tuple-element.79), channel_id=1, source_target_pairs={{0,8},{8,0},{16,24},{24,16},{1,9},{9,1},{17,25},{25,17},{2,10},{10... | collective-permute-start | bytes 884744 | tf_op jit(solution)/shard_map/ppermute | solution.py:43
  93.8 5.2 %collective-permute-done.21.refs_2_ = bf16[208,768]{1,0:T(8,128)(2,1)S(1)} collective-permute-done((bf16[208,768]{1,0:T(8,128)(2,1)S(1)}, bf16[208,768]{1,0:T(8,128)(2,1)S(1)}, u32[]{:S(2)}, u32[]{:S(2)}) %collective-permute-start.21) | collective-permute-done | bytes 319520 | tf_op jit(solution)/shard_map/ppermute | solution.py:43
  99.8 2.3 %shard_map.258 = (f32[64,768]{1,0:T(8,128)}, bf16[64,768]{1,0:T(8,128)(2,1)}, bf16[64,768]{1,0:T(8,128)(2,1)}, bf16[64,768]{1,0:T(8,128)(2,1)}) custom-call(f32[208,768]{1,0:T(8,128)} %get-tuple-element.67.refs_0_, bf16[208,768]{1,0:T(8,128)(2,1)} %copy-done.2, bf16[208,768]{1,0:T(8,128)(2,1)} %copy-done.3, bf16[208,768]{1,0:T(8,128)(2,1)} %copy-done.4), custom_call_target="tpu_custom_call" | custom-call | tf_op jit(solution)/shard_map/pallas_call | solution.py:622
  102.0 1.2 collective-permute-start.23
  103.2 1.1 collective-permute-start.24
  104.7 2.2 %collective-permute-start.25 = (bf16[64,768]{1,0:T(8,128)(2,1)}, bf16[64,768]{1,0:T(8,128)(2,1)S(1)}, u32[]{:S(2)}, u32[]{:S(2)}) collective-permute-start(bf16[64,768]{1,0:T(8,128)(2,1)} %get-tuple-element.74), channel_id=1, source_target_pairs={{0,6},{2,4},{4,2},{6,0},{1,7},{3,5},{5,3},{7,1},{8,14},{10,12},{12... | collective-permute-start | bytes 294920 | tf_op jit(solution)/shard_map/ppermute | solution.py:43
  107.0 3.9 %collective-permute-done.28.refs_2_ = bf16[192,768]{1,0:T(8,128)(2,1)S(1)} collective-permute-done((bf16[192,768]{1,0:T(8,128)(2,1)}, bf16[192,768]{1,0:T(8,128)(2,1)S(1)}, u32[]{:S(2)}, u32[]{:S(2)}) %collective-permute-start.28) | collective-permute-done | bytes 294944 | tf_op jit(solution)/shard_map/ppermute | solution.py:43
  111.7 2.2 %shard_map.261 = (f32[48,768]{1,0:T(8,128)}, bf16[48,768]{1,0:T(8,128)(2,1)}, bf16[48,768]{1,0:T(8,128)(2,1)}, bf16[48,768]{1,0:T(8,128)(2,1)}) custom-call(f32[192,768]{1,0:T(8,128)} %get-tuple-element.78.refs_0_, bf16[192,768]{1,0:T(8,128)(2,1)} %copy-done.5, bf16[192,768]{1,0:T(8,128)(2,1)} %copy-done.6, bf16[192,768]{1,0:T(8,128)(2,1)} %copy-done.7), custom_call_target="tpu_custom_call" | custom-call | tf_op jit(solution)/shard_map/pallas_call | solution.py:622
  113.9 1.2 collective-permute-start.30
  115.1 1.1 collective-permute-start.31
  116.2 2.1 %collective-permute-start.32 = (bf16[48,768]{1,0:T(8,128)(2,1)}, bf16[48,768]{1,0:T(8,128)(2,1)S(1)}, u32[]{:S(2)}, u32[]{:S(2)}) collective-permute-start(bf16[48,768]{1,0:T(8,128)(2,1)} %get-tuple-element.85), channel_id=1, source_target_pairs={{0,6},{2,4},{4,2},{6,0},{1,7},{3,5},{5,3},{7,1},{8,14},{10,12},{12... | collective-permute-start | bytes 221192 | tf_op jit(solution)/shard_map/ppermute | solution.py:43
  119.0 2.0 %shard_map.259 = (f32[48,1536]{1,0:T(8,128)}, f32[48,1536]{1,0:T(8,128)}, f32[24,128]{1,0:T(8,128)}, f32[6,128]{1,0:T(8,128)}, f32[6,128]{1,0:T(8,128)}, /*index=5*/f32[9,128]{1,0:T(8,128)}, f32[12,128]{1,0:T(8,128)}) custom-call(f32[64,768]{1,0:T(8,128)} %get-tuple-element.71.refs_0_, bf16[64,768]{1,0:T(8,128)(2,1)} %copy-done.8, ...), custom_call_target="tpu_custom_call" | custom-call | tf_op jit(solution)/shard_map/pallas_call | solution.py:644
  121.0 3.3 %collective-permute-done.31.refs_2_ = bf16[48,768]{1,0:T(8,128)(2,1)S(1)} collective-permute-done((bf16[48,768]{1,0:T(8,128)(2,1)}, bf16[48,768]{1,0:T(8,128)(2,1)S(1)}, u32[]{:S(2)}, u32[]{:S(2)}) %collective-permute-start.31) | collective-permute-done | bytes 73760 | tf_op jit(solution)/shard_map/ppermute | solution.py:43
  124.9 1.8 %shard_map.262 = (f32[48,1152]{1,0:T(8,128)}, f32[48,384]{1,0:T(8,128)}) custom-call(f32[48,768]{1,0:T(8,128)} %get-tuple-element.82.refs_0_, bf16[48,768]{1,0:T(8,128)(2,1)} %copy-done.12, bf16[48,768]{1,0:T(8,128)(2,1)} %copy-done.13, bf16[48,768]{1,0:T(8,128)(2,1)} %copy-done.14), custom_call_target="tpu_custom_call" | custom-call | tf_op jit(solution)/shard_map/pallas_call | solution.py:639
  127.3 1.3 %shard_map.260 = (f32[6,128]{1,0:T(8,128)}, f32[6,128]{1,0:T(8,128)}, f32[6,128]{1,0:T(8,128)}, f32[6,128]{1,0:T(8,128)}) custom-call(f32[24,128]{1,0:T(8,128)} %get-tuple-element.75.refs_0_, f32[24,128]{1,0:T(8,128)} %copy-done.17), custom_call_target="tpu_custom_call" | custom-call | tf_op jit(solution)/shard_map/pallas_call | solution.py:661
  130.1 0.8 pad_maximum_fusion.2
  (135 shorter events, 11.4 us)
Async XLA Ops:
  0.6 23.5 %copy-start = (f32[2,64,768]{2,1,0:T(8,128)S(1)}, f32[2,64,768]{2,1,0:T(8,128)}, u32[]{:S(2)}) copy-start(f32[2,64,768]{2,1,0:T(8,128)} %param.29) | copy-start | bytes 1179652
  2.4 32.2 %collective-permute-start.9 = (bf16[48,768]{1,0:T(8,128)(2,1)}, bf16[48,768]{1,0:T(8,128)(2,1)S(1)}, u32[]{:S(2)}, u32[]{:S(2)}) collective-permute-start(bf16[48,768]{1,0:T(8,128)(2,1)} %get-tuple-element.60), channel_id=1, source_target_pairs={{0,2},{2,0},{4,6},{6,4},{1,3},{3,1},{5,7},{7,5},{8,10},{10,8},{12,... | collective-permute-start | bytes 221192 | tf_op jit(solution)/shard_map/ppermute | solution.py:43
  5.4 31.5 %collective-permute-start.11 = (bf16[48,768]{1,0:T(8,128)(2,1)}, bf16[48,768]{1,0:T(8,128)(2,1)S(1)}, u32[]{:S(2)}, u32[]{:S(2)}) collective-permute-start(bf16[48,768]{1,0:T(8,128)(2,1)} %get-tuple-element.60), channel_id=1, source_target_pairs={{0,6},{2,4},{4,2},{6,0},{1,7},{3,5},{5,3},{7,1},{8,14},{10,12},{12... | collective-permute-start | bytes 221192 | tf_op jit(solution)/shard_map/ppermute | solution.py:43
  10.0 13.0 %collective-permute-start = (bf16[2,1,1,64,768]{4,3,0,2,1:T(8,128)(2,1)S(1)}, bf16[2,1,1,64,768]{4,3,0,2,1:T(8,128)(2,1)S(1)}, u32[]{:S(2)}, u32[]{:S(2)}) collective-permute-start(bf16[2,1,1,64,768]{4,3,0,2,1:T(8,128)(2,1)S(1)} %maximum_bitcast_fusion), channel_id=1, source_target_pairs={{0,4},{2,6},{4,0},{6,2},{1,5},{3,7},{5,1},{7,3},{8,12},{10,14},{12... | collective-permute-start | bytes 589832 | tf_op jit(solution)/shard_map/ppermute | solution.py:43
  10.2 24.5 %collective-permute-start.10 = (bf16[48,768]{1,0:T(8,128)(2,1)}, bf16[48,768]{1,0:T(8,128)(2,1)S(1)}, u32[]{:S(2)}, u32[]{:S(2)}) collective-permute-start(bf16[48,768]{1,0:T(8,128)(2,1)} %get-tuple-element.59), channel_id=1, source_target_pairs={{0,4},{2,6},{4,0},{6,2},{1,5},{3,7},{5,1},{7,3},{8,12},{10,14},{12... | collective-permute-start | bytes 221192 | tf_op jit(solution)/shard_map/ppermute | solution.py:43
  14.8 10.0 %copy-start.11 = (bf16[48,768]{1,0:T(8,128)(2,1)S(1)}, bf16[48,768]{1,0:T(8,128)(2,1)}, u32[]{:S(2)}) copy-start(bf16[48,768]{1,0:T(8,128)(2,1)} %get-tuple-element.55) | copy-start | bytes 221188
  14.8 19.2 %copy-start.30 = (bf16[48,768]{1,0:T(8,128)(2,1)S(1)}, bf16[48,768]{1,0:T(8,128)(2,1)}, u32[]{:S(2)}) copy-start(bf16[48,768]{1,0:T(8,128)(2,1)} %get-tuple-element.57) | copy-start | bytes 221188
  14.8 23.7 %collective-permute-start.3 = (bf16[48,768]{1,0:T(8,128)(2,1)}, bf16[48,768]{1,0:T(8,128)(2,1)S(1)}, u32[]{:S(2)}, u32[]{:S(2)}) collective-permute-start(bf16[48,768]{1,0:T(8,128)(2,1)} %get-tuple-element.56), channel_id=1, source_target_pairs={{0,2},{2,0},{4,6},{6,4},{1,3},{3,1},{5,7},{7,5},{8,10},{10,8},{12,... | collective-permute-start | bytes 221192 | tf_op jit(solution)/shard_map/ppermute | solution.py:43
  23.1 10.8 %collective-permute-start.1 = (bf16[2,1,2,64,768]{4,3,0,2,1:T(8,128)(2,1)S(1)}, bf16[2,1,2,64,768]{4,3,0,2,1:T(8,128)(2,1)S(1)}, u32[]{:S(2)}, u32[]{:S(2)}) collective-permute-start(bf16[2,1,2,64,768]{4,3,0,2,1:T(8,128)(2,1)S(1)} %pad_maximum_fusion.1), channel_id=1, source_target_pairs={{0,2},{2,0},{4,6},{6,4},{1,3},{3,1},{5,7},{7,5},{8,10},{10,8},{12,... | collective-permute-start | bytes 1179656 | tf_op jit(solution)/shard_map/ppermute | solution.py:43
  33.9 8.0 %collective-permute-start.4 = (bf16[48,768]{1,0:T(8,128)(2,1)S(1)}, bf16[48,768]{1,0:T(8,128)(2,1)S(1)}, u32[]{:S(2)}, u32[]{:S(2)}) collective-permute-start(bf16[48,768]{1,0:T(8,128)(2,1)S(1)} %copy-done.30), channel_id=1, source_target_pairs={{0,4},{2,6},{4,0},{6,2},{1,5},{3,7},{5,1},{7,3},{8,12},{10,14},{12... | collective-permute-start | bytes 221192 | tf_op jit(solution)/shard_map/ppermute | solution.py:43
  34.6 21.9 %copy-start.1 = (bf16[2,1,4,64,768]{4,3,2,0,1:T(8,128)(2,1)}, bf16[2,1,4,64,768]{4,3,2,0,1:T(8,128)(2,1)S(1)}, u32[]{:S(2)}) copy-start(bf16[2,1,4,64,768]{4,3,2,0,1:T(8,128)(2,1)S(1)} %copy.44) | copy-start | bytes 2359300
  34.6 21.1 %collective-permute-start.2 = (bf16[2,1,256,768]{3,2,1,0:T(8,128)(2,1)S(1)}, bf16[2,1,256,768]{3,2,1,0:T(8,128)(2,1)S(1)}, u32[]{:S(2)}, u32[]{:S(2)}) collective-permute-start(bf16[2,1,256,768]{3,2,1,0:T(8,128)(2,1)S(1)} %bitcast.48), channel_id=1, source_target_pairs={{0,1},{1,0},{2,3},{3,2},{4,5},{5,4},{6,7},{7,6},{8,9},{9,8},{10,11... | collective-permute-start | bytes 2359304 | tf_op jit(solution)/shard_map/ppermute | solution.py:43
  34.8 9.6 %collective-permute-start.5 = (bf16[48,768]{1,0:T(8,128)(2,1)S(1)}, bf16[48,768]{1,0:T(8,128)(2,1)S(1)}, u32[]{:S(2)}, u32[]{:S(2)}) collective-permute-start(bf16[48,768]{1,0:T(8,128)(2,1)S(1)} %copy-done.29), channel_id=1, source_target_pairs={{0,6},{2,4},{4,2},{6,0},{1,7},{3,5},{5,3},{7,1},{8,14},{10,12},{12... | collective-permute-start | bytes 221192 | tf_op jit(solution)/shard_map/ppermute | solution.py:43
  36.9 19.5 %copy-start.16 = (bf16[192,768]{1,0:T(8,128)(2,1)}, bf16[192,768]{1,0:T(8,128)(2,1)S(1)}, u32[]{:S(2)}) copy-start(bf16[192,768]{1,0:T(8,128)(2,1)S(1)} %constant_dynamic-update-slice_fusion.4.refs_2_) | copy-start | bytes 884740
  36.9 9.9 %collective-permute-start.12 = (bf16[192,768]{1,0:T(8,128)(2,1)S(1)}, bf16[192,768]{1,0:T(8,128)(2,1)S(1)}, u32[]{:S(2)}, u32[]{:S(2)}) collective-permute-start(bf16[192,768]{1,0:T(8,128)(2,1)S(1)} %constant_dynamic-update-slice_fusion.4.refs_2_), channel_id=1, source_target_pairs={{0,8},{8,0},{16,24},{24,16},{1,9},{9,1},{17,25},{25,17},{2,10},{10... | collective-permute-start | bytes 884744 | tf_op jit(solution)/shard_map/ppermute | solution.py:43
  38.5 15.2 %collective-permute-start.13 = (bf16[192,768]{1,0:T(8,128)(2,1)S(1)}, bf16[192,768]{1,0:T(8,128)(2,1)S(1)}, u32[]{:S(2)}, u32[]{:S(2)}) collective-permute-start(bf16[192,768]{1,0:T(8,128)(2,1)S(1)} %constant_dynamic-update-slice_fusion.4.refs_2_), channel_id=1, source_target_pairs={{0,16},{8,24},{16,0},{24,8},{1,17},{9,25},{17,1},{25,9},{2,18},{10... | collective-permute-start | bytes 884744 | tf_op jit(solution)/shard_map/ppermute | solution.py:43
  41.9 13.8 %collective-permute-start.14 = (bf16[192,768]{1,0:T(8,128)(2,1)S(1)}, bf16[192,768]{1,0:T(8,128)(2,1)S(1)}, u32[]{:S(2)}, u32[]{:S(2)}) collective-permute-start(bf16[192,768]{1,0:T(8,128)(2,1)S(1)} %constant_dynamic-update-slice_fusion.4.refs_2_), channel_id=1, source_target_pairs={{0,24},{8,16},{16,8},{24,0},{1,25},{9,17},{17,9},{25,1},{2,26},{10... | collective-permute-start | bytes 884744 | tf_op jit(solution)/shard_map/ppermute | solution.py:43
  44.4 20.7 %copy-start.15 = (bf16[192,768]{1,0:T(8,128)(2,1)}, bf16[192,768]{1,0:T(8,128)(2,1)S(1)}, u32[]{:S(2)}) copy-start(bf16[192,768]{1,0:T(8,128)(2,1)S(1)} %constant_dynamic-update-slice_fusion.refs_2_) | copy-start | bytes 884740
  44.4 20.7 %collective-permute-start.6 = (bf16[192,768]{1,0:T(8,128)(2,1)S(1)}, bf16[192,768]{1,0:T(8,128)(2,1)S(1)}, u32[]{:S(2)}, u32[]{:S(2)}) collective-permute-start(bf16[192,768]{1,0:T(8,128)(2,1)S(1)} %constant_dynamic-update-slice_fusion.refs_2_), channel_id=1, source_target_pairs={{0,8},{8,0},{16,24},{24,16},{1,9},{9,1},{17,25},{25,17},{2,10},{10... | collective-permute-start | bytes 884744 | tf_op jit(solution)/shard_map/ppermute | solution.py:43
  46.9 9.6 %copy-start.25 = (bf16[192,768]{1,0:T(8,128)(2,1)}, bf16[192,768]{1,0:T(8,128)(2,1)S(1)}, u32[]{:S(2)}) copy-start(bf16[192,768]{1,0:T(8,128)(2,1)S(1)} %collective-permute-done.12.refs_3_) | copy-start | bytes 884740
  46.9 19.5 %collective-permute-start.7 = (bf16[192,768]{1,0:T(8,128)(2,1)S(1)}, bf16[192,768]{1,0:T(8,128)(2,1)}, u32[]{:S(2)}, u32[]{:S(2)}) collective-permute-start(bf16[192,768]{1,0:T(8,128)(2,1)S(1)} %constant_dynamic-update-slice_fusion.refs_2_), channel_id=1, source_target_pairs={{0,16},{8,24},{16,0},{24,8},{1,17},{9,25},{17,1},{25,9},{2,18},{10... | collective-permute-start | bytes 884744 | tf_op jit(solution)/shard_map/ppermute | solution.py:43
  53.8 12.7 %collective-permute-start.8 = (bf16[192,768]{1,0:T(8,128)(2,1)S(1)}, bf16[192,768]{1,0:T(8,128)(2,1)}, u32[]{:S(2)}, u32[]{:S(2)}) collective-permute-start(bf16[192,768]{1,0:T(8,128)(2,1)S(1)} %constant_dynamic-update-slice_fusion.refs_2_), channel_id=1, source_target_pairs={{0,24},{8,16},{16,8},{24,0},{1,25},{9,17},{17,9},{25,1},{2,26},{10... | collective-permute-start | bytes 884744 | tf_op jit(solution)/shard_map/ppermute | solution.py:43
  73.8 3.6 %collective-permute-start.15 = (f32[2,1,256,768]{3,2,1,0:T(8,128)}, f32[2,1,256,768]{3,2,1,0:T(8,128)S(1)}, u32[]{:S(2)}, u32[]{:S(2)}) collective-permute-start(f32[2,1,256,768]{3,2,1,0:T(8,128)} %get-tuple-element.66), channel_id=1, source_target_pairs={{0,1},{1,0},{2,3},{3,2},{4,5},{5,4},{6,7},{7,6},{8,9},{9,8},{10,11... | collective-permute-start | bytes 4718600 | tf_op jit(solution)/shard_map/ppermute | solution.py:43
  77.4 2.9 %copy-start.23 = (bf16[208,768]{1,0:T(8,128)(2,1)S(1)}, bf16[208,768]{1,0:T(8,128)(2,1)}, u32[]{:S(2)}) copy-start(bf16[208,768]{1,0:T(8,128)(2,1)} %get-tuple-element.68) | copy-start | bytes 958468
  77.4 5.0 %copy-start.22 = (bf16[208,768]{1,0:T(8,128)(2,1)S(1)}, bf16[208,768]{1,0:T(8,128)(2,1)}, u32[]{:S(2)}) copy-start(bf16[208,768]{1,0:T(8,128)(2,1)} %get-tuple-element.69) | copy-start | bytes 958468
  77.4 5.0 %copy-start.21 = (bf16[208,768]{1,0:T(8,128)(2,1)S(1)}, bf16[208,768]{1,0:T(8,128)(2,1)}, u32[]{:S(2)}) copy-start(bf16[208,768]{1,0:T(8,128)(2,1)} %get-tuple-element.70) | copy-start | bytes 958468
  79.1 19.8 %copy-start.24 = (bf16[192,768]{1,0:T(8,128)(2,1)S(1)}, bf16[192,768]{1,0:T(8,128)(2,1)}, u32[]{:S(2)}) copy-start(bf16[192,768]{1,0:T(8,128)(2,1)} %get-tuple-element.81) | copy-start | bytes 884740
  79.2 11.2 %collective-permute-start.16 = (bf16[2,1,2,64,768]{4,3,2,1,0:T(8,128)(2,1)S(1)}, bf16[2,1,2,64,768]{4,3,2,1,0:T(8,128)(2,1)S(1)}, u32[]{:S(2)}, u32[]{:S(2)}) collective-permute-start(bf16[2,1,2,64,768]{4,3,2,1,0:T(8,128)(2,1)S(1)} %split.26), channel_id=1, source_target_pairs={{0,2},{2,0},{4,6},{6,4},{1,3},{3,1},{5,7},{7,5},{8,10},{10,8},{12,... | collective-permute-start | bytes 1179656 | tf_op jit(solution)/shard_map/ppermute | solution.py:43
  80.3 13.4 %collective-permute-start.20 = (bf16[208,768]{1,0:T(8,128)(2,1)S(1)}, bf16[208,768]{1,0:T(8,128)(2,1)S(1)}, u32[]{:S(2)}, u32[]{:S(2)}) collective-permute-start(bf16[208,768]{1,0:T(8,128)(2,1)S(1)} %copy-done.23), channel_id=1, source_target_pairs={{0,8},{8,0},{16,24},{24,16},{1,9},{9,1},{17,25},{25,17},{2,10},{10... | collective-permute-start | bytes 958472 | tf_op jit(solution)/shard_map/ppermute | solution.py:43
  82.4 16.5 %collective-permute-start.21 = (bf16[208,768]{1,0:T(8,128)(2,1)S(1)}, bf16[208,768]{1,0:T(8,128)(2,1)S(1)}, u32[]{:S(2)}, u32[]{:S(2)}) collective-permute-start(bf16[208,768]{1,0:T(8,128)(2,1)S(1)} %copy-done.22), channel_id=1, source_target_pairs={{0,16},{8,24},{16,0},{24,8},{1,17},{9,25},{17,1},{25,9},{2,18},{10... | collective-permute-start | bytes 958472 | tf_op jit(solution)/shard_map/ppermute | solution.py:43
  82.5 16.5 %collective-permute-start.22 = (bf16[208,768]{1,0:T(8,128)(2,1)S(1)}, bf16[208,768]{1,0:T(8,128)(2,1)S(1)}, u32[]{:S(2)}, u32[]{:S(2)}) collective-permute-start(bf16[208,768]{1,0:T(8,128)(2,1)S(1)} %copy-done.21), channel_id=1, source_target_pairs={{0,24},{8,16},{16,8},{24,0},{1,25},{9,17},{17,9},{25,1},{2,26},{10... | collective-permute-start | bytes 958472 | tf_op jit(solution)/shard_map/ppermute | solution.py:43
  90.5 12.7 %collective-permute-start.17 = (bf16[2,1,1,64,768]{4,3,2,1,0:T(8,128)(2,1)S(1)}, bf16[2,1,1,64,768]{4,3,2,1,0:T(8,128)(2,1)S(1)}, u32[]{:S(2)}, u32[]{:S(2)}) collective-permute-start(bf16[2,1,1,64,768]{4,3,2,1,0:T(8,128)(2,1)S(1)} %split.27), channel_id=1, source_target_pairs={{0,4},{2,6},{4,0},{6,2},{1,5},{3,7},{5,1},{7,3},{8,12},{10,14},{12... | collective-permute-start | bytes 589832 | tf_op jit(solution)/shard_map/ppermute | solution.py:43
  91.7 13.0 %collective-permute-start.27 = (bf16[192,768]{1,0:T(8,128)(2,1)}, bf16[192,768]{1,0:T(8,128)(2,1)S(1)}, u32[]{:S(2)}, u32[]{:S(2)}) collective-permute-start(bf16[192,768]{1,0:T(8,128)(2,1)} %get-tuple-element.79), channel_id=1, source_target_pairs={{0,8},{8,0},{16,24},{24,16},{1,9},{9,1},{17,25},{25,17},{2,10},{10... | collective-permute-start | bytes 884744 | tf_op jit(solution)/shard_map/ppermute | solution.py:43
  93.7 5.3 %copy-start.2 = (bf16[208,768]{1,0:T(8,128)(2,1)}, bf16[208,768]{1,0:T(8,128)(2,1)S(1)}, u32[]{:S(2)}) copy-start(bf16[208,768]{1,0:T(8,128)(2,1)S(1)} %collective-permute-done.20.refs_1_) | copy-start | bytes 958468
  93.7 17.2 %collective-permute-start.28 = (bf16[192,768]{1,0:T(8,128)(2,1)}, bf16[192,768]{1,0:T(8,128)(2,1)S(1)}, u32[]{:S(2)}, u32[]{:S(2)}) collective-permute-start(bf16[192,768]{1,0:T(8,128)(2,1)} %get-tuple-element.80), channel_id=1, source_target_pairs={{0,16},{8,24},{16,0},{24,8},{1,17},{9,25},{17,1},{25,9},{2,18},{10... | collective-permute-start | bytes 884744 | tf_op jit(solution)/shard_map/ppermute | solution.py:43
  98.9 12.0 %collective-permute-start.29 = (bf16[192,768]{1,0:T(8,128)(2,1)S(1)}, bf16[192,768]{1,0:T(8,128)(2,1)S(1)}, u32[]{:S(2)}, u32[]{:S(2)}) collective-permute-start(bf16[192,768]{1,0:T(8,128)(2,1)S(1)} %copy-done.24), channel_id=1, source_target_pairs={{0,24},{8,16},{16,8},{24,0},{1,25},{9,17},{17,9},{25,1},{2,26},{10... | collective-permute-start | bytes 884744 | tf_op jit(solution)/shard_map/ppermute | solution.py:43
  102.0 13.0 %collective-permute-start.23 = (bf16[64,768]{1,0:T(8,128)(2,1)}, bf16[64,768]{1,0:T(8,128)(2,1)S(1)}, u32[]{:S(2)}, u32[]{:S(2)}) collective-permute-start(bf16[64,768]{1,0:T(8,128)(2,1)} %get-tuple-element.72), channel_id=1, source_target_pairs={{0,2},{2,0},{4,6},{6,4},{1,3},{3,1},{5,7},{7,5},{8,10},{10,8},{12,... | collective-permute-start | bytes 294920 | tf_op jit(solution)/shard_map/ppermute | solution.py:43
  103.2 12.9 %collective-permute-start.24 = (bf16[64,768]{1,0:T(8,128)(2,1)}, bf16[64,768]{1,0:T(8,128)(2,1)S(1)}, u32[]{:S(2)}, u32[]{:S(2)}) collective-permute-start(bf16[64,768]{1,0:T(8,128)(2,1)} %get-tuple-element.73), channel_id=1, source_target_pairs={{0,4},{2,6},{4,0},{6,2},{1,5},{3,7},{5,1},{7,3},{8,12},{10,14},{12... | collective-permute-start | bytes 294920 | tf_op jit(solution)/shard_map/ppermute | solution.py:43
  104.7 6.3 %copy-start.5 = (bf16[192,768]{1,0:T(8,128)(2,1)}, bf16[192,768]{1,0:T(8,128)(2,1)S(1)}, u32[]{:S(2)}) copy-start(bf16[192,768]{1,0:T(8,128)(2,1)S(1)} %collective-permute-done.27.refs_1_) | copy-start | bytes 884740
  104.7 13.6 %collective-permute-start.25 = (bf16[64,768]{1,0:T(8,128)(2,1)}, bf16[64,768]{1,0:T(8,128)(2,1)S(1)}, u32[]{:S(2)}, u32[]{:S(2)}) collective-permute-start(bf16[64,768]{1,0:T(8,128)(2,1)} %get-tuple-element.74), channel_id=1, source_target_pairs={{0,6},{2,4},{4,2},{6,0},{1,7},{3,5},{5,3},{7,1},{8,14},{10,12},{12... | collective-permute-start | bytes 294920 | tf_op jit(solution)/shard_map/ppermute | solution.py:43
  110.9 17.7 %collective-permute-start.18 = (bf16[1,64,768]{2,1,0:T(8,128)(2,1)S(1)}, bf16[1,64,768]{2,1,0:T(8,128)(2,1)S(1)}, u32[]{:S(2)}, u32[]{:S(2)}) collective-permute-start(bf16[1,64,768]{2,1,0:T(8,128)(2,1)S(1)} %get-tuple-element.103), channel_id=1, source_target_pairs={{0,1},{1,0},{2,3},{3,2},{4,5},{5,4},{6,7},{7,6},{8,9},{9,8},{10,11... | collective-permute-start | bytes 294920 | tf_op jit(solution)/shard_map/ppermute | solution.py:43
  113.9 7.0 %collective-permute-start.30 = (bf16[48,768]{1,0:T(8,128)(2,1)}, bf16[48,768]{1,0:T(8,128)(2,1)S(1)}, u32[]{:S(2)}, u32[]{:S(2)}) collective-permute-start(bf16[48,768]{1,0:T(8,128)(2,1)} %get-tuple-element.83), channel_id=1, source_target_pairs={{0,2},{2,0},{4,6},{6,4},{1,3},{3,1},{5,7},{7,5},{8,10},{10,8},{12,... | collective-permute-start | bytes 221192 | tf_op jit(solution)/shard_map/ppermute | solution.py:43
  115.1 3.2 %copy-start.8 = (bf16[64,768]{1,0:T(8,128)(2,1)}, bf16[64,768]{1,0:T(8,128)(2,1)S(1)}, u32[]{:S(2)}) copy-start(bf16[64,768]{1,0:T(8,128)(2,1)S(1)} %collective-permute-done.23.refs_1_) | copy-start | bytes 294916
  115.1 9.1 %collective-permute-start.31 = (bf16[48,768]{1,0:T(8,128)(2,1)}, bf16[48,768]{1,0:T(8,128)(2,1)S(1)}, u32[]{:S(2)}, u32[]{:S(2)}) collective-permute-start(bf16[48,768]{1,0:T(8,128)(2,1)} %get-tuple-element.84), channel_id=1, source_target_pairs={{0,4},{2,6},{4,0},{6,2},{1,5},{3,7},{5,1},{7,3},{8,12},{10,14},{12... | collective-permute-start | bytes 221192 | tf_op jit(solution)/shard_map/ppermute | solution.py:43
  116.2 8.1 %collective-permute-start.32 = (bf16[48,768]{1,0:T(8,128)(2,1)}, bf16[48,768]{1,0:T(8,128)(2,1)S(1)}, u32[]{:S(2)}, u32[]{:S(2)}) collective-permute-start(bf16[48,768]{1,0:T(8,128)(2,1)} %get-tuple-element.85), channel_id=1, source_target_pairs={{0,6},{2,4},{4,2},{6,0},{1,7},{3,5},{5,3},{7,1},{8,14},{10,12},{12... | collective-permute-start | bytes 221192 | tf_op jit(solution)/shard_map/ppermute | solution.py:43
  120.9 5.8 %collective-permute-start.26 = (f32[24,128]{1,0:T(8,128)}, f32[24,128]{1,0:T(8,128)S(1)}, u32[]{:S(2)}, u32[]{:S(2)}) collective-permute-start(f32[24,128]{1,0:T(8,128)} %get-tuple-element.75.refs_0_), channel_id=1, source_target_pairs={{0,1},{1,0},{2,3},{3,2},{4,5},{5,4},{6,7},{7,6},{8,9},{9,8},{10,11... | collective-permute-start | bytes 36872 | tf_op jit(solution)/shard_map/ppermute | solution.py:43
  120.9 3.3 %copy-start.12 = (bf16[48,768]{1,0:T(8,128)(2,1)}, bf16[48,768]{1,0:T(8,128)(2,1)S(1)}, u32[]{:S(2)}) copy-start(bf16[48,768]{1,0:T(8,128)(2,1)S(1)} %collective-permute-done.30.refs_1_) | copy-start | bytes 221188
  128.7 1.4 %collective-permute-start.19 = (f32[1,64,768]{2,1,0:T(8,128)S(1)}, f32[1,64,768]{2,1,0:T(8,128)S(1)}, u32[]{:S(2)}, u32[]{:S(2)}) collective-permute-start(f32[1,64,768]{2,1,0:T(8,128)S(1)} %get-tuple-element.102), channel_id=1, source_target_pairs={{0,1},{1,0},{2,3},{3,2},{4,5},{5,4},{6,7},{7,6},{8,9},{9,8},{10,11... | collective-permute-start | bytes 589832 | tf_op jit(solution)/shard_map/ppermute | solution.py:43
  (16 other events, 19.6 us)

commit v4 on v3

--- a/solution.py
+++ b/solution.py
@@ -225,9 +225,9 @@
     ]
     gain, shift = row_of(gain_ref), row_of(shift_ref)
     outs = refs[core_count + fsdp_count + 7 :]
-    branch, norm_out, sums, bias_out = outs[:4]
+    mixed, proj_out, weight, bias_out = outs[:4]
     grad_outs = outs[4 : 4 + fsdp_count]
-    weight, grads, mixed, total = outs[4 + fsdp_count :]
+    grads, total = outs[4 + fsdp_count :]
     size = pos_col.shape[0]
     cols = weight.shape[1]
     features = own_heads * HD
@@ -313,16 +313,7 @@
         total[:, high_cols:] = jnp.zeros((weight.shape[0], cols - high_cols), jnp.float32)
     total[:, low_cols:] += dot_first(seq_grads, mixed[...])
     send_blocks(total, grad_outs, grad_outs[0].shape[0])
-    branch[...] = dot_last(mixed[...], weight[:, low_cols:])
-    norm_grad = dot_last(proj_low, weight[:, :high_cols])
-    norm_out[...] = norm_grad * gain
-    sums[...] = jnp.concatenate(
-        [
-            jnp.sum(norm_grad * centred, axis=0, keepdims=True),
-            jnp.sum(norm_grad, axis=0, keepdims=True),
-        ],
-        axis=0,
-    )
+    proj_out[...] = proj_low
     bias_out[:, :high_cols] = jnp.sum(proj_grad, axis=0, keepdims=True)
     if cols > high_cols:
         bias_out[:, high_cols:] = jnp.zeros((1, cols - high_cols), jnp.float32)
@@ -336,17 +327,18 @@
         shift_ref,
         bias_ref,
         columns_ref,
-        attn_branch,
-        attn_norm,
-        attn_sums,
+        attn_gain_ref,
+        mixed,
+        proj_low,
+        attn_weight,
         attn_bias,
-    ) = refs[core_count + fsdp_count : core_count + fsdp_count + 8]
-    outs = refs[core_count + fsdp_count + 8 :]
+    ) = refs[core_count + fsdp_count : core_count + fsdp_count + 9]
+    outs = refs[core_count + fsdp_count + 9 :]
     both = outs[:core_count]
     grad_outs = outs[core_count : core_count + fsdp_count]
     weight, total = outs[core_count + fsdp_count :]
     gain, shift = row_of(gain_ref), row_of(shift_ref)
-    size, width = attn_branch.shape
+    size, width = mixed.shape[0], weight.shape[0]
     both_cols = weight.shape[1]
     padded = both_cols // 2
     ctx_at = lax.axis_index("ctx")
@@ -373,12 +365,19 @@
     total[:, :padded] = dot_first(mlp_in, pre_low)
     total[:, padded:] = dot_first(grad_rows, hidden)
     norm_grad = dot_last(pre_low, up)
+    low_cols = attn_weight.shape[1] - mixed.shape[1]
+    attn_branch = dot_last(mixed[...], attn_weight[:, low_cols:])
+    attn_norm = dot_last(proj_low[...], attn_weight[:, : proj_low.shape[1]])
+    slot = core * near + inner
+    seq_centred = centred[:size]
+    for i in range(1, core_count * near):
+        seq_centred = jnp.where(slot == i, centred[i * size : (i + 1) * size], seq_centred)
     bias_sum = jnp.concatenate(
         [jnp.sum(pre_grad, axis=0, keepdims=True), jnp.zeros((1, padded), jnp.float32)], axis=1
     )
     vectors = [
-        attn_sums[0:1, :],
-        attn_sums[1:2, :],
+        jnp.sum(attn_norm * seq_centred, axis=0, keepdims=True),
+        jnp.sum(attn_norm, axis=0, keepdims=True),
         jnp.sum(norm_grad * centred, axis=0, keepdims=True),
         jnp.sum(norm_grad, axis=0, keepdims=True),
         row_of(columns_ref),
@@ -387,14 +386,15 @@
     extra = [piece for vector in vectors for piece in folded(vector, both_cols)] + [bias_sum]
     send_blocks(total, grad_outs, width // fsdp_count, extra)
     norm_grad = norm_grad * gain
+    attn_norm = attn_norm * row_of(attn_gain_ref)
     branch = dot_last(hidden, down)
     for j in range(core_count):
         for i in range(near):
             here = (core == j) & (inner == i)
             at = (j * near + i) * size
             out = both[j]
-            out[0, i] = branch[at : at + size] + jnp.where(here, attn_branch[...], 0.0)
-            out[1, i] = norm_grad[at : at + size] + jnp.where(here, attn_norm[...], 0.0)
+            out[0, i] = branch[at : at + size] + jnp.where(here, attn_branch, 0.0)
+            out[1, i] = norm_grad[at : at + size] + jnp.where(here, attn_norm, 0.0)
 
 
 def sum_blocks_kernel(fsdp_count, ctx_count, rows_here, *refs):
@@ -552,7 +552,7 @@
     vector_rows = -(-vector_rows // SUBLANES) * SUBLANES
 
     row_blocks = ctx_count if loose else 1
-    attn_branch, attn_norm, attn_sums, qkv_bias_part, *early_grads = local_kernel(
+    mixed, proj_low, attn_weight, qkv_bias_part, *early_grads = local_kernel(
         functools.partial(
             attention_kernel,
             fsdp_count,
@@ -564,15 +564,14 @@
             seqs,
             row_blocks,
         ),
-        [shaped((size, width), f32)] * 2
-        + [shaped((2, width), f32), shaped((1, cols), f32)]
+        [
+            shaped((size, cols - low_cols), bf16),
+            shaped((size, high_cols), bf16),
+            shaped((width, cols), bf16),
+            shaped((1, cols), f32),
+        ]
         + grad_blocks(cols),
-        [
-            pltpu.VMEM((width, cols), bf16),
-            pltpu.VMEM((size, high_cols), f32),
-            pltpu.VMEM((size, cols - low_cols), bf16),
-            pltpu.VMEM((width, cols), f32),
-        ],
+        [pltpu.VMEM((size, high_cols), f32), pltpu.VMEM((width, cols), f32)],
         flops=16 * size * width * cols,
         moved=16 * size * width,
     )(
@@ -601,9 +600,10 @@
         tiled(mlp_shift),
         tiled(up_bias),
         tiled(column_sums),
-        attn_branch,
-        attn_norm,
-        attn_sums,
+        tiled(attn_gain),
+        mixed,
+        proj_low,
+        attn_weight,
         qkv_bias_part,
     )
     row_parts, late_grads = outs[:tp_count], outs[tp_count:]

time: 131 us -> 132 us (level)
  transfers between devices with their start and end apart: 33 -> 33, of which waited for: 12 -> 13; matrix products, arithmetic and copies ran while one was open for 7% -> 7% of each run, Pallas kernels for 15% -> 14%
where the time goes in v4:
time: 132 us; the launch traced here: 131 us
  waiting for transfers between devices  47.4 us (36%)
  starting transfers between devices  37.5 us (28%)
  Pallas kernels  28.3 us (21%)
  other arithmetic  9.73 us (7%)
  local copies, waits for them, and re-layouts  7.05 us (5%)
    ppermute x33, waiting for transfers between devices, swap(): lax.ppermute(value, axis, [(i, i ^ bit) for i in range(lax.axis_size(axis...  47.4 us
    ppermute x33, starting transfers between devices, swap(): lax.ppermute(value, axis, [(i, i ^ bit) for i in range(lax.axis_size(axis...  37.5 us
    pallas_call x1, Pallas kernels, on_device(): local_kernel(functools.partial(mlp_kernel, fsdp_count, tp_count, near, he...  7.88 us
    pallas_call x1, Pallas kernels, on_device(): local_kernel(functools.partial(attention_kernel, fsdp_count, tp_count, ne...  7.45 us
    unnamed x68, local copies, waits for them, and re-layouts  6.11 us
    pallas_call x2, Pallas kernels, scatter_weights(): local_kernel(functools.partial(sum_blocks_kernel, fsdp_count, ctx_count,...  4.46 us
  transfers between devices with their start and end apart: 33, of which 13 were waited for; matrix products, arithmetic and copies ran while one was open for 7% of the time, Pallas kernels for 14%

profile of v4, /device:TPU:0, one launch (start us, length us, event | category | flops | bytes accessed | tf_op | source)
XLA Modules:
  0.0 131.2 jit_solution(13395926909566958090)
XLA Ops:
  0.7 1.7 %shard_map.255 = (bf16[48,768]{1,0:T(8,128)(2,1)}, bf16[48,768]{1,0:T(8,128)(2,1)}) custom-call(bf16[48,1152]{1,0:T(8,128)(2,1)} %qkv_ref.1, bf16[48,384]{1,0:T(8,128)(2,1)} %bitcast.52), custom_call_target="tpu_custom_call" | custom-call | tf_op jit(solution)/shard_map/pallas_call | solution.py:507
  2.4 3.1 %collective-permute-start.9 = (bf16[48,768]{1,0:T(8,128)(2,1)}, bf16[48,768]{1,0:T(8,128)(2,1)S(1)}, u32[]{:S(2)}, u32[]{:S(2)}) collective-permute-start(bf16[48,768]{1,0:T(8,128)(2,1)} %get-tuple-element.60), channel_id=1, source_target_pairs={{0,2},{2,0},{4,6},{6,4},{1,3},{3,1},{5,7},{7,5},{8,10},{10,8},{12,... | collective-permute-start | bytes 221192 | tf_op jit(solution)/shard_map/ppermute | solution.py:43
  5.4 2.5 %collective-permute-start.11 = (bf16[48,768]{1,0:T(8,128)(2,1)}, bf16[48,768]{1,0:T(8,128)(2,1)S(1)}, u32[]{:S(2)}, u32[]{:S(2)}) collective-permute-start(bf16[48,768]{1,0:T(8,128)(2,1)} %get-tuple-element.60), channel_id=1, source_target_pairs={{0,6},{2,4},{4,2},{6,0},{1,7},{3,5},{5,3},{7,1},{8,14},{10,12},{12... | collective-permute-start | bytes 221192 | tf_op jit(solution)/shard_map/ppermute | solution.py:43
  7.9 1.1 convert_reduce_fusion
  9.0 1.1 convert_bitcast_fusion
  10.2 2.8 %collective-permute-start.10 = (bf16[48,768]{1,0:T(8,128)(2,1)}, bf16[48,768]{1,0:T(8,128)(2,1)S(1)}, u32[]{:S(2)}, u32[]{:S(2)}) collective-permute-start(bf16[48,768]{1,0:T(8,128)(2,1)} %get-tuple-element.59), channel_id=1, source_target_pairs={{0,4},{2,6},{4,0},{6,2},{1,5},{3,7},{5,1},{7,3},{8,12},{10,14},{12... | collective-permute-start | bytes 221192 | tf_op jit(solution)/shard_map/ppermute | solution.py:43
  13.0 1.7 %shard_map.254 = (bf16[48,768]{1,0:T(8,128)(2,1)}, bf16[48,768]{1,0:T(8,128)(2,1)}, bf16[48,768]{1,0:T(8,128)(2,1)}, bf16[48,768]{1,0:T(8,128)(2,1)}) custom-call(bf16[48,1536]{1,0:T(8,128)(2,1)} %up_ref.1, bf16[48,1536]{1,0:T(8,128)(2,1)} %bitcast.51), custom_call_target="tpu_custom_call" | custom-call | tf_op jit(solution)/shard_map/pallas_call | solution.py:511
  16.4 0.9 constant_dynamic-update-slice_fusion.7
  17.3 5.8 %collective-permute-done = bf16[2,1,1,64,768]{4,3,0,2,1:T(8,128)(2,1)S(1)} collective-permute-done((bf16[2,1,1,64,768]{4,3,0,2,1:T(8,128)(2,1)S(1)}, bf16[2,1,1,64,768]{4,3,0,2,1:T(8,128)(2,1)S(1)}, u32[]{:S(2)}, u32[]{:S(2)}) %collective-permute-start) | collective-permute-done | bytes 196640 | tf_op jit(solution)/shard_map/ppermute | solution.py:43
  23.3 0.8 copy.45.refs_11_
  24.7 1.2 fusion.11
  26.0 7.9 %collective-permute-done.1 = bf16[2,1,2,64,768]{4,3,0,2,1:T(8,128)(2,1)S(1)} collective-permute-done((bf16[2,1,2,64,768]{4,3,0,2,1:T(8,128)(2,1)S(1)}, bf16[2,1,2,64,768]{4,3,0,2,1:T(8,128)(2,1)S(1)}, u32[]{:S(2)}, u32[]{:S(2)}) %collective-permute-start.1) | collective-permute-done | bytes 393248 | tf_op jit(solution)/shard_map/ppermute | solution.py:43
  34.8 2.1 %collective-permute-start.5 = (bf16[48,768]{1,0:T(8,128)(2,1)S(1)}, bf16[48,768]{1,0:T(8,128)(2,1)S(1)}, u32[]{:S(2)}, u32[]{:S(2)}) collective-permute-start(bf16[48,768]{1,0:T(8,128)(2,1)S(1)} %copy-done.29), channel_id=1, source_target_pairs={{0,6},{2,4},{4,2},{6,0},{1,7},{3,5},{5,3},{7,1},{8,14},{10,12},{12... | collective-permute-start | bytes 221192 | tf_op jit(solution)/shard_map/ppermute | solution.py:43
  36.9 1.6 %collective-permute-start.12 = (bf16[192,768]{1,0:T(8,128)(2,1)S(1)}, bf16[192,768]{1,0:T(8,128)(2,1)S(1)}, u32[]{:S(2)}, u32[]{:S(2)}) collective-permute-start(bf16[192,768]{1,0:T(8,128)(2,1)S(1)} %constant_dynamic-update-slice_fusion.4.refs_2_), channel_id=1, source_target_pairs={{0,8},{8,0},{16,24},{24,16},{1,9},{9,1},{17,25},{25,17},{2,10},{10... | collective-permute-start | bytes 884744 | tf_op jit(solution)/shard_map/ppermute | solution.py:43
  38.5 1.5 %collective-permute-start.13 = (bf16[192,768]{1,0:T(8,128)(2,1)S(1)}, bf16[192,768]{1,0:T(8,128)(2,1)S(1)}, u32[]{:S(2)}, u32[]{:S(2)}) collective-permute-start(bf16[192,768]{1,0:T(8,128)(2,1)S(1)} %constant_dynamic-update-slice_fusion.4.refs_2_), channel_id=1, source_target_pairs={{0,16},{8,24},{16,0},{24,8},{1,17},{9,25},{17,1},{25,9},{2,18},{10... | collective-permute-start | bytes 884744 | tf_op jit(solution)/shard_map/ppermute | solution.py:43
  40.0 1.9 %collective-permute-done.4 = bf16[48,768]{1,0:T(8,128)(2,1)S(1)} collective-permute-done((bf16[48,768]{1,0:T(8,128)(2,1)S(1)}, bf16[48,768]{1,0:T(8,128)(2,1)S(1)}, u32[]{:S(2)}, u32[]{:S(2)}) %collective-permute-start.4) | collective-permute-done | bytes 73760 | tf_op jit(solution)/shard_map/ppermute | solution.py:43
  41.9 2.4 %collective-permute-start.14 = (bf16[192,768]{1,0:T(8,128)(2,1)S(1)}, bf16[192,768]{1,0:T(8,128)(2,1)S(1)}, u32[]{:S(2)}, u32[]{:S(2)}) collective-permute-start(bf16[192,768]{1,0:T(8,128)(2,1)S(1)} %constant_dynamic-update-slice_fusion.4.refs_2_), channel_id=1, source_target_pairs={{0,24},{8,16},{16,8},{24,0},{1,25},{9,17},{17,9},{25,1},{2,26},{10... | collective-permute-start | bytes 884744 | tf_op jit(solution)/shard_map/ppermute | solution.py:43
  45.0 1.9 %collective-permute-done.12.refs_3_ = bf16[192,768]{1,0:T(8,128)(2,1)S(1)} collective-permute-done((bf16[192,768]{1,0:T(8,128)(2,1)S(1)}, bf16[192,768]{1,0:T(8,128)(2,1)S(1)}, u32[]{:S(2)}, u32[]{:S(2)}) %collective-permute-start.12) | collective-permute-done | bytes 294944 | tf_op jit(solution)/shard_map/ppermute | solution.py:43
  46.9 1.5 %collective-permute-start.7 = (bf16[192,768]{1,0:T(8,128)(2,1)S(1)}, bf16[192,768]{1,0:T(8,128)(2,1)}, u32[]{:S(2)}, u32[]{:S(2)}) collective-permute-start(bf16[192,768]{1,0:T(8,128)(2,1)S(1)} %constant_dynamic-update-slice_fusion.refs_2_), channel_id=1, source_target_pairs={{0,16},{8,24},{16,0},{24,8},{1,17},{9,25},{17,1},{25,9},{2,18},{10... | collective-permute-start | bytes 884744 | tf_op jit(solution)/shard_map/ppermute | solution.py:43
  48.4 5.3 %collective-permute-done.13.refs_4_ = bf16[192,768]{1,0:T(8,128)(2,1)S(1)} collective-permute-done((bf16[192,768]{1,0:T(8,128)(2,1)S(1)}, bf16[192,768]{1,0:T(8,128)(2,1)S(1)}, u32[]{:S(2)}, u32[]{:S(2)}) %collective-permute-start.13) | collective-permute-done | bytes 294944 | tf_op jit(solution)/shard_map/ppermute | solution.py:43
  53.8 1.3 %collective-permute-start.8 = (bf16[192,768]{1,0:T(8,128)(2,1)S(1)}, bf16[192,768]{1,0:T(8,128)(2,1)}, u32[]{:S(2)}, u32[]{:S(2)}) collective-permute-start(bf16[192,768]{1,0:T(8,128)(2,1)S(1)} %constant_dynamic-update-slice_fusion.refs_2_), channel_id=1, source_target_pairs={{0,24},{8,16},{16,8},{24,0},{1,25},{9,17},{17,9},{25,1},{2,26},{10... | collective-permute-start | bytes 884744 | tf_op jit(solution)/shard_map/ppermute | solution.py:43
  56.5 0.9 copy-done.20
  57.4 7.5 %shard_map.256 = (bf16[256,256]{1,0:T(8,128)(2,1)}, bf16[256,640]{1,0:T(8,128)(2,1)}, bf16[768,768]{1,0:T(8,128)(2,1)}, f32[1,768]{1,0:T(1,128)}, f32[192,768]{1...) custom-call(bf16[2,1,256,768]{3,2,1,0:T(8,128)(2,1)} %bitcast.49, ...), custom_call_target="tpu_custom_call" | custom-call | flops 2415919104 | bytes 3145728 | tf_op jit(solution)/shard_map/pallas_call | solution.py:555
  64.8 1.6 %collective-permute-done.7.refs_4_ = bf16[192,768]{1,0:T(8,128)(2,1)} collective-permute-done((bf16[192,768]{1,0:T(8,128)(2,1)S(1)}, bf16[192,768]{1,0:T(8,128)(2,1)}, u32[]{:S(2)}, u32[]{:S(2)}) %collective-permute-start.7) | collective-permute-done | bytes 294944 | tf_op jit(solution)/shard_map/ppermute | solution.py:43
  66.4 7.9 %shard_map.257 = (f32[2,1,256,768]{3,2,1,0:T(8,128)}, f32[2,1,256,768]{3,2,1,0:T(8,128)}, f32[208,768]{1,0:T(8,128)}, bf16[208,768]{1,0:T(8,128)(2,1)}, bf16[208...) custom-call(bf16[2,1,256,768]{3,2,1,0:T(8,128)(2,1)} %bitcast.50, bf16[2,1,256,768]{3,2,1,0:T(8,128)(2,1)} %copy-done.20, ...), custom_call_target="tpu_custom_call" | custom-call | flops 1811939328 | bytes 6291456 | tf_op jit(solution)/shard_map/pallas_call | solution.py:588
  74.4 3.6 %collective-permute-done.15 = f32[2,1,256,768]{3,2,1,0:T(8,128)S(1)} collective-permute-done((f32[2,1,256,768]{3,2,1,0:T(8,128)}, f32[2,1,256,768]{3,2,1,0:T(8,128)S(1)}, u32[]{:S(2)}, u32[]{:S(2)}) %collective-permute-start.15) | collective-permute-done | bytes 1572896 | tf_op jit(solution)/shard_map/ppermute | solution.py:43
  78.0 1.7 %add.312 = f32[2,1,256,768]{3,2,1,0:T(8,128)S(1)} add(f32[2,1,256,768]{3,2,1,0:T(8,128)} %get-tuple-element.65, f32[2,1,256,768]{3,2,1,0:T(8,128)S(1)} %collective-permute-done.15) | non-fusion elementwise | flops 393216 | bytes 4718592 | tf_op jit(solution)/shard_map/add | solution.py:610
  79.8 0.9 collective-permute-start.16
  80.9 1.8 %collective-permute-start.20 = (bf16[208,768]{1,0:T(8,128)(2,1)S(1)}, bf16[208,768]{1,0:T(8,128)(2,1)S(1)}, u32[]{:S(2)}, u32[]{:S(2)}) collective-permute-start(bf16[208,768]{1,0:T(8,128)(2,1)S(1)} %copy-done.23), channel_id=1, source_target_pairs={{0,8},{8,0},{16,24},{24,16},{1,9},{9,1},{17,25},{25,17},{2,10},{10... | collective-permute-start | bytes 958472 | tf_op jit(solution)/shard_map/ppermute | solution.py:43
  83.0 1.4 %collective-permute-start.22 = (bf16[208,768]{1,0:T(8,128)(2,1)S(1)}, bf16[208,768]{1,0:T(8,128)(2,1)S(1)}, u32[]{:S(2)}, u32[]{:S(2)}) collective-permute-start(bf16[208,768]{1,0:T(8,128)(2,1)S(1)} %copy-done.21), channel_id=1, source_target_pairs={{0,24},{8,16},{16,8},{24,0},{1,25},{9,17},{17,9},{25,1},{2,26},{10... | collective-permute-start | bytes 958472 | tf_op jit(solution)/shard_map/ppermute | solution.py:43
  84.4 6.5 %collective-permute-done.16 = bf16[2,1,2,64,768]{4,3,2,1,0:T(8,128)(2,1)S(1)} collective-permute-done((bf16[2,1,2,64,768]{4,3,2,1,0:T(8,128)(2,1)S(1)}, bf16[2,1,2,64,768]{4,3,2,1,0:T(8,128)(2,1)S(1)}, u32[]{:S(2)}, u32[]{:S(2)}) %collective-permute-start.16) | collective-permute-done | bytes 393248 | tf_op jit(solution)/shard_map/ppermute | solution.py:43
  91.1 1.1 collective-permute-start.17
  92.2 1.7 %collective-permute-start.27 = (bf16[192,768]{1,0:T(8,128)(2,1)}, bf16[192,768]{1,0:T(8,128)(2,1)S(1)}, u32[]{:S(2)}, u32[]{:S(2)}) collective-permute-start(bf16[192,768]{1,0:T(8,128)(2,1)} %get-tuple-element.79), channel_id=1, source_target_pairs={{0,8},{8,0},{16,24},{24,16},{1,9},{9,1},{17,25},{25,17},{2,10},{10... | collective-permute-start | bytes 884744 | tf_op jit(solution)/shard_map/ppermute | solution.py:43
  94.3 4.3 %collective-permute-done.21.refs_2_ = bf16[208,768]{1,0:T(8,128)(2,1)S(1)} collective-permute-done((bf16[208,768]{1,0:T(8,128)(2,1)S(1)}, bf16[208,768]{1,0:T(8,128)(2,1)S(1)}, u32[]{:S(2)}, u32[]{:S(2)}) %collective-permute-start.21) | collective-permute-done | bytes 319520 | tf_op jit(solution)/shard_map/ppermute | solution.py:43
  99.9 2.3 %shard_map.258 = (f32[64,768]{1,0:T(8,128)}, bf16[64,768]{1,0:T(8,128)(2,1)}, bf16[64,768]{1,0:T(8,128)(2,1)}, bf16[64,768]{1,0:T(8,128)(2,1)}) custom-call(f32[208,768]{1,0:T(8,128)} %get-tuple-element.67.refs_0_, bf16[208,768]{1,0:T(8,128)(2,1)} %copy-done.2, bf16[208,768]{1,0:T(8,128)(2,1)} %copy-done.3, bf16[208,768]{1,0:T(8,128)(2,1)} %copy-done.4), custom_call_target="tpu_custom_call" | custom-call | tf_op jit(solution)/shard_map/pallas_call | solution.py:622
  102.2 1.2 collective-permute-start.23
  103.4 1.1 collective-permute-start.24
  104.9 2.2 %collective-permute-start.25 = (bf16[64,768]{1,0:T(8,128)(2,1)}, bf16[64,768]{1,0:T(8,128)(2,1)S(1)}, u32[]{:S(2)}, u32[]{:S(2)}) collective-permute-start(bf16[64,768]{1,0:T(8,128)(2,1)} %get-tuple-element.74), channel_id=1, source_target_pairs={{0,6},{2,4},{4,2},{6,0},{1,7},{3,5},{5,3},{7,1},{8,14},{10,12},{12... | collective-permute-start | bytes 294920 | tf_op jit(solution)/shard_map/ppermute | solution.py:43
  107.2 4.0 %collective-permute-done.28.refs_2_ = bf16[192,768]{1,0:T(8,128)(2,1)S(1)} collective-permute-done((bf16[192,768]{1,0:T(8,128)(2,1)}, bf16[192,768]{1,0:T(8,128)(2,1)S(1)}, u32[]{:S(2)}, u32[]{:S(2)}) %collective-permute-start.28) | collective-permute-done | bytes 294944 | tf_op jit(solution)/shard_map/ppermute | solution.py:43
  112.0 2.2 %shard_map.261 = (f32[48,768]{1,0:T(8,128)}, bf16[48,768]{1,0:T(8,128)(2,1)}, bf16[48,768]{1,0:T(8,128)(2,1)}, bf16[48,768]{1,0:T(8,128)(2,1)}) custom-call(f32[192,768]{1,0:T(8,128)} %get-tuple-element.78.refs_0_, bf16[192,768]{1,0:T(8,128)(2,1)} %copy-done.5, bf16[192,768]{1,0:T(8,128)(2,1)} %copy-done.6, bf16[192,768]{1,0:T(8,128)(2,1)} %copy-done.7), custom_call_target="tpu_custom_call" | custom-call | tf_op jit(solution)/shard_map/pallas_call | solution.py:622
  114.2 1.2 collective-permute-start.30
  115.4 1.1 collective-permute-start.31
  116.4 2.1 %collective-permute-start.32 = (bf16[48,768]{1,0:T(8,128)(2,1)}, bf16[48,768]{1,0:T(8,128)(2,1)S(1)}, u32[]{:S(2)}, u32[]{:S(2)}) collective-permute-start(bf16[48,768]{1,0:T(8,128)(2,1)} %get-tuple-element.85), channel_id=1, source_target_pairs={{0,6},{2,4},{4,2},{6,0},{1,7},{3,5},{5,3},{7,1},{8,14},{10,12},{12... | collective-permute-start | bytes 221192 | tf_op jit(solution)/shard_map/ppermute | solution.py:43
  119.2 2.0 %shard_map.259 = (f32[48,1536]{1,0:T(8,128)}, f32[48,1536]{1,0:T(8,128)}, f32[24,128]{1,0:T(8,128)}, f32[6,128]{1,0:T(8,128)}, f32[6,128]{1,0:T(8,128)}, /*index=5*/f32[9,128]{1,0:T(8,128)}, f32[12,128]{1,0:T(8,128)}) custom-call(f32[64,768]{1,0:T(8,128)} %get-tuple-element.71.refs_0_, bf16[64,768]{1,0:T(8,128)(2,1)} %copy-done.8, ...), custom_call_target="tpu_custom_call" | custom-call | tf_op jit(solution)/shard_map/pallas_call | solution.py:644
  121.2 3.3 %collective-permute-done.31.refs_2_ = bf16[48,768]{1,0:T(8,128)(2,1)S(1)} collective-permute-done((bf16[48,768]{1,0:T(8,128)(2,1)}, bf16[48,768]{1,0:T(8,128)(2,1)S(1)}, u32[]{:S(2)}, u32[]{:S(2)}) %collective-permute-start.31) | collective-permute-done | bytes 73760 | tf_op jit(solution)/shard_map/ppermute | solution.py:43
  125.2 1.8 %shard_map.262 = (f32[48,1152]{1,0:T(8,128)}, f32[48,384]{1,0:T(8,128)}) custom-call(f32[48,768]{1,0:T(8,128)} %get-tuple-element.82.refs_0_, bf16[48,768]{1,0:T(8,128)(2,1)} %copy-done.12, bf16[48,768]{1,0:T(8,128)(2,1)} %copy-done.13, bf16[48,768]{1,0:T(8,128)(2,1)} %copy-done.14), custom_call_target="tpu_custom_call" | custom-call | tf_op jit(solution)/shard_map/pallas_call | solution.py:639
  127.6 1.3 %shard_map.260 = (f32[6,128]{1,0:T(8,128)}, f32[6,128]{1,0:T(8,128)}, f32[6,128]{1,0:T(8,128)}, f32[6,128]{1,0:T(8,128)}) custom-call(f32[24,128]{1,0:T(8,128)} %get-tuple-element.75.refs_0_, f32[24,128]{1,0:T(8,128)} %copy-done.17), custom_call_target="tpu_custom_call" | custom-call | tf_op jit(solution)/shard_map/pallas_call | solution.py:661
  130.4 0.8 pad_maximum_fusion.2
  (135 shorter events, 12.6 us)
Async XLA Ops:
  0.6 23.5 %copy-start = (f32[2,64,768]{2,1,0:T(8,128)S(1)}, f32[2,64,768]{2,1,0:T(8,128)}, u32[]{:S(2)}) copy-start(f32[2,64,768]{2,1,0:T(8,128)} %param.29) | copy-start | bytes 1179652
  2.4 32.2 %collective-permute-start.9 = (bf16[48,768]{1,0:T(8,128)(2,1)}, bf16[48,768]{1,0:T(8,128)(2,1)S(1)}, u32[]{:S(2)}, u32[]{:S(2)}) collective-permute-start(bf16[48,768]{1,0:T(8,128)(2,1)} %get-tuple-element.60), channel_id=1, source_target_pairs={{0,2},{2,0},{4,6},{6,4},{1,3},{3,1},{5,7},{7,5},{8,10},{10,8},{12,... | collective-permute-start | bytes 221192 | tf_op jit(solution)/shard_map/ppermute | solution.py:43
  5.4 31.5 %collective-permute-start.11 = (bf16[48,768]{1,0:T(8,128)(2,1)}, bf16[48,768]{1,0:T(8,128)(2,1)S(1)}, u32[]{:S(2)}, u32[]{:S(2)}) collective-permute-start(bf16[48,768]{1,0:T(8,128)(2,1)} %get-tuple-element.60), channel_id=1, source_target_pairs={{0,6},{2,4},{4,2},{6,0},{1,7},{3,5},{5,3},{7,1},{8,14},{10,12},{12... | collective-permute-start | bytes 221192 | tf_op jit(solution)/shard_map/ppermute | solution.py:43
  10.0 13.0 %collective-permute-start = (bf16[2,1,1,64,768]{4,3,0,2,1:T(8,128)(2,1)S(1)}, bf16[2,1,1,64,768]{4,3,0,2,1:T(8,128)(2,1)S(1)}, u32[]{:S(2)}, u32[]{:S(2)}) collective-permute-start(bf16[2,1,1,64,768]{4,3,0,2,1:T(8,128)(2,1)S(1)} %maximum_bitcast_fusion), channel_id=1, source_target_pairs={{0,4},{2,6},{4,0},{6,2},{1,5},{3,7},{5,1},{7,3},{8,12},{10,14},{12... | collective-permute-start | bytes 589832 | tf_op jit(solution)/shard_map/ppermute | solution.py:43
  10.2 24.5 %collective-permute-start.10 = (bf16[48,768]{1,0:T(8,128)(2,1)}, bf16[48,768]{1,0:T(8,128)(2,1)S(1)}, u32[]{:S(2)}, u32[]{:S(2)}) collective-permute-start(bf16[48,768]{1,0:T(8,128)(2,1)} %get-tuple-element.59), channel_id=1, source_target_pairs={{0,4},{2,6},{4,0},{6,2},{1,5},{3,7},{5,1},{7,3},{8,12},{10,14},{12... | collective-permute-start | bytes 221192 | tf_op jit(solution)/shard_map/ppermute | solution.py:43
  14.8 10.0 %copy-start.11 = (bf16[48,768]{1,0:T(8,128)(2,1)S(1)}, bf16[48,768]{1,0:T(8,128)(2,1)}, u32[]{:S(2)}) copy-start(bf16[48,768]{1,0:T(8,128)(2,1)} %get-tuple-element.55) | copy-start | bytes 221188
  14.8 19.2 %copy-start.30 = (bf16[48,768]{1,0:T(8,128)(2,1)S(1)}, bf16[48,768]{1,0:T(8,128)(2,1)}, u32[]{:S(2)}) copy-start(bf16[48,768]{1,0:T(8,128)(2,1)} %get-tuple-element.57) | copy-start | bytes 221188
  14.8 23.7 %collective-permute-start.3 = (bf16[48,768]{1,0:T(8,128)(2,1)}, bf16[48,768]{1,0:T(8,128)(2,1)S(1)}, u32[]{:S(2)}, u32[]{:S(2)}) collective-permute-start(bf16[48,768]{1,0:T(8,128)(2,1)} %get-tuple-element.56), channel_id=1, source_target_pairs={{0,2},{2,0},{4,6},{6,4},{1,3},{3,1},{5,7},{7,5},{8,10},{10,8},{12,... | collective-permute-start | bytes 221192 | tf_op jit(solution)/shard_map/ppermute | solution.py:43
  23.1 10.8 %collective-permute-start.1 = (bf16[2,1,2,64,768]{4,3,0,2,1:T(8,128)(2,1)S(1)}, bf16[2,1,2,64,768]{4,3,0,2,1:T(8,128)(2,1)S(1)}, u32[]{:S(2)}, u32[]{:S(2)}) collective-permute-start(bf16[2,1,2,64,768]{4,3,0,2,1:T(8,128)(2,1)S(1)} %pad_maximum_fusion.1), channel_id=1, source_target_pairs={{0,2},{2,0},{4,6},{6,4},{1,3},{3,1},{5,7},{7,5},{8,10},{10,8},{12,... | collective-permute-start | bytes 1179656 | tf_op jit(solution)/shard_map/ppermute | solution.py:43
  33.9 8.0 %collective-permute-start.4 = (bf16[48,768]{1,0:T(8,128)(2,1)S(1)}, bf16[48,768]{1,0:T(8,128)(2,1)S(1)}, u32[]{:S(2)}, u32[]{:S(2)}) collective-permute-start(bf16[48,768]{1,0:T(8,128)(2,1)S(1)} %copy-done.30), channel_id=1, source_target_pairs={{0,4},{2,6},{4,0},{6,2},{1,5},{3,7},{5,1},{7,3},{8,12},{10,14},{12... | collective-permute-start | bytes 221192 | tf_op jit(solution)/shard_map/ppermute | solution.py:43
  34.6 21.9 %copy-start.1 = (bf16[2,1,4,64,768]{4,3,2,0,1:T(8,128)(2,1)}, bf16[2,1,4,64,768]{4,3,2,0,1:T(8,128)(2,1)S(1)}, u32[]{:S(2)}) copy-start(bf16[2,1,4,64,768]{4,3,2,0,1:T(8,128)(2,1)S(1)} %copy.44) | copy-start | bytes 2359300
  34.6 21.1 %collective-permute-start.2 = (bf16[2,1,256,768]{3,2,1,0:T(8,128)(2,1)S(1)}, bf16[2,1,256,768]{3,2,1,0:T(8,128)(2,1)S(1)}, u32[]{:S(2)}, u32[]{:S(2)}) collective-permute-start(bf16[2,1,256,768]{3,2,1,0:T(8,128)(2,1)S(1)} %bitcast.48), channel_id=1, source_target_pairs={{0,1},{1,0},{2,3},{3,2},{4,5},{5,4},{6,7},{7,6},{8,9},{9,8},{10,11... | collective-permute-start | bytes 2359304 | tf_op jit(solution)/shard_map/ppermute | solution.py:43
  34.8 9.6 %collective-permute-start.5 = (bf16[48,768]{1,0:T(8,128)(2,1)S(1)}, bf16[48,768]{1,0:T(8,128)(2,1)S(1)}, u32[]{:S(2)}, u32[]{:S(2)}) collective-permute-start(bf16[48,768]{1,0:T(8,128)(2,1)S(1)} %copy-done.29), channel_id=1, source_target_pairs={{0,6},{2,4},{4,2},{6,0},{1,7},{3,5},{5,3},{7,1},{8,14},{10,12},{12... | collective-permute-start | bytes 221192 | tf_op jit(solution)/shard_map/ppermute | solution.py:43
  36.9 19.5 %copy-start.16 = (bf16[192,768]{1,0:T(8,128)(2,1)}, bf16[192,768]{1,0:T(8,128)(2,1)S(1)}, u32[]{:S(2)}) copy-start(bf16[192,768]{1,0:T(8,128)(2,1)S(1)} %constant_dynamic-update-slice_fusion.4.refs_2_) | copy-start | bytes 884740
  36.9 9.9 %collective-permute-start.12 = (bf16[192,768]{1,0:T(8,128)(2,1)S(1)}, bf16[192,768]{1,0:T(8,128)(2,1)S(1)}, u32[]{:S(2)}, u32[]{:S(2)}) collective-permute-start(bf16[192,768]{1,0:T(8,128)(2,1)S(1)} %constant_dynamic-update-slice_fusion.4.refs_2_), channel_id=1, source_target_pairs={{0,8},{8,0},{16,24},{24,16},{1,9},{9,1},{17,25},{25,17},{2,10},{10... | collective-permute-start | bytes 884744 | tf_op jit(solution)/shard_map/ppermute | solution.py:43
  38.5 15.2 %collective-permute-start.13 = (bf16[192,768]{1,0:T(8,128)(2,1)S(1)}, bf16[192,768]{1,0:T(8,128)(2,1)S(1)}, u32[]{:S(2)}, u32[]{:S(2)}) collective-permute-start(bf16[192,768]{1,0:T(8,128)(2,1)S(1)} %constant_dynamic-update-slice_fusion.4.refs_2_), channel_id=1, source_target_pairs={{0,16},{8,24},{16,0},{24,8},{1,17},{9,25},{17,1},{25,9},{2,18},{10... | collective-permute-start | bytes 884744 | tf_op jit(solution)/shard_map/ppermute | solution.py:43
  41.9 13.8 %collective-permute-start.14 = (bf16[192,768]{1,0:T(8,128)(2,1)S(1)}, bf16[192,768]{1,0:T(8,128)(2,1)S(1)}, u32[]{:S(2)}, u32[]{:S(2)}) collective-permute-start(bf16[192,768]{1,0:T(8,128)(2,1)S(1)} %constant_dynamic-update-slice_fusion.4.refs_2_), channel_id=1, source_target_pairs={{0,24},{8,16},{16,8},{24,0},{1,25},{9,17},{17,9},{25,1},{2,26},{10... | collective-permute-start | bytes 884744 | tf_op jit(solution)/shard_map/ppermute | solution.py:43
  44.4 20.4 %copy-start.15 = (bf16[192,768]{1,0:T(8,128)(2,1)}, bf16[192,768]{1,0:T(8,128)(2,1)S(1)}, u32[]{:S(2)}) copy-start(bf16[192,768]{1,0:T(8,128)(2,1)S(1)} %constant_dynamic-update-slice_fusion.refs_2_) | copy-start | bytes 884740
  44.4 20.4 %collective-permute-start.6 = (bf16[192,768]{1,0:T(8,128)(2,1)S(1)}, bf16[192,768]{1,0:T(8,128)(2,1)S(1)}, u32[]{:S(2)}, u32[]{:S(2)}) collective-permute-start(bf16[192,768]{1,0:T(8,128)(2,1)S(1)} %constant_dynamic-update-slice_fusion.refs_2_), channel_id=1, source_target_pairs={{0,8},{8,0},{16,24},{24,16},{1,9},{9,1},{17,25},{25,17},{2,10},{10... | collective-permute-start | bytes 884744 | tf_op jit(solution)/shard_map/ppermute | solution.py:43
  46.9 9.6 %copy-start.25 = (bf16[192,768]{1,0:T(8,128)(2,1)}, bf16[192,768]{1,0:T(8,128)(2,1)S(1)}, u32[]{:S(2)}) copy-start(bf16[192,768]{1,0:T(8,128)(2,1)S(1)} %collective-permute-done.12.refs_3_) | copy-start | bytes 884740
  46.9 19.5 %collective-permute-start.7 = (bf16[192,768]{1,0:T(8,128)(2,1)S(1)}, bf16[192,768]{1,0:T(8,128)(2,1)}, u32[]{:S(2)}, u32[]{:S(2)}) collective-permute-start(bf16[192,768]{1,0:T(8,128)(2,1)S(1)} %constant_dynamic-update-slice_fusion.refs_2_), channel_id=1, source_target_pairs={{0,16},{8,24},{16,0},{24,8},{1,17},{9,25},{17,1},{25,9},{2,18},{10... | collective-permute-start | bytes 884744 | tf_op jit(solution)/shard_map/ppermute | solution.py:43
  53.8 12.7 %collective-permute-start.8 = (bf16[192,768]{1,0:T(8,128)(2,1)S(1)}, bf16[192,768]{1,0:T(8,128)(2,1)}, u32[]{:S(2)}, u32[]{:S(2)}) collective-permute-start(bf16[192,768]{1,0:T(8,128)(2,1)S(1)} %constant_dynamic-update-slice_fusion.refs_2_), channel_id=1, source_target_pairs={{0,24},{8,16},{16,8},{24,0},{1,25},{9,17},{17,9},{25,1},{2,26},{10... | collective-permute-start | bytes 884744 | tf_op jit(solution)/shard_map/ppermute | solution.py:43
  74.3 3.7 %collective-permute-start.15 = (f32[2,1,256,768]{3,2,1,0:T(8,128)}, f32[2,1,256,768]{3,2,1,0:T(8,128)S(1)}, u32[]{:S(2)}, u32[]{:S(2)}) collective-permute-start(f32[2,1,256,768]{3,2,1,0:T(8,128)} %get-tuple-element.66), channel_id=1, source_target_pairs={{0,1},{1,0},{2,3},{3,2},{4,5},{5,4},{6,7},{7,6},{8,9},{9,8},{10,11... | collective-permute-start | bytes 4718600 | tf_op jit(solution)/shard_map/ppermute | solution.py:43
  78.0 2.9 %copy-start.23 = (bf16[208,768]{1,0:T(8,128)(2,1)S(1)}, bf16[208,768]{1,0:T(8,128)(2,1)}, u32[]{:S(2)}) copy-start(bf16[208,768]{1,0:T(8,128)(2,1)} %get-tuple-element.68) | copy-start | bytes 958468
  78.0 4.7 %copy-start.22 = (bf16[208,768]{1,0:T(8,128)(2,1)S(1)}, bf16[208,768]{1,0:T(8,128)(2,1)}, u32[]{:S(2)}) copy-start(bf16[208,768]{1,0:T(8,128)(2,1)} %get-tuple-element.69) | copy-start | bytes 958468
  78.0 5.0 %copy-start.21 = (bf16[208,768]{1,0:T(8,128)(2,1)S(1)}, bf16[208,768]{1,0:T(8,128)(2,1)}, u32[]{:S(2)}) copy-start(bf16[208,768]{1,0:T(8,128)(2,1)} %get-tuple-element.70) | copy-start | bytes 958468
  79.7 18.9 %copy-start.24 = (bf16[192,768]{1,0:T(8,128)(2,1)S(1)}, bf16[192,768]{1,0:T(8,128)(2,1)}, u32[]{:S(2)}) copy-start(bf16[192,768]{1,0:T(8,128)(2,1)} %get-tuple-element.81) | copy-start | bytes 884740
  79.8 11.2 %collective-permute-start.16 = (bf16[2,1,2,64,768]{4,3,2,1,0:T(8,128)(2,1)S(1)}, bf16[2,1,2,64,768]{4,3,2,1,0:T(8,128)(2,1)S(1)}, u32[]{:S(2)}, u32[]{:S(2)}) collective-permute-start(bf16[2,1,2,64,768]{4,3,2,1,0:T(8,128)(2,1)S(1)} %split.26), channel_id=1, source_target_pairs={{0,2},{2,0},{4,6},{6,4},{1,3},{3,1},{5,7},{7,5},{8,10},{10,8},{12,... | collective-permute-start | bytes 1179656 | tf_op jit(solution)/shard_map/ppermute | solution.py:43
  80.9 13.1 %collective-permute-start.20 = (bf16[208,768]{1,0:T(8,128)(2,1)S(1)}, bf16[208,768]{1,0:T(8,128)(2,1)S(1)}, u32[]{:S(2)}, u32[]{:S(2)}) collective-permute-start(bf16[208,768]{1,0:T(8,128)(2,1)S(1)} %copy-done.23), channel_id=1, source_target_pairs={{0,8},{8,0},{16,24},{24,16},{1,9},{9,1},{17,25},{25,17},{2,10},{10... | collective-permute-start | bytes 958472 | tf_op jit(solution)/shard_map/ppermute | solution.py:43
  82.7 16.0 %collective-permute-start.21 = (bf16[208,768]{1,0:T(8,128)(2,1)S(1)}, bf16[208,768]{1,0:T(8,128)(2,1)S(1)}, u32[]{:S(2)}, u32[]{:S(2)}) collective-permute-start(bf16[208,768]{1,0:T(8,128)(2,1)S(1)} %copy-done.22), channel_id=1, source_target_pairs={{0,16},{8,24},{16,0},{24,8},{1,17},{9,25},{17,1},{25,9},{2,18},{10... | collective-permute-start | bytes 958472 | tf_op jit(solution)/shard_map/ppermute | solution.py:43
  83.0 16.2 %collective-permute-start.22 = (bf16[208,768]{1,0:T(8,128)(2,1)S(1)}, bf16[208,768]{1,0:T(8,128)(2,1)S(1)}, u32[]{:S(2)}, u32[]{:S(2)}) collective-permute-start(bf16[208,768]{1,0:T(8,128)(2,1)S(1)} %copy-done.21), channel_id=1, source_target_pairs={{0,24},{8,16},{16,8},{24,0},{1,25},{9,17},{17,9},{25,1},{2,26},{10... | collective-permute-start | bytes 958472 | tf_op jit(solution)/shard_map/ppermute | solution.py:43
  91.1 12.3 %collective-permute-start.17 = (bf16[2,1,1,64,768]{4,3,2,1,0:T(8,128)(2,1)S(1)}, bf16[2,1,1,64,768]{4,3,2,1,0:T(8,128)(2,1)S(1)}, u32[]{:S(2)}, u32[]{:S(2)}) collective-permute-start(bf16[2,1,1,64,768]{4,3,2,1,0:T(8,128)(2,1)S(1)} %split.27), channel_id=1, source_target_pairs={{0,4},{2,6},{4,0},{6,2},{1,5},{3,7},{5,1},{7,3},{8,12},{10,14},{12... | collective-permute-start | bytes 589832 | tf_op jit(solution)/shard_map/ppermute | solution.py:43
  92.2 12.6 %collective-permute-start.27 = (bf16[192,768]{1,0:T(8,128)(2,1)}, bf16[192,768]{1,0:T(8,128)(2,1)S(1)}, u32[]{:S(2)}, u32[]{:S(2)}) collective-permute-start(bf16[192,768]{1,0:T(8,128)(2,1)} %get-tuple-element.79), channel_id=1, source_target_pairs={{0,8},{8,0},{16,24},{24,16},{1,9},{9,1},{17,25},{25,17},{2,10},{10... | collective-permute-start | bytes 884744 | tf_op jit(solution)/shard_map/ppermute | solution.py:43
  94.0 5.2 %copy-start.2 = (bf16[208,768]{1,0:T(8,128)(2,1)}, bf16[208,768]{1,0:T(8,128)(2,1)S(1)}, u32[]{:S(2)}) copy-start(bf16[208,768]{1,0:T(8,128)(2,1)S(1)} %collective-permute-done.20.refs_1_) | copy-start | bytes 958468
  94.0 17.2 %collective-permute-start.28 = (bf16[192,768]{1,0:T(8,128)(2,1)}, bf16[192,768]{1,0:T(8,128)(2,1)S(1)}, u32[]{:S(2)}, u32[]{:S(2)}) collective-permute-start(bf16[192,768]{1,0:T(8,128)(2,1)} %get-tuple-element.80), channel_id=1, source_target_pairs={{0,16},{8,24},{16,0},{24,8},{1,17},{9,25},{17,1},{25,9},{2,18},{10... | collective-permute-start | bytes 884744 | tf_op jit(solution)/shard_map/ppermute | solution.py:43
  98.6 12.5 %collective-permute-start.29 = (bf16[192,768]{1,0:T(8,128)(2,1)S(1)}, bf16[192,768]{1,0:T(8,128)(2,1)S(1)}, u32[]{:S(2)}, u32[]{:S(2)}) collective-permute-start(bf16[192,768]{1,0:T(8,128)(2,1)S(1)} %copy-done.24), channel_id=1, source_target_pairs={{0,24},{8,16},{16,8},{24,0},{1,25},{9,17},{17,9},{25,1},{2,26},{10... | collective-permute-start | bytes 884744 | tf_op jit(solution)/shard_map/ppermute | solution.py:43
  102.2 13.1 %collective-permute-start.23 = (bf16[64,768]{1,0:T(8,128)(2,1)}, bf16[64,768]{1,0:T(8,128)(2,1)S(1)}, u32[]{:S(2)}, u32[]{:S(2)}) collective-permute-start(bf16[64,768]{1,0:T(8,128)(2,1)} %get-tuple-element.72), channel_id=1, source_target_pairs={{0,2},{2,0},{4,6},{6,4},{1,3},{3,1},{5,7},{7,5},{8,10},{10,8},{12,... | collective-permute-start | bytes 294920 | tf_op jit(solution)/shard_map/ppermute | solution.py:43
  103.4 13.0 %collective-permute-start.24 = (bf16[64,768]{1,0:T(8,128)(2,1)}, bf16[64,768]{1,0:T(8,128)(2,1)S(1)}, u32[]{:S(2)}, u32[]{:S(2)}) collective-permute-start(bf16[64,768]{1,0:T(8,128)(2,1)} %get-tuple-element.73), channel_id=1, source_target_pairs={{0,4},{2,6},{4,0},{6,2},{1,5},{3,7},{5,1},{7,3},{8,12},{10,14},{12... | collective-permute-start | bytes 294920 | tf_op jit(solution)/shard_map/ppermute | solution.py:43
  104.9 6.3 %copy-start.5 = (bf16[192,768]{1,0:T(8,128)(2,1)}, bf16[192,768]{1,0:T(8,128)(2,1)S(1)}, u32[]{:S(2)}) copy-start(bf16[192,768]{1,0:T(8,128)(2,1)S(1)} %collective-permute-done.27.refs_1_) | copy-start | bytes 884740
  104.9 13.7 %collective-permute-start.25 = (bf16[64,768]{1,0:T(8,128)(2,1)}, bf16[64,768]{1,0:T(8,128)(2,1)S(1)}, u32[]{:S(2)}, u32[]{:S(2)}) collective-permute-start(bf16[64,768]{1,0:T(8,128)(2,1)} %get-tuple-element.74), channel_id=1, source_target_pairs={{0,6},{2,4},{4,2},{6,0},{1,7},{3,5},{5,3},{7,1},{8,14},{10,12},{12... | collective-permute-start | bytes 294920 | tf_op jit(solution)/shard_map/ppermute | solution.py:43
  111.2 17.8 %collective-permute-start.18 = (bf16[1,64,768]{2,1,0:T(8,128)(2,1)S(1)}, bf16[1,64,768]{2,1,0:T(8,128)(2,1)S(1)}, u32[]{:S(2)}, u32[]{:S(2)}) collective-permute-start(bf16[1,64,768]{2,1,0:T(8,128)(2,1)S(1)} %get-tuple-element.103), channel_id=1, source_target_pairs={{0,1},{1,0},{2,3},{3,2},{4,5},{5,4},{6,7},{7,6},{8,9},{9,8},{10,11... | collective-permute-start | bytes 294920 | tf_op jit(solution)/shard_map/ppermute | solution.py:43
  114.2 7.0 %collective-permute-start.30 = (bf16[48,768]{1,0:T(8,128)(2,1)}, bf16[48,768]{1,0:T(8,128)(2,1)S(1)}, u32[]{:S(2)}, u32[]{:S(2)}) collective-permute-start(bf16[48,768]{1,0:T(8,128)(2,1)} %get-tuple-element.83), channel_id=1, source_target_pairs={{0,2},{2,0},{4,6},{6,4},{1,3},{3,1},{5,7},{7,5},{8,10},{10,8},{12,... | collective-permute-start | bytes 221192 | tf_op jit(solution)/shard_map/ppermute | solution.py:43
  115.4 3.2 %copy-start.8 = (bf16[64,768]{1,0:T(8,128)(2,1)}, bf16[64,768]{1,0:T(8,128)(2,1)S(1)}, u32[]{:S(2)}) copy-start(bf16[64,768]{1,0:T(8,128)(2,1)S(1)} %collective-permute-done.23.refs_1_) | copy-start | bytes 294916
  115.4 9.1 %collective-permute-start.31 = (bf16[48,768]{1,0:T(8,128)(2,1)}, bf16[48,768]{1,0:T(8,128)(2,1)S(1)}, u32[]{:S(2)}, u32[]{:S(2)}) collective-permute-start(bf16[48,768]{1,0:T(8,128)(2,1)} %get-tuple-element.84), channel_id=1, source_target_pairs={{0,4},{2,6},{4,0},{6,2},{1,5},{3,7},{5,1},{7,3},{8,12},{10,14},{12... | collective-permute-start | bytes 221192 | tf_op jit(solution)/shard_map/ppermute | solution.py:43
  116.4 8.1 %collective-permute-start.32 = (bf16[48,768]{1,0:T(8,128)(2,1)}, bf16[48,768]{1,0:T(8,128)(2,1)S(1)}, u32[]{:S(2)}, u32[]{:S(2)}) collective-permute-start(bf16[48,768]{1,0:T(8,128)(2,1)} %get-tuple-element.85), channel_id=1, source_target_pairs={{0,6},{2,4},{4,2},{6,0},{1,7},{3,5},{5,3},{7,1},{8,14},{10,12},{12... | collective-permute-start | bytes 221192 | tf_op jit(solution)/shard_map/ppermute | solution.py:43
  121.2 5.8 %collective-permute-start.26 = (f32[24,128]{1,0:T(8,128)}, f32[24,128]{1,0:T(8,128)S(1)}, u32[]{:S(2)}, u32[]{:S(2)}) collective-permute-start(f32[24,128]{1,0:T(8,128)} %get-tuple-element.75.refs_0_), channel_id=1, source_target_pairs={{0,1},{1,0},{2,3},{3,2},{4,5},{5,4},{6,7},{7,6},{8,9},{9,8},{10,11... | collective-permute-start | bytes 36872 | tf_op jit(solution)/shard_map/ppermute | solution.py:43
  121.2 3.3 %copy-start.12 = (bf16[48,768]{1,0:T(8,128)(2,1)}, bf16[48,768]{1,0:T(8,128)(2,1)S(1)}, u32[]{:S(2)}) copy-start(bf16[48,768]{1,0:T(8,128)(2,1)S(1)} %collective-permute-done.30.refs_1_) | copy-start | bytes 221188
  128.9 1.4 %collective-permute-start.19 = (f32[1,64,768]{2,1,0:T(8,128)S(1)}, f32[1,64,768]{2,1,0:T(8,128)S(1)}, u32[]{:S(2)}, u32[]{:S(2)}) collective-permute-start(f32[1,64,768]{2,1,0:T(8,128)S(1)} %get-tuple-element.102), channel_id=1, source_target_pairs={{0,1},{1,0},{2,3},{3,2},{4,5},{5,4},{6,7},{7,6},{8,9},{9,8},{10,11... | collective-permute-start | bytes 589832 | tf_op jit(solution)/shard_map/ppermute | solution.py:43
  (16 other events, 19.8 us)

commit v5 on v4

--- a/solution.py
+++ b/solution.py
@@ -458,14 +458,6 @@
     put_row(up_bias_out, jnp.concatenate(swapped(ups, ctx_at), axis=1))
 
 
-def gains_end_kernel(count, *refs):
-    parts, outs = refs[:count], refs[count : count + 4]
-    total = tree_sum([part[...] for part in parts])
-    rows = total.shape[0] // 4
-    for i, out in enumerate(outs):
-        out[...] = total[i * rows : (i + 1) * rows]
-
-
 def on_device(
     tokens,
     group_order,
@@ -629,7 +621,8 @@
     late_pieces = scatter_weights(late_grads)
     block_half = own_tokens.astype(f32) + branches + (dense_bias + down_bias)
     block_out = both_cores(block_half.astype(bf16))
-    own_centred, own_inverse = normed_rows(own_tokens.astype(f32))
+    later_tokens, _ = lax.optimization_barrier((own_tokens, chunks))
+    own_centred, own_inverse = normed_rows(later_tokens.astype(f32))
     inner = (
         inner
         - jnp.mean(inner, axis=-1, keepdims=True)
@@ -656,13 +649,7 @@
             ],
         )(*late_pieces)
     )
-    gains = [
-        part.reshape(width)
-        for part in local_kernel(
-            functools.partial(gains_end_kernel, tp_count),
-            [shaped((width // LANES, LANES), f32)] * 4,
-        )(*spread(gains, "tp"))
-    ]
+    gains = sum(spread(gains, "tp")).reshape(4, width)
     return (
         block_out,
         tokens_grad,

time: 132 us -> 135 us (1.023)
  starting transfers between devices: 37.5 us -> 40.8 us
  waiting for transfers between devices: 47.4 us -> 49.9 us
    ppermute x33, starting transfers between devices: 37.5 us -> 40.8 us  [swap(): lax.ppermute(value, axis, [(i, i ^ bit) for i in range(lax.axis_size(axis...]
    ppermute x33, waiting for transfers between devices: 47.4 us -> 49.9 us  [swap(): lax.ppermute(value, axis, [(i, i ^ bit) for i in range(lax.axis_size(axis...]
    unnamed x68 -> x56, local copies, waits for them, and re-layouts: 6.11 us -> 4.58 us
  transfers between devices with their start and end apart: 33 -> 33, of which waited for: 13 -> 14; matrix products, arithmetic and copies ran while one was open for 7% -> 8% of each run, Pallas kernels for 14% -> 13%
where the time goes in v5:
time: 135 us
  waiting for transfers between devices  49.9 us (37%)
  starting transfers between devices  40.8 us (30%)
  Pallas kernels  27.1 us (20%)
  other arithmetic  9.64 us (7%)
  local copies, waits for them, and re-layouts  6.15 us (5%)
    ppermute x33, waiting for transfers between devices, swap(): lax.ppermute(value, axis, [(i, i ^ bit) for i in range(lax.axis_size(axis...  49.9 us
    ppermute x33, starting transfers between devices, swap(): lax.ppermute(value, axis, [(i, i ^ bit) for i in range(lax.axis_size(axis...  40.8 us
    pallas_call x1, Pallas kernels, on_device(): local_kernel(functools.partial(mlp_kernel, fsdp_count, tp_count, near, he...  7.97 us
    pallas_call x1, Pallas kernels, on_device(): local_kernel(functools.partial(attention_kernel, fsdp_count, tp_count, ne...  7.44 us
    unnamed x56, local copies, waits for them, and re-layouts  4.58 us
    pallas_call x2, Pallas kernels, scatter_weights(): local_kernel(functools.partial(sum_blocks_kernel, fsdp_count, ctx_count,...  4.47 us
  transfers between devices with their start and end apart: 33, of which 14 were waited for; matrix products, arithmetic and copies ran while one was open for 8% of the time, Pallas kernels for 13%

profile of v5, /device:TPU:0, one launch (start us, length us, event | category | flops | bytes accessed | tf_op | source)
XLA Modules:
  0.0 134.7 jit_solution(2192933292472481354)
XLA Ops:
  0.7 1.7 %shard_map.255 = (bf16[48,768]{1,0:T(8,128)(2,1)}, bf16[48,768]{1,0:T(8,128)(2,1)}) custom-call(bf16[48,1152]{1,0:T(8,128)(2,1)} %qkv_ref.1, bf16[48,384]{1,0:T(8,128)(2,1)} %bitcast.60), custom_call_target="tpu_custom_call" | custom-call | tf_op jit(solution)/shard_map/pallas_call | solution.py:499
  2.4 3.1 %collective-permute-start.9 = (bf16[48,768]{1,0:T(8,128)(2,1)}, bf16[48,768]{1,0:T(8,128)(2,1)S(1)}, u32[]{:S(2)}, u32[]{:S(2)}) collective-permute-start(bf16[48,768]{1,0:T(8,128)(2,1)} %get-tuple-element.57), channel_id=1, source_target_pairs={{0,2},{2,0},{4,6},{6,4},{1,3},{3,1},{5,7},{7,5},{8,10},{10,8},{12,... | collective-permute-start | bytes 221192 | tf_op jit(solution)/shard_map/ppermute | solution.py:43
  5.4 2.5 %collective-permute-start.11 = (bf16[48,768]{1,0:T(8,128)(2,1)}, bf16[48,768]{1,0:T(8,128)(2,1)S(1)}, u32[]{:S(2)}, u32[]{:S(2)}) collective-permute-start(bf16[48,768]{1,0:T(8,128)(2,1)} %get-tuple-element.57), channel_id=1, source_target_pairs={{0,6},{2,4},{4,2},{6,0},{1,7},{3,5},{5,3},{7,1},{8,14},{10,12},{12... | collective-permute-start | bytes 221192 | tf_op jit(solution)/shard_map/ppermute | solution.py:43
  7.9 1.0 convert_bitcast_fusion
  8.9 1.0 fusion.22
  10.1 2.8 %collective-permute-start.10 = (bf16[48,768]{1,0:T(8,128)(2,1)}, bf16[48,768]{1,0:T(8,128)(2,1)S(1)}, u32[]{:S(2)}, u32[]{:S(2)}) collective-permute-start(bf16[48,768]{1,0:T(8,128)(2,1)} %get-tuple-element.56), channel_id=1, source_target_pairs={{0,4},{2,6},{4,0},{6,2},{1,5},{3,7},{5,1},{7,3},{8,12},{10,14},{12... | collective-permute-start | bytes 221192 | tf_op jit(solution)/shard_map/ppermute | solution.py:43
  12.9 1.7 %shard_map.254 = (bf16[48,768]{1,0:T(8,128)(2,1)}, bf16[48,768]{1,0:T(8,128)(2,1)}, bf16[48,768]{1,0:T(8,128)(2,1)}, bf16[48,768]{1,0:T(8,128)(2,1)}) custom-call(bf16[48,1536]{1,0:T(8,128)(2,1)} %up_ref.1, bf16[48,1536]{1,0:T(8,128)(2,1)} %bitcast.59), custom_call_target="tpu_custom_call" | custom-call | tf_op jit(solution)/shard_map/pallas_call | solution.py:503
  16.3 0.9 constant_dynamic-update-slice_fusion.7
  17.2 5.8 %collective-permute-done = bf16[2,1,1,64,768]{4,3,0,2,1:T(8,128)(2,1)S(1)} collective-permute-done((bf16[2,1,1,64,768]{4,3,0,2,1:T(8,128)(2,1)S(1)}, bf16[2,1,1,64,768]{4,3,0,2,1:T(8,128)(2,1)S(1)}, u32[]{:S(2)}, u32[]{:S(2)}) %collective-permute-start) | collective-permute-done | bytes 196640 | tf_op jit(solution)/shard_map/ppermute | solution.py:43
  23.2 0.8 copy.45.refs_11_
  24.6 1.2 fusion.12
  25.9 7.9 %collective-permute-done.1 = bf16[2,1,2,64,768]{4,3,0,2,1:T(8,128)(2,1)S(1)} collective-permute-done((bf16[2,1,2,64,768]{4,3,0,2,1:T(8,128)(2,1)S(1)}, bf16[2,1,2,64,768]{4,3,0,2,1:T(8,128)(2,1)S(1)}, u32[]{:S(2)}, u32[]{:S(2)}) %collective-permute-start.1) | collective-permute-done | bytes 393248 | tf_op jit(solution)/shard_map/ppermute | solution.py:43
  34.7 2.1 %collective-permute-start.5 = (bf16[48,768]{1,0:T(8,128)(2,1)S(1)}, bf16[48,768]{1,0:T(8,128)(2,1)S(1)}, u32[]{:S(2)}, u32[]{:S(2)}) collective-permute-start(bf16[48,768]{1,0:T(8,128)(2,1)S(1)} %copy-done.23), channel_id=1, source_target_pairs={{0,6},{2,4},{4,2},{6,0},{1,7},{3,5},{5,3},{7,1},{8,14},{10,12},{12... | collective-permute-start | bytes 221192 | tf_op jit(solution)/shard_map/ppermute | solution.py:43
  36.8 1.6 %collective-permute-start.12 = (bf16[192,768]{1,0:T(8,128)(2,1)S(1)}, bf16[192,768]{1,0:T(8,128)(2,1)S(1)}, u32[]{:S(2)}, u32[]{:S(2)}) collective-permute-start(bf16[192,768]{1,0:T(8,128)(2,1)S(1)} %constant_dynamic-update-slice_fusion.4.refs_2_), channel_id=1, source_target_pairs={{0,8},{8,0},{16,24},{24,16},{1,9},{9,1},{17,25},{25,17},{2,10},{10... | collective-permute-start | bytes 884744 | tf_op jit(solution)/shard_map/ppermute | solution.py:43
  38.4 1.5 %collective-permute-start.13 = (bf16[192,768]{1,0:T(8,128)(2,1)S(1)}, bf16[192,768]{1,0:T(8,128)(2,1)S(1)}, u32[]{:S(2)}, u32[]{:S(2)}) collective-permute-start(bf16[192,768]{1,0:T(8,128)(2,1)S(1)} %constant_dynamic-update-slice_fusion.4.refs_2_), channel_id=1, source_target_pairs={{0,16},{8,24},{16,0},{24,8},{1,17},{9,25},{17,1},{25,9},{2,18},{10... | collective-permute-start | bytes 884744 | tf_op jit(solution)/shard_map/ppermute | solution.py:43
  39.9 1.8 %collective-permute-done.4 = bf16[48,768]{1,0:T(8,128)(2,1)S(1)} collective-permute-done((bf16[48,768]{1,0:T(8,128)(2,1)S(1)}, bf16[48,768]{1,0:T(8,128)(2,1)S(1)}, u32[]{:S(2)}, u32[]{:S(2)}) %collective-permute-start.4) | collective-permute-done | bytes 73760 | tf_op jit(solution)/shard_map/ppermute | solution.py:43
  41.7 2.4 %collective-permute-start.14 = (bf16[192,768]{1,0:T(8,128)(2,1)S(1)}, bf16[192,768]{1,0:T(8,128)(2,1)S(1)}, u32[]{:S(2)}, u32[]{:S(2)}) collective-permute-start(bf16[192,768]{1,0:T(8,128)(2,1)S(1)} %constant_dynamic-update-slice_fusion.4.refs_2_), channel_id=1, source_target_pairs={{0,24},{8,16},{16,8},{24,0},{1,25},{9,17},{17,9},{25,1},{2,26},{10... | collective-permute-start | bytes 884744 | tf_op jit(solution)/shard_map/ppermute | solution.py:43
  44.8 2.0 %collective-permute-done.12.refs_3_ = bf16[192,768]{1,0:T(8,128)(2,1)S(1)} collective-permute-done((bf16[192,768]{1,0:T(8,128)(2,1)S(1)}, bf16[192,768]{1,0:T(8,128)(2,1)S(1)}, u32[]{:S(2)}, u32[]{:S(2)}) %collective-permute-start.12) | collective-permute-done | bytes 294944 | tf_op jit(solution)/shard_map/ppermute | solution.py:43
  46.8 1.5 %collective-permute-start.7 = (bf16[192,768]{1,0:T(8,128)(2,1)S(1)}, bf16[192,768]{1,0:T(8,128)(2,1)}, u32[]{:S(2)}, u32[]{:S(2)}) collective-permute-start(bf16[192,768]{1,0:T(8,128)(2,1)S(1)} %constant_dynamic-update-slice_fusion.refs_2_), channel_id=1, source_target_pairs={{0,16},{8,24},{16,0},{24,8},{1,17},{9,25},{17,1},{25,9},{2,18},{10... | collective-permute-start | bytes 884744 | tf_op jit(solution)/shard_map/ppermute | solution.py:43
  48.3 5.3 %collective-permute-done.13.refs_4_ = bf16[192,768]{1,0:T(8,128)(2,1)S(1)} collective-permute-done((bf16[192,768]{1,0:T(8,128)(2,1)S(1)}, bf16[192,768]{1,0:T(8,128)(2,1)S(1)}, u32[]{:S(2)}, u32[]{:S(2)}) %collective-permute-start.13) | collective-permute-done | bytes 294944 | tf_op jit(solution)/shard_map/ppermute | solution.py:43
  53.6 1.3 collective-permute-start.8
  56.4 0.9 copy-done.18
  57.2 7.4 %shard_map.256 = (bf16[256,256]{1,0:T(8,128)(2,1)}, bf16[256,640]{1,0:T(8,128)(2,1)}, bf16[768,768]{1,0:T(8,128)(2,1)}, f32[1,768]{1,0:T(1,128)}, f32[192,768]{1...) custom-call(bf16[2,1,256,768]{3,2,1,0:T(8,128)(2,1)} %bitcast.57, ...), custom_call_target="tpu_custom_call" | custom-call | flops 2415919104 | bytes 3145728 | tf_op jit(solution)/shard_map/pallas_call | solution.py:547
  64.7 1.6 %collective-permute-done.7.refs_4_ = bf16[192,768]{1,0:T(8,128)(2,1)} collective-permute-done((bf16[192,768]{1,0:T(8,128)(2,1)S(1)}, bf16[192,768]{1,0:T(8,128)(2,1)}, u32[]{:S(2)}, u32[]{:S(2)}) %collective-permute-start.7) | collective-permute-done | bytes 294944 | tf_op jit(solution)/shard_map/ppermute | solution.py:43
  66.3 8.0 %shard_map.257 = (f32[2,1,256,768]{3,2,1,0:T(8,128)}, f32[2,1,256,768]{3,2,1,0:T(8,128)}, f32[208,768]{1,0:T(8,128)}, bf16[208,768]{1,0:T(8,128)(2,1)}, bf16[208...) custom-call(bf16[2,1,256,768]{3,2,1,0:T(8,128)(2,1)} %bitcast.58, bf16[2,1,256,768]{3,2,1,0:T(8,128)(2,1)} %copy-done.18, ...), custom_call_target="tpu_custom_call" | custom-call | flops 1811939328 | bytes 6291456 | tf_op jit(solution)/shard_map/pallas_call | solution.py:580
  74.4 1.7 %collective-permute-start.20 = (bf16[208,768]{1,0:T(8,128)(2,1)}, bf16[208,768]{1,0:T(8,128)(2,1)S(1)}, u32[]{:S(2)}, u32[]{:S(2)}) collective-permute-start(bf16[208,768]{1,0:T(8,128)(2,1)} %get-tuple-element.66), channel_id=1, source_target_pairs={{0,8},{8,0},{16,24},{24,16},{1,9},{9,1},{17,25},{25,17},{2,10},{10... | collective-permute-start | bytes 958472 | tf_op jit(solution)/shard_map/ppermute | solution.py:43
  76.6 1.6 %collective-permute-start.27 = (bf16[192,768]{1,0:T(8,128)(2,1)}, bf16[192,768]{1,0:T(8,128)(2,1)}, u32[]{:S(2)}, u32[]{:S(2)}) collective-permute-start(bf16[192,768]{1,0:T(8,128)(2,1)} %get-tuple-element.75), channel_id=1, source_target_pairs={{0,8},{8,0},{16,24},{24,16},{1,9},{9,1},{17,25},{25,17},{2,10},{10... | collective-permute-start | bytes 884744 | tf_op jit(solution)/shard_map/ppermute | solution.py:43
  78.7 1.5 %collective-permute-start.22 = (bf16[208,768]{1,0:T(8,128)(2,1)}, bf16[208,768]{1,0:T(8,128)(2,1)S(1)}, u32[]{:S(2)}, u32[]{:S(2)}) collective-permute-start(bf16[208,768]{1,0:T(8,128)(2,1)} %get-tuple-element.68), channel_id=1, source_target_pairs={{0,24},{8,16},{16,8},{24,0},{1,25},{9,17},{17,9},{25,1},{2,26},{10... | collective-permute-start | bytes 958472 | tf_op jit(solution)/shard_map/ppermute | solution.py:43
  80.2 1.6 %add.315 = f32[2,1,256,768]{3,2,1,0:T(8,128)S(1)} add(f32[2,1,256,768]{3,2,1,0:T(8,128)} %get-tuple-element.62, f32[2,1,256,768]{3,2,1,0:T(8,128)S(1)} %collective-permute-done.15) | non-fusion elementwise | flops 393216 | bytes 4718592 | tf_op jit(solution)/shard_map/add | solution.py:602
  81.8 3.2 %collective-permute-done.20.refs_1_ = bf16[208,768]{1,0:T(8,128)(2,1)S(1)} collective-permute-done((bf16[208,768]{1,0:T(8,128)(2,1)}, bf16[208,768]{1,0:T(8,128)(2,1)S(1)}, u32[]{:S(2)}, u32[]{:S(2)}) %collective-permute-start.20) | collective-permute-done | bytes 319520 | tf_op jit(solution)/shard_map/ppermute | solution.py:43
  85.1 0.8 collective-permute-start.16
  86.0 0.8 collective-permute-done.21.refs_2_
  86.8 1.3 collective-permute-start.29
  88.1 11.2 %collective-permute-done.22.refs_3_ = bf16[208,768]{1,0:T(8,128)(2,1)S(1)} collective-permute-done((bf16[208,768]{1,0:T(8,128)(2,1)}, bf16[208,768]{1,0:T(8,128)(2,1)S(1)}, u32[]{:S(2)}, u32[]{:S(2)}) %collective-permute-start.22) | collective-permute-done | bytes 319520 | tf_op jit(solution)/shard_map/ppermute | solution.py:43
  100.0 2.3 %shard_map.258 = (f32[64,768]{1,0:T(8,128)}, bf16[64,768]{1,0:T(8,128)(2,1)}, bf16[64,768]{1,0:T(8,128)(2,1)}, bf16[64,768]{1,0:T(8,128)(2,1)}) custom-call(f32[208,768]{1,0:T(8,128)} %get-tuple-element.65.refs_0_, bf16[208,768]{1,0:T(8,128)(2,1)} %copy-done.3, bf16[208,768]{1,0:T(8,128)(2,1)} %copy-done.4, bf16[208,768]{1,0:T(8,128)(2,1)} %copy-done.5), custom_call_target="tpu_custom_call" | custom-call | tf_op jit(solution)/shard_map/pallas_call | solution.py:614
  102.3 0.8 collective-permute-start.23
  103.1 1.5 %collective-permute-start.24 = (bf16[64,768]{1,0:T(8,128)(2,1)}, bf16[64,768]{1,0:T(8,128)(2,1)S(1)}, u32[]{:S(2)}, u32[]{:S(2)}) collective-permute-start(bf16[64,768]{1,0:T(8,128)(2,1)} %get-tuple-element.71), channel_id=1, source_target_pairs={{0,4},{2,6},{4,0},{6,2},{1,5},{3,7},{5,1},{7,3},{8,12},{10,14},{12... | collective-permute-start | bytes 294920 | tf_op jit(solution)/shard_map/ppermute | solution.py:43
  104.7 0.9 collective-permute-done.28.refs_2_
  105.6 1.8 %collective-permute-start.25 = (bf16[64,768]{1,0:T(8,128)(2,1)}, bf16[64,768]{1,0:T(8,128)(2,1)S(1)}, u32[]{:S(2)}, u32[]{:S(2)}) collective-permute-start(bf16[64,768]{1,0:T(8,128)(2,1)} %get-tuple-element.72), channel_id=1, source_target_pairs={{0,6},{2,4},{4,2},{6,0},{1,7},{3,5},{5,3},{7,1},{8,14},{10,12},{12... | collective-permute-start | bytes 294920 | tf_op jit(solution)/shard_map/ppermute | solution.py:43
  107.6 2.2 %shard_map.260 = (f32[48,768]{1,0:T(8,128)}, bf16[48,768]{1,0:T(8,128)(2,1)}, bf16[48,768]{1,0:T(8,128)(2,1)}, bf16[48,768]{1,0:T(8,128)(2,1)}) custom-call(f32[192,768]{1,0:T(8,128)} %get-tuple-element.74.refs_0_, bf16[192,768]{1,0:T(8,128)(2,1)} %collective-permute-done.27.refs_1_, bf16[192,768]{1,0:T(8,128)(2,1)} %collective-permute-done.28.refs_2_, ...), custom_call_target="tpu_custom_call" | custom-call | tf_op jit(solution)/shard_map/pallas_call | solution.py:614
  109.8 2.5 %collective-permute-start.31 = (bf16[48,768]{1,0:T(8,128)(2,1)}, bf16[48,768]{1,0:T(8,128)(2,1)S(1)}, u32[]{:S(2)}, u32[]{:S(2)}) collective-permute-start(bf16[48,768]{1,0:T(8,128)(2,1)} %get-tuple-element.80), channel_id=1, source_target_pairs={{0,4},{2,6},{4,0},{6,2},{1,5},{3,7},{5,1},{7,3},{8,12},{10,14},{12... | collective-permute-start | bytes 221192 | tf_op jit(solution)/shard_map/ppermute | solution.py:43
  112.3 1.8 %collective-permute-done.24.refs_2_ = bf16[64,768]{1,0:T(8,128)(2,1)S(1)} collective-permute-done((bf16[64,768]{1,0:T(8,128)(2,1)}, bf16[64,768]{1,0:T(8,128)(2,1)S(1)}, u32[]{:S(2)}, u32[]{:S(2)}) %collective-permute-start.24) | collective-permute-done | bytes 98336 | tf_op jit(solution)/shard_map/ppermute | solution.py:43
  114.1 1.6 %collective-permute-start.32 = (bf16[48,768]{1,0:T(8,128)(2,1)}, bf16[48,768]{1,0:T(8,128)(2,1)S(1)}, u32[]{:S(2)}, u32[]{:S(2)}) collective-permute-start(bf16[48,768]{1,0:T(8,128)(2,1)} %get-tuple-element.81), channel_id=1, source_target_pairs={{0,6},{2,4},{4,2},{6,0},{1,7},{3,5},{5,3},{7,1},{8,14},{10,12},{12... | collective-permute-start | bytes 221192 | tf_op jit(solution)/shard_map/ppermute | solution.py:43
  116.4 2.0 %shard_map.259 = (f32[48,1536]{1,0:T(8,128)}, f32[48,1536]{1,0:T(8,128)}, f32[24,128]{1,0:T(8,128)}, f32[6,128]{1,0:T(8,128)}, f32[6,128]{1,0:T(8,128)}, /*index=5*/f32[9,128]{1,0:T(8,128)}, f32[12,128]{1,0:T(8,128)}) custom-call(f32[64,768]{1,0:T(8,128)} %get-tuple-element.69.refs_0_, bf16[64,768]{1,0:T(8,128)(2,1)} %copy-done.6, ...), custom_call_target="tpu_custom_call" | custom-call | tf_op jit(solution)/shard_map/pallas_call | solution.py:637
  118.5 2.8 %collective-permute-start.17 = (bf16[2,1,1,64,768]{4,3,2,1,0:T(8,128)(2,1)S(1)}, bf16[2,1,1,64,768]{4,3,2,1,0:T(8,128)(2,1)S(1)}, u32[]{:S(2)}, u32[]{:S(2)}) collective-permute-start(bf16[2,1,1,64,768]{4,3,2,1,0:T(8,128)(2,1)S(1)} %split.27), channel_id=1, source_target_pairs={{0,4},{2,6},{4,0},{6,2},{1,5},{3,7},{5,1},{7,3},{8,12},{10,14},{12... | collective-permute-start | bytes 589832 | tf_op jit(solution)/shard_map/ppermute | solution.py:43
  122.0 1.8 %shard_map.261 = (f32[48,1152]{1,0:T(8,128)}, f32[48,384]{1,0:T(8,128)}) custom-call(f32[48,768]{1,0:T(8,128)} %get-tuple-element.78.refs_0_, bf16[48,768]{1,0:T(8,128)(2,1)} %copy-done.10, bf16[48,768]{1,0:T(8,128)(2,1)} %copy-done.11, bf16[48,768]{1,0:T(8,128)(2,1)} %copy-done.12), custom_call_target="tpu_custom_call" | custom-call | tf_op jit(solution)/shard_map/pallas_call | solution.py:632
  123.9 7.2 %collective-permute-done.17 = bf16[2,1,1,64,768]{4,3,2,1,0:T(8,128)(2,1)S(1)} collective-permute-done((bf16[2,1,1,64,768]{4,3,2,1,0:T(8,128)(2,1)S(1)}, bf16[2,1,1,64,768]{4,3,2,1,0:T(8,128)(2,1)S(1)}, u32[]{:S(2)}, u32[]{:S(2)}) %collective-permute-start.17) | collective-permute-done | bytes 196640 | tf_op jit(solution)/shard_map/ppermute | solution.py:43
  133.9 0.8 pad_maximum_fusion.2
  (126 shorter events, 11.9 us)
Async XLA Ops:
  0.6 23.3 %copy-start = (f32[2,64,768]{2,1,0:T(8,128)S(1)}, f32[2,64,768]{2,1,0:T(8,128)}, u32[]{:S(2)}) copy-start(f32[2,64,768]{2,1,0:T(8,128)} %param.29) | copy-start | bytes 1179652
  2.4 32.2 %collective-permute-start.9 = (bf16[48,768]{1,0:T(8,128)(2,1)}, bf16[48,768]{1,0:T(8,128)(2,1)S(1)}, u32[]{:S(2)}, u32[]{:S(2)}) collective-permute-start(bf16[48,768]{1,0:T(8,128)(2,1)} %get-tuple-element.57), channel_id=1, source_target_pairs={{0,2},{2,0},{4,6},{6,4},{1,3},{3,1},{5,7},{7,5},{8,10},{10,8},{12,... | collective-permute-start | bytes 221192 | tf_op jit(solution)/shard_map/ppermute | solution.py:43
  5.4 31.4 %collective-permute-start.11 = (bf16[48,768]{1,0:T(8,128)(2,1)}, bf16[48,768]{1,0:T(8,128)(2,1)S(1)}, u32[]{:S(2)}, u32[]{:S(2)}) collective-permute-start(bf16[48,768]{1,0:T(8,128)(2,1)} %get-tuple-element.57), channel_id=1, source_target_pairs={{0,6},{2,4},{4,2},{6,0},{1,7},{3,5},{5,3},{7,1},{8,14},{10,12},{12... | collective-permute-start | bytes 221192 | tf_op jit(solution)/shard_map/ppermute | solution.py:43
  9.9 13.0 %collective-permute-start = (bf16[2,1,1,64,768]{4,3,0,2,1:T(8,128)(2,1)S(1)}, bf16[2,1,1,64,768]{4,3,0,2,1:T(8,128)(2,1)S(1)}, u32[]{:S(2)}, u32[]{:S(2)}) collective-permute-start(bf16[2,1,1,64,768]{4,3,0,2,1:T(8,128)(2,1)S(1)} %maximum_bitcast_fusion), channel_id=1, source_target_pairs={{0,4},{2,6},{4,0},{6,2},{1,5},{3,7},{5,1},{7,3},{8,12},{10,14},{12... | collective-permute-start | bytes 589832 | tf_op jit(solution)/shard_map/ppermute | solution.py:43
  10.1 24.6 %collective-permute-start.10 = (bf16[48,768]{1,0:T(8,128)(2,1)}, bf16[48,768]{1,0:T(8,128)(2,1)S(1)}, u32[]{:S(2)}, u32[]{:S(2)}) collective-permute-start(bf16[48,768]{1,0:T(8,128)(2,1)} %get-tuple-element.56), channel_id=1, source_target_pairs={{0,4},{2,6},{4,0},{6,2},{1,5},{3,7},{5,1},{7,3},{8,12},{10,14},{12... | collective-permute-start | bytes 221192 | tf_op jit(solution)/shard_map/ppermute | solution.py:43
  14.6 10.0 %copy-start.9 = (bf16[48,768]{1,0:T(8,128)(2,1)S(1)}, bf16[48,768]{1,0:T(8,128)(2,1)}, u32[]{:S(2)}) copy-start(bf16[48,768]{1,0:T(8,128)(2,1)} %get-tuple-element.52) | copy-start | bytes 221188
  14.6 19.2 %copy-start.24 = (bf16[48,768]{1,0:T(8,128)(2,1)S(1)}, bf16[48,768]{1,0:T(8,128)(2,1)}, u32[]{:S(2)}) copy-start(bf16[48,768]{1,0:T(8,128)(2,1)} %get-tuple-element.54) | copy-start | bytes 221188
  14.6 23.8 %collective-permute-start.3 = (bf16[48,768]{1,0:T(8,128)(2,1)}, bf16[48,768]{1,0:T(8,128)(2,1)S(1)}, u32[]{:S(2)}, u32[]{:S(2)}) collective-permute-start(bf16[48,768]{1,0:T(8,128)(2,1)} %get-tuple-element.53), channel_id=1, source_target_pairs={{0,2},{2,0},{4,6},{6,4},{1,3},{3,1},{5,7},{7,5},{8,10},{10,8},{12,... | collective-permute-start | bytes 221192 | tf_op jit(solution)/shard_map/ppermute | solution.py:43
  23.0 10.8 %collective-permute-start.1 = (bf16[2,1,2,64,768]{4,3,0,2,1:T(8,128)(2,1)S(1)}, bf16[2,1,2,64,768]{4,3,0,2,1:T(8,128)(2,1)S(1)}, u32[]{:S(2)}, u32[]{:S(2)}) collective-permute-start(bf16[2,1,2,64,768]{4,3,0,2,1:T(8,128)(2,1)S(1)} %pad_maximum_fusion.1), channel_id=1, source_target_pairs={{0,2},{2,0},{4,6},{6,4},{1,3},{3,1},{5,7},{7,5},{8,10},{10,8},{12,... | collective-permute-start | bytes 1179656 | tf_op jit(solution)/shard_map/ppermute | solution.py:43
  33.8 7.9 %collective-permute-start.4 = (bf16[48,768]{1,0:T(8,128)(2,1)S(1)}, bf16[48,768]{1,0:T(8,128)(2,1)S(1)}, u32[]{:S(2)}, u32[]{:S(2)}) collective-permute-start(bf16[48,768]{1,0:T(8,128)(2,1)S(1)} %copy-done.24), channel_id=1, source_target_pairs={{0,4},{2,6},{4,0},{6,2},{1,5},{3,7},{5,1},{7,3},{8,12},{10,14},{12... | collective-permute-start | bytes 221192 | tf_op jit(solution)/shard_map/ppermute | solution.py:43
  34.6 21.8 %copy-start.2 = (bf16[2,1,4,64,768]{4,3,2,0,1:T(8,128)(2,1)}, bf16[2,1,4,64,768]{4,3,2,0,1:T(8,128)(2,1)S(1)}, u32[]{:S(2)}) copy-start(bf16[2,1,4,64,768]{4,3,2,0,1:T(8,128)(2,1)S(1)} %copy.44) | copy-start | bytes 2359300
  34.6 21.0 %collective-permute-start.2 = (bf16[2,1,256,768]{3,2,1,0:T(8,128)(2,1)S(1)}, bf16[2,1,256,768]{3,2,1,0:T(8,128)(2,1)S(1)}, u32[]{:S(2)}, u32[]{:S(2)}) collective-permute-start(bf16[2,1,256,768]{3,2,1,0:T(8,128)(2,1)S(1)} %bitcast.56), channel_id=1, source_target_pairs={{0,1},{1,0},{2,3},{3,2},{4,5},{5,4},{6,7},{7,6},{8,9},{9,8},{10,11... | collective-permute-start | bytes 2359304 | tf_op jit(solution)/shard_map/ppermute | solution.py:43
  34.7 9.4 %collective-permute-start.5 = (bf16[48,768]{1,0:T(8,128)(2,1)S(1)}, bf16[48,768]{1,0:T(8,128)(2,1)S(1)}, u32[]{:S(2)}, u32[]{:S(2)}) collective-permute-start(bf16[48,768]{1,0:T(8,128)(2,1)S(1)} %copy-done.23), channel_id=1, source_target_pairs={{0,6},{2,4},{4,2},{6,0},{1,7},{3,5},{5,3},{7,1},{8,14},{10,12},{12... | collective-permute-start | bytes 221192 | tf_op jit(solution)/shard_map/ppermute | solution.py:43
  36.8 19.5 %copy-start.14 = (bf16[192,768]{1,0:T(8,128)(2,1)}, bf16[192,768]{1,0:T(8,128)(2,1)S(1)}, u32[]{:S(2)}) copy-start(bf16[192,768]{1,0:T(8,128)(2,1)S(1)} %constant_dynamic-update-slice_fusion.4.refs_2_) | copy-start | bytes 884740
  36.8 9.9 %collective-permute-start.12 = (bf16[192,768]{1,0:T(8,128)(2,1)S(1)}, bf16[192,768]{1,0:T(8,128)(2,1)S(1)}, u32[]{:S(2)}, u32[]{:S(2)}) collective-permute-start(bf16[192,768]{1,0:T(8,128)(2,1)S(1)} %constant_dynamic-update-slice_fusion.4.refs_2_), channel_id=1, source_target_pairs={{0,8},{8,0},{16,24},{24,16},{1,9},{9,1},{17,25},{25,17},{2,10},{10... | collective-permute-start | bytes 884744 | tf_op jit(solution)/shard_map/ppermute | solution.py:43
  38.4 15.2 %collective-permute-start.13 = (bf16[192,768]{1,0:T(8,128)(2,1)S(1)}, bf16[192,768]{1,0:T(8,128)(2,1)S(1)}, u32[]{:S(2)}, u32[]{:S(2)}) collective-permute-start(bf16[192,768]{1,0:T(8,128)(2,1)S(1)} %constant_dynamic-update-slice_fusion.4.refs_2_), channel_id=1, source_target_pairs={{0,16},{8,24},{16,0},{24,8},{1,17},{9,25},{17,1},{25,9},{2,18},{10... | collective-permute-start | bytes 884744 | tf_op jit(solution)/shard_map/ppermute | solution.py:43
  41.7 13.9 %collective-permute-start.14 = (bf16[192,768]{1,0:T(8,128)(2,1)S(1)}, bf16[192,768]{1,0:T(8,128)(2,1)S(1)}, u32[]{:S(2)}, u32[]{:S(2)}) collective-permute-start(bf16[192,768]{1,0:T(8,128)(2,1)S(1)} %constant_dynamic-update-slice_fusion.4.refs_2_), channel_id=1, source_target_pairs={{0,24},{8,16},{16,8},{24,0},{1,25},{9,17},{17,9},{25,1},{2,26},{10... | collective-permute-start | bytes 884744 | tf_op jit(solution)/shard_map/ppermute | solution.py:43
  44.1 20.5 %copy-start.13 = (bf16[192,768]{1,0:T(8,128)(2,1)}, bf16[192,768]{1,0:T(8,128)(2,1)S(1)}, u32[]{:S(2)}) copy-start(bf16[192,768]{1,0:T(8,128)(2,1)S(1)} %constant_dynamic-update-slice_fusion.refs_2_) | copy-start | bytes 884740
  44.2 20.5 %collective-permute-start.6 = (bf16[192,768]{1,0:T(8,128)(2,1)S(1)}, bf16[192,768]{1,0:T(8,128)(2,1)S(1)}, u32[]{:S(2)}, u32[]{:S(2)}) collective-permute-start(bf16[192,768]{1,0:T(8,128)(2,1)S(1)} %constant_dynamic-update-slice_fusion.refs_2_), channel_id=1, source_target_pairs={{0,8},{8,0},{16,24},{24,16},{1,9},{9,1},{17,25},{25,17},{2,10},{10... | collective-permute-start | bytes 884744 | tf_op jit(solution)/shard_map/ppermute | solution.py:43
  46.8 9.6 %copy-start.19 = (bf16[192,768]{1,0:T(8,128)(2,1)}, bf16[192,768]{1,0:T(8,128)(2,1)S(1)}, u32[]{:S(2)}) copy-start(bf16[192,768]{1,0:T(8,128)(2,1)S(1)} %collective-permute-done.12.refs_3_) | copy-start | bytes 884740
  46.8 19.5 %collective-permute-start.7 = (bf16[192,768]{1,0:T(8,128)(2,1)S(1)}, bf16[192,768]{1,0:T(8,128)(2,1)}, u32[]{:S(2)}, u32[]{:S(2)}) collective-permute-start(bf16[192,768]{1,0:T(8,128)(2,1)S(1)} %constant_dynamic-update-slice_fusion.refs_2_), channel_id=1, source_target_pairs={{0,16},{8,24},{16,0},{24,8},{1,17},{9,25},{17,1},{25,9},{2,18},{10... | collective-permute-start | bytes 884744 | tf_op jit(solution)/shard_map/ppermute | solution.py:43
  53.6 2.7 %copy-start.20 = (bf16[192,768]{1,0:T(8,128)(2,1)}, bf16[192,768]{1,0:T(8,128)(2,1)S(1)}, u32[]{:S(2)}) copy-start(bf16[192,768]{1,0:T(8,128)(2,1)S(1)} %collective-permute-done.13.refs_4_) | copy-start | bytes 884740
  53.6 12.7 %collective-permute-start.8 = (bf16[192,768]{1,0:T(8,128)(2,1)S(1)}, bf16[192,768]{1,0:T(8,128)(2,1)}, u32[]{:S(2)}, u32[]{:S(2)}) collective-permute-start(bf16[192,768]{1,0:T(8,128)(2,1)S(1)} %constant_dynamic-update-slice_fusion.refs_2_), channel_id=1, source_target_pairs={{0,24},{8,16},{16,8},{24,0},{1,25},{9,17},{17,9},{25,1},{2,26},{10... | collective-permute-start | bytes 884744 | tf_op jit(solution)/shard_map/ppermute | solution.py:43
  66.3 9.8 %copy-start.16 = (f32[768]{0:T(1024)S(1)}, f32[768]{0:T(1024)}, u32[]{:S(2)}) copy-start(f32[768]{0:T(1024)} %param.22) | copy-start | bytes 9220
  66.3 9.8 %copy-start.17 = (f32[768]{0:T(1024)S(1)}, f32[768]{0:T(1024)}, u32[]{:S(2)}) copy-start(f32[768]{0:T(1024)} %param.28) | copy-start | bytes 9220
  66.3 10.3 %copy-start.1 = (bf16[2,64,768]{2,1,0:T(8,128)(2,1)S(1)}, bf16[2,64,768]{2,1,0:T(8,128)(2,1)}, u32[]{:S(2)}) copy-start(bf16[2,64,768]{2,1,0:T(8,128)(2,1)} %param.15) | copy-start | bytes 589828
  74.3 4.4 %collective-permute-start.15 = (f32[2,1,256,768]{3,2,1,0:T(8,128)}, f32[2,1,256,768]{3,2,1,0:T(8,128)S(1)}, u32[]{:S(2)}, u32[]{:S(2)}) collective-permute-start(f32[2,1,256,768]{3,2,1,0:T(8,128)} %get-tuple-element.63), channel_id=1, source_target_pairs={{0,1},{1,0},{2,3},{3,2},{4,5},{5,4},{6,7},{7,6},{8,9},{9,8},{10,11... | collective-permute-start | bytes 4718600 | tf_op jit(solution)/shard_map/ppermute | solution.py:43
  74.4 10.7 %collective-permute-start.20 = (bf16[208,768]{1,0:T(8,128)(2,1)}, bf16[208,768]{1,0:T(8,128)(2,1)S(1)}, u32[]{:S(2)}, u32[]{:S(2)}) collective-permute-start(bf16[208,768]{1,0:T(8,128)(2,1)} %get-tuple-element.66), channel_id=1, source_target_pairs={{0,8},{8,0},{16,24},{24,16},{1,9},{9,1},{17,25},{25,17},{2,10},{10... | collective-permute-start | bytes 958472 | tf_op jit(solution)/shard_map/ppermute | solution.py:43
  76.1 10.7 %collective-permute-start.21 = (bf16[208,768]{1,0:T(8,128)(2,1)}, bf16[208,768]{1,0:T(8,128)(2,1)S(1)}, u32[]{:S(2)}, u32[]{:S(2)}) collective-permute-start(bf16[208,768]{1,0:T(8,128)(2,1)} %get-tuple-element.67), channel_id=1, source_target_pairs={{0,16},{8,24},{16,0},{24,8},{1,17},{9,25},{17,1},{25,9},{2,18},{10... | collective-permute-start | bytes 958472 | tf_op jit(solution)/shard_map/ppermute | solution.py:43
  76.6 26.5 %collective-permute-start.27 = (bf16[192,768]{1,0:T(8,128)(2,1)}, bf16[192,768]{1,0:T(8,128)(2,1)}, u32[]{:S(2)}, u32[]{:S(2)}) collective-permute-start(bf16[192,768]{1,0:T(8,128)(2,1)} %get-tuple-element.75), channel_id=1, source_target_pairs={{0,8},{8,0},{16,24},{24,16},{1,9},{9,1},{17,25},{25,17},{2,10},{10... | collective-permute-start | bytes 884744 | tf_op jit(solution)/shard_map/ppermute | solution.py:43
  78.2 27.4 %collective-permute-start.28 = (bf16[192,768]{1,0:T(8,128)(2,1)}, bf16[192,768]{1,0:T(8,128)(2,1)}, u32[]{:S(2)}, u32[]{:S(2)}) collective-permute-start(bf16[192,768]{1,0:T(8,128)(2,1)} %get-tuple-element.76), channel_id=1, source_target_pairs={{0,16},{8,24},{16,0},{24,8},{1,17},{9,25},{17,1},{25,9},{2,18},{10... | collective-permute-start | bytes 884744 | tf_op jit(solution)/shard_map/ppermute | solution.py:43
  78.7 20.6 %collective-permute-start.22 = (bf16[208,768]{1,0:T(8,128)(2,1)}, bf16[208,768]{1,0:T(8,128)(2,1)S(1)}, u32[]{:S(2)}, u32[]{:S(2)}) collective-permute-start(bf16[208,768]{1,0:T(8,128)(2,1)} %get-tuple-element.68), channel_id=1, source_target_pairs={{0,24},{8,16},{16,8},{24,0},{1,25},{9,17},{17,9},{25,1},{2,26},{10... | collective-permute-start | bytes 958472 | tf_op jit(solution)/shard_map/ppermute | solution.py:43
  85.1 14.2 %copy-start.3 = (bf16[208,768]{1,0:T(8,128)(2,1)}, bf16[208,768]{1,0:T(8,128)(2,1)S(1)}, u32[]{:S(2)}) copy-start(bf16[208,768]{1,0:T(8,128)(2,1)S(1)} %collective-permute-done.20.refs_1_) | copy-start | bytes 958468
  85.1 33.3 %collective-permute-start.16 = (bf16[2,1,2,64,768]{4,3,2,1,0:T(8,128)(2,1)S(1)}, bf16[2,1,2,64,768]{4,3,2,1,0:T(8,128)(2,1)S(1)}, u32[]{:S(2)}, u32[]{:S(2)}) collective-permute-start(bf16[2,1,2,64,768]{4,3,2,1,0:T(8,128)(2,1)S(1)} %split.26), channel_id=1, source_target_pairs={{0,2},{2,0},{4,6},{6,4},{1,3},{3,1},{5,7},{7,5},{8,10},{10,8},{12,... | collective-permute-start | bytes 1179656 | tf_op jit(solution)/shard_map/ppermute | solution.py:43
  86.8 12.5 %copy-start.4 = (bf16[208,768]{1,0:T(8,128)(2,1)}, bf16[208,768]{1,0:T(8,128)(2,1)S(1)}, u32[]{:S(2)}) copy-start(bf16[208,768]{1,0:T(8,128)(2,1)S(1)} %collective-permute-done.21.refs_2_) | copy-start | bytes 958468
  86.8 20.8 %collective-permute-start.29 = (bf16[192,768]{1,0:T(8,128)(2,1)}, bf16[192,768]{1,0:T(8,128)(2,1)}, u32[]{:S(2)}, u32[]{:S(2)}) collective-permute-start(bf16[192,768]{1,0:T(8,128)(2,1)} %get-tuple-element.77), channel_id=1, source_target_pairs={{0,24},{8,16},{16,8},{24,0},{1,25},{9,17},{17,9},{25,1},{2,26},{10... | collective-permute-start | bytes 884744 | tf_op jit(solution)/shard_map/ppermute | solution.py:43
  102.3 7.5 %collective-permute-start.23 = (bf16[64,768]{1,0:T(8,128)(2,1)}, bf16[64,768]{1,0:T(8,128)(2,1)S(1)}, u32[]{:S(2)}, u32[]{:S(2)}) collective-permute-start(bf16[64,768]{1,0:T(8,128)(2,1)} %get-tuple-element.70), channel_id=1, source_target_pairs={{0,2},{2,0},{4,6},{6,4},{1,3},{3,1},{5,7},{7,5},{8,10},{10,8},{12,... | collective-permute-start | bytes 294920 | tf_op jit(solution)/shard_map/ppermute | solution.py:43
  103.1 11.0 %collective-permute-start.24 = (bf16[64,768]{1,0:T(8,128)(2,1)}, bf16[64,768]{1,0:T(8,128)(2,1)S(1)}, u32[]{:S(2)}, u32[]{:S(2)}) collective-permute-start(bf16[64,768]{1,0:T(8,128)(2,1)} %get-tuple-element.71), channel_id=1, source_target_pairs={{0,4},{2,6},{4,0},{6,2},{1,5},{3,7},{5,1},{7,3},{8,12},{10,14},{12... | collective-permute-start | bytes 294920 | tf_op jit(solution)/shard_map/ppermute | solution.py:43
  105.6 10.1 %collective-permute-start.25 = (bf16[64,768]{1,0:T(8,128)(2,1)}, bf16[64,768]{1,0:T(8,128)(2,1)S(1)}, u32[]{:S(2)}, u32[]{:S(2)}) collective-permute-start(bf16[64,768]{1,0:T(8,128)(2,1)} %get-tuple-element.72), channel_id=1, source_target_pairs={{0,6},{2,4},{4,2},{6,0},{1,7},{3,5},{5,3},{7,1},{8,14},{10,12},{12... | collective-permute-start | bytes 294920 | tf_op jit(solution)/shard_map/ppermute | solution.py:43
  109.8 11.6 %collective-permute-start.30 = (bf16[48,768]{1,0:T(8,128)(2,1)}, bf16[48,768]{1,0:T(8,128)(2,1)S(1)}, u32[]{:S(2)}, u32[]{:S(2)}) collective-permute-start(bf16[48,768]{1,0:T(8,128)(2,1)} %get-tuple-element.79), channel_id=1, source_target_pairs={{0,2},{2,0},{4,6},{6,4},{1,3},{3,1},{5,7},{7,5},{8,10},{10,8},{12,... | collective-permute-start | bytes 221192 | tf_op jit(solution)/shard_map/ppermute | solution.py:43
  109.8 5.9 %copy-start.6 = (bf16[64,768]{1,0:T(8,128)(2,1)}, bf16[64,768]{1,0:T(8,128)(2,1)S(1)}, u32[]{:S(2)}) copy-start(bf16[64,768]{1,0:T(8,128)(2,1)S(1)} %collective-permute-done.23.refs_1_) | copy-start | bytes 294916
  109.8 11.6 %collective-permute-start.31 = (bf16[48,768]{1,0:T(8,128)(2,1)}, bf16[48,768]{1,0:T(8,128)(2,1)S(1)}, u32[]{:S(2)}, u32[]{:S(2)}) collective-permute-start(bf16[48,768]{1,0:T(8,128)(2,1)} %get-tuple-element.80), channel_id=1, source_target_pairs={{0,4},{2,6},{4,0},{6,2},{1,5},{3,7},{5,1},{7,3},{8,12},{10,14},{12... | collective-permute-start | bytes 221192 | tf_op jit(solution)/shard_map/ppermute | solution.py:43
  114.1 7.3 %collective-permute-start.32 = (bf16[48,768]{1,0:T(8,128)(2,1)}, bf16[48,768]{1,0:T(8,128)(2,1)S(1)}, u32[]{:S(2)}, u32[]{:S(2)}) collective-permute-start(bf16[48,768]{1,0:T(8,128)(2,1)} %get-tuple-element.81), channel_id=1, source_target_pairs={{0,6},{2,4},{4,2},{6,0},{1,7},{3,5},{5,3},{7,1},{8,14},{10,12},{12... | collective-permute-start | bytes 221192 | tf_op jit(solution)/shard_map/ppermute | solution.py:43
  118.3 5.5 %copy-start.15 = (f32[24,128]{1,0:T(8,128)S(1)}, f32[24,128]{1,0:T(8,128)}, u32[]{:S(2)}) copy-start(f32[24,128]{1,0:T(8,128)} %get-tuple-element.73) | copy-start | bytes 36868
  118.3 5.5 %collective-permute-start.26 = (f32[24,128]{1,0:T(8,128)}, f32[24,128]{1,0:T(8,128)S(1)}, u32[]{:S(2)}, u32[]{:S(2)}) collective-permute-start(f32[24,128]{1,0:T(8,128)} %get-tuple-element.73), channel_id=1, source_target_pairs={{0,1},{1,0},{2,3},{3,2},{4,5},{5,4},{6,7},{7,6},{8,9},{9,8},{10,11... | collective-permute-start | bytes 36872 | tf_op jit(solution)/shard_map/ppermute | solution.py:43
  118.5 12.6 %collective-permute-start.17 = (bf16[2,1,1,64,768]{4,3,2,1,0:T(8,128)(2,1)S(1)}, bf16[2,1,1,64,768]{4,3,2,1,0:T(8,128)(2,1)S(1)}, u32[]{:S(2)}, u32[]{:S(2)}) collective-permute-start(bf16[2,1,1,64,768]{4,3,2,1,0:T(8,128)(2,1)S(1)} %split.27), channel_id=1, source_target_pairs={{0,4},{2,6},{4,0},{6,2},{1,5},{3,7},{5,1},{7,3},{8,12},{10,14},{12... | collective-permute-start | bytes 589832 | tf_op jit(solution)/shard_map/ppermute | solution.py:43
  131.6 1.4 %collective-permute-start.18 = (bf16[1,64,768]{2,1,0:T(8,128)(2,1)S(1)}, bf16[1,64,768]{2,1,0:T(8,128)(2,1)S(1)}, u32[]{:S(2)}, u32[]{:S(2)}) collective-permute-start(bf16[1,64,768]{2,1,0:T(8,128)(2,1)S(1)} %get-tuple-element.97), channel_id=1, source_target_pairs={{0,1},{1,0},{2,3},{3,2},{4,5},{5,4},{6,7},{7,6},{8,9},{9,8},{10,11... | collective-permute-start | bytes 294920 | tf_op jit(solution)/shard_map/ppermute | solution.py:43
  132.3 1.6 %collective-permute-start.19 = (f32[1,64,768]{2,1,0:T(8,128)S(1)}, f32[1,64,768]{2,1,0:T(8,128)S(1)}, u32[]{:S(2)}, u32[]{:S(2)}) collective-permute-start(f32[1,64,768]{2,1,0:T(8,128)S(1)} %get-tuple-element.96), channel_id=1, source_target_pairs={{0,1},{1,0},{2,3},{3,2},{4,5},{5,4},{6,7},{7,6},{8,9},{9,8},{10,11... | collective-permute-start | bytes 589832 | tf_op jit(solution)/shard_map/ppermute | solution.py:43
  (10 other events, 9.0 us)
